TPU v7x, 32 devices: a whole 2x2x4 slice. The times are simulated.
32 devices in a mesh: case: 2 (over y), filt: 16 (over z, x, core).
Axes of the slice: x: 2, y: 2, z: 4, core: 2. Of those that a mesh axis runs over, the one named last changes fastest.
Arguments:
- inputs: bfloat16 [2048, 2304], P('filt', 'case'), may hold values from -6 to 6
- weight: bfloat16 [9, 2048, 2048], P(None, 'filt'), may hold values from -0.046875 to 0.046875
- bias_vector: float32 [2048], P('filt'), may hold values from -3 to 3
- cotangent: bfloat16 [2048, 2304], P('filt', 'case'), may hold values from -64 to 64
Outputs:
- activated: bfloat16 [2048, 2304], P('filt', 'case')
- input_grad: bfloat16 [2048, 2304], P('filt', 'case')
- weight_grad: float32 [9, 2048, 2048], P(None, 'filt')
- bias_grad: float32 [2048], P('filt')
All inputs are finite; a program needn't handle non-finite values.
Results may differ from a plain program's by a relative error of at most 0.0075.
Values may be sent and summed in bfloat16 or wider, within the bound.
No kernel may reach another device: no remote copies, remote signals or barrier semaphores. Data moves between devices by JAX's collectives and lax.ppermute only.
A program may use at most 192 MiB of HBM per device.

v0:
```python
import functools

import jax
import jax.numpy as jnp
import numpy as np
from jax import lax
from jax.experimental import pallas as pl
from jax.experimental.pallas import tpu as pltpu
from jax.sharding import PartitionSpec as P

GRID = 24
FIELD = GRID * GRID
STEPS = (-1, 0, 1)
EDGE = 8
F32 = jnp.float32
BF16 = jnp.bfloat16
MIB = 1024 * 1024
VMEM = pl.BlockSpec(memory_space=pltpu.VMEM)
SMEM = pl.BlockSpec(memory_space=pltpu.SMEM)


def chip_cycle(chips):
    rows = 4
    cols = chips // rows
    walk = [(r, 0) for r in range(rows)]
    for r in reversed(range(rows)):
        across = range(1, cols) if (rows - 1 - r) % 2 == 0 else reversed(range(1, cols))
        walk += [(r, c) for c in across]
    return [r * cols + c for r, c in walk]


def rows_moved(v, a):
    if a == 0:
        return v
    gap = jnp.zeros((GRID, v.shape[1]), v.dtype)
    pieces = []
    for s in range(0, v.shape[0], FIELD):
        pieces += [v[s + GRID : s + FIELD], gap] if a > 0 else [gap, v[s : s + FIELD - GRID]]
    return jnp.concatenate(pieces, axis=0)


def grid_columns(cells, lanes):
    r = lax.broadcasted_iota(jnp.int32, (cells, lanes), 0)
    return lax.rem(r, GRID)


def columns_moved(field, v, b, col):
    if b == 0:
        return v
    cells, lanes = v.shape
    field[EDGE : EDGE + cells, :lanes] = v
    moved = field[EDGE + b : EDGE + b + cells, :lanes]
    ok = col >= 1 if b < 0 else col < GRID - 1
    return jnp.where(ok, moved, 0.0)


def clear_edges(field):
    rows, lanes = field.shape
    field[0:EDGE, :] = jnp.zeros((EDGE, lanes), field.dtype)
    field[rows - EDGE : rows, :] = jnp.zeros((EDGE, lanes), field.dtype)


def forward_sums(q_ref, slots, xs, w_own, w_sib, carry, b):
    lanes = xs[0][0].shape[1] if isinstance(xs[0], (list, tuple)) else xs[0].shape[1]
    total = None if carry is None else carry
    for a in STEPS:
        tap = (a + 1) * 3 + b + 1
        part = None
        for n, x in zip(slots, xs):
            cols = pl.ds(pl.multiple_of(q_ref[n] * lanes, lanes), lanes)
            w = jnp.concatenate([w_own[tap, :, cols], w_sib[tap, :, cols]], axis=0)
            v = jnp.concatenate([p[...] for p in x], axis=0) if isinstance(x, (list, tuple)) else x[...]
            y = lax.dot_general(v, w, (((1,), (1,)), ((), ())), preferred_element_type=F32)
            part = y if part is None else part + y
        part = rows_moved(part, a)
        total = part if total is None else total + part
    return total


def forward_kernel(slots, has_carry, q_ref, w_own, w_sib, *refs):
    refs = list(refs)
    carry = refs.pop(0) if has_carry else None
    xs, out = refs[:-1], refs[-1]
    for b in STEPS:
        before = carry[b + 1] if has_carry else None
        out[b + 1] = forward_sums(q_ref, slots, xs, w_own, w_sib, before, b)


def forward_call(q, slots, xs, w_own, w_sib, carry):
    cells, lanes = xs[0].shape
    outs = 2 * w_own.shape[1]
    args = ([] if carry is None else [carry]) + list(xs)
    return pl.pallas_call(
        functools.partial(forward_kernel, slots, carry is not None),
        out_shape=jax.ShapeDtypeStruct((3, cells, outs), F32),
        in_specs=[SMEM] + [VMEM] * (2 + len(args)),
        out_specs=VMEM,
        compiler_params=pltpu.CompilerParams(vmem_limit_bytes=8 * MIB),
        cost_estimate=pl.CostEstimate(
            flops=18 * len(xs) * cells * lanes * outs, transcendentals=0, bytes_accessed=8 * MIB
        ),
        name="forward",
    )(q, w_own, w_sib, *args)


def gate_kernel(slots, halves, q_ref, w_own, w_sib, carry, bias, cot_own, cot_sib, *refs):
    xs = refs[: len(slots) * halves]
    act_own, act_sib, g_own, g_sib, g9, field = refs[len(slots) * halves :]
    xs = [xs[n : n + halves] for n in range(0, len(xs), halves)]
    cells = act_own.shape[0]
    part = act_own.shape[1]
    lanes = 2 * part
    col = grid_columns(cells, lanes)
    clear_edges(field)
    preact = bias[0:1, :]
    for b in (0, -1, 1):
        sums = forward_sums(q_ref, slots, xs, w_own, w_sib, carry[b + 1], b)
        preact = preact + columns_moved(field, sums, b, col)
    gate = jax.nn.sigmoid(preact)
    act = (preact * gate).astype(BF16)
    act_own[...], act_sib[...] = act[:, :part], act[:, part:]
    cot = jnp.concatenate([cot_own[...], cot_sib[...]], axis=1).astype(F32)
    grad = (cot * gate * (1.0 + preact * (1.0 - gate))).astype(BF16)
    g_own[...], g_sib[...] = grad[:, :part], grad[:, part:]
    grad = grad.astype(F32)
    for b in STEPS:
        side = columns_moved(field, grad, -b, col)
        for a in STEPS:
            tap = (a + 1) * 3 + b + 1
            g9[:, tap * lanes : (tap + 1) * lanes] = rows_moved(side, -a).astype(BF16)


def gate_call(q, slots, xs, w_own, w_sib, carry, bias, cot_own, cot_sib):
    cells = carry.shape[1]
    outs = carry.shape[2]
    part = outs // 2
    halves = len(xs[0])
    flat = [p for x in xs for p in x]
    piece = jax.ShapeDtypeStruct((cells, part), BF16)
    return pl.pallas_call(
        functools.partial(gate_kernel, slots, halves),
        out_shape=[piece] * 4 + [jax.ShapeDtypeStruct((cells, 9 * outs), BF16)],
        in_specs=[SMEM] + [VMEM] * (6 + len(flat)),
        out_specs=[VMEM] * 5,
        scratch_shapes=[pltpu.VMEM((cells + 2 * EDGE, outs), F32)],
        compiler_params=pltpu.CompilerParams(vmem_limit_bytes=10 * MIB),
        cost_estimate=pl.CostEstimate(
            flops=18 * len(xs) * cells * flat[0].shape[1] * outs,
            transcendentals=cells * outs,
            bytes_accessed=8 * MIB,
        ),
        name="gate",
    )(q, w_own, w_sib, carry, bias, cot_own, cot_sib, *flat)


def input_grad_kernel(slots, pieces, q_ref, w_own, w_sib, g9, *outs):
    lanes = outs[0].shape[1]
    outs = list(outs)
    for n in slots:
        cols = pl.ds(pl.multiple_of(q_ref[n] * lanes, lanes), lanes)
        w = jnp.concatenate([w[tap, :, cols] for tap in range(9) for w in (w_own, w_sib)], axis=0)
        total = jnp.dot(g9[...], w, preferred_element_type=F32)
        rows = total.shape[0] // pieces
        for p in range(pieces):
            out = outs.pop(0)
            out[...] = total[p * rows : (p + 1) * rows].astype(out.dtype)


def input_grad_call(q, slots, dtype, pieces, g9, w_own, w_sib, lanes):
    cells, depth = g9.shape
    count = len(slots) * pieces
    return pl.pallas_call(
        functools.partial(input_grad_kernel, slots, pieces),
        out_shape=[jax.ShapeDtypeStruct((cells // pieces, lanes), dtype)] * count,
        in_specs=[SMEM] + [VMEM] * 3,
        out_specs=[VMEM] * count,
        compiler_params=pltpu.CompilerParams(vmem_limit_bytes=8 * MIB),
        cost_estimate=pl.CostEstimate(
            flops=2 * len(slots) * cells * depth * lanes, transcendentals=0, bytes_accessed=8 * MIB
        ),
        name="input_grad",
    )(q, w_own, w_sib, g9)


def displaced_kernel(scale, *refs):
    gs = refs[:-3]
    out, bias_out, field = refs[-3:]
    cells = out.shape[1]
    part = out.shape[0] // 9
    clear_edges(field)
    grad = jnp.concatenate([g[...] for g in gs], axis=0).astype(F32)
    bias_out[...] = jnp.sum(grad, axis=0, keepdims=True) * scale
    col = grid_columns(cells, part)
    for b in STEPS:
        side = columns_moved(field, grad, -b, col)
        for a in STEPS:
            tap = (a + 1) * 3 + b + 1
            moved = rows_moved(side, -a).astype(BF16)
            out[tap * part : (tap + 1) * part, :] = jnp.transpose(moved)


def displaced_call(gs, scale):
    cells = sum(g.shape[0] for g in gs)
    part = gs[0].shape[1]
    return pl.pallas_call(
        functools.partial(displaced_kernel, scale),
        out_shape=[
            jax.ShapeDtypeStruct((9 * part, cells), BF16),
            jax.ShapeDtypeStruct((1, part), F32),
        ],
        in_specs=[VMEM] * len(gs),
        out_specs=[VMEM] * 2,
        scratch_shapes=[pltpu.VMEM((cells + 2 * EDGE, part), F32)],
        compiler_params=pltpu.CompilerParams(vmem_limit_bytes=16 * MIB),
        cost_estimate=pl.CostEstimate(flops=9 * cells * part, transcendentals=0, bytes_accessed=8 * MIB),
        name="displaced",
    )(*gs)


def weight_grad_kernel(blocks, pieces, scale, q_ref, g9t, *refs):
    xs, out = refs[: blocks * pieces], refs[-1]
    for m in range(blocks):

        @pl.when(pl.program_id(0) == m)
        def _(m=m):
            x = jnp.concatenate([x[...] for x in xs[m * pieces : (m + 1) * pieces]], axis=0)
            out[...] = jnp.dot(g9t[...], x, preferred_element_type=F32) * scale


def weight_grad_call(q, slots, g9t, xs, total, scale, channels):
    blocks = len(slots)
    pieces = len(xs[0])
    rows, cells = g9t.shape
    lanes = xs[0][0].shape[1]
    flat = [x for group in xs for x in group]
    first = slots[0]
    aliased = [] if total is None else [total]
    return pl.pallas_call(
        functools.partial(weight_grad_kernel, blocks, pieces, scale),
        out_shape=jax.ShapeDtypeStruct((rows, channels), F32),
        grid_spec=pltpu.PrefetchScalarGridSpec(
            num_scalar_prefetch=1,
            grid=(blocks,),
            in_specs=[VMEM] * (1 + len(flat)) + [pl.BlockSpec(memory_space=pl.ANY)] * len(aliased),
            out_specs=pl.BlockSpec((rows, lanes), lambda k, q: (0, q[first + k])),
        ),
        input_output_aliases={2 + len(flat): 0} if aliased else {},
        compiler_params=pltpu.CompilerParams(
            dimension_semantics=("arbitrary",), vmem_limit_bytes=12 * MIB
        ),
        cost_estimate=pl.CostEstimate(
            flops=2 * blocks * rows * cells * lanes,
            transcendentals=0,
            bytes_accessed=2 * rows * cells + blocks * (2 * cells * lanes + 4 * rows * lanes),
        ),
        name="weight_grad",
    )(q, g9t, *flat, *aliased)


def body(inputs, weight, bias_vector, cotangent):
    part, cells = inputs.shape
    devices = lax.axis_size("filt")
    case_rows = lax.axis_size("case")
    channels = part * devices
    chips = devices // 2
    half = cells // 2
    lanes = 2 * part
    far = chips // 2
    scale = 1.0 / (cells // FIELD * case_rows)

    cycle = chip_cycle(chips)
    offsets = [0]
    for d in range(1, far):
        offsets += [-d, d]
    offsets.append(far)
    slot = {d: n for n, d in enumerate(offsets)}
    place = {chip: n for n, chip in enumerate(cycle)}
    table = np.array(
        [[cycle[(place[chip] + d) % chips] for d in offsets] for chip in range(chips)], np.int32
    )
    me = lax.axis_index("filt")
    core = me % 2
    q = lax.dynamic_index_in_dim(jnp.asarray(table), me // 2, 0, keepdims=False)

    forwards, backwards = [], []
    for n, chip in enumerate(cycle):
        for c in range(2):
            forwards.append((2 * chip + c, 2 * cycle[(n + 1) % chips] + c))
            backwards.append((2 * chip + c, 2 * cycle[(n - 1) % chips] + c))
    swap = [(n, n ^ 1) for n in range(devices)]
    onward = lambda v: lax.ppermute(v, "filt", forwards)
    back = lambda v: lax.ppermute(v, "filt", backwards)
    sibling = lambda v: lax.ppermute(v, "filt", swap)
    pair = case_rows == 2
    across = lambda v: lax.ppermute(v, "case", [(0, 1), (1, 0)])
    tie = lambda *v: lax.optimization_barrier(v)

    x_t = jnp.transpose(inputs)
    mine = lax.dynamic_slice_in_dim(x_t, core * half, half, 0)
    theirs = sibling(lax.dynamic_slice_in_dim(x_t, (1 - core) * half, half, 0))
    own_block = jnp.where(
        core == 0,
        jnp.concatenate([mine, theirs], axis=1),
        jnp.concatenate([theirs, mine], axis=1),
    )
    block = {0: own_block, -1: onward(own_block), 1: back(own_block)}
    theirs, weight, cotangent, bias_vector = tie(theirs, weight, cotangent, bias_vector)
    w_own, w_sib = weight, sibling(weight)
    cot_t = jnp.transpose(cotangent)
    cot_own = lax.dynamic_slice_in_dim(cot_t, core * half, half, 0)
    cot_sib = sibling(lax.dynamic_slice_in_dim(cot_t, (1 - core) * half, half, 0))
    bias_row = bias_vector[None, :]
    bias_row = jnp.concatenate([bias_row, sibling(bias_row)], axis=1)

    carry = forward_call(q, [0, 1, 2], [block[d] for d in (0, -1, 1)], w_own, w_sib, None)
    for s in range(2, far):
        block[-s], block[s] = onward(block[-s + 1]), back(block[s - 1])
        block[-s], block[s], carry = tie(block[-s], block[s], carry)
        if s < far - 1:
            carry = forward_call(q, [slot[-s], slot[s]], [block[-s], block[s]], w_own, w_sib, carry)
    s = far - 1
    top, low = onward(block[-s][: half // 2]), back(block[s][half // 2 :])
    carry = forward_call(q, [slot[-s], slot[s]], [block[-s], block[s]], w_own, w_sib, carry)
    top, low, carry = tie(top, low, carry)
    act_own, act_sib, g_own, g_sib, g9 = gate_call(
        q, [slot[far]], [[top, low]], w_own, w_sib, carry, bias_row, cot_own, cot_sib
    )

    grad_at = lambda ds, dtype, pieces=1: input_grad_call(
        q, [slot[d] for d in ds], dtype, pieces, g9, w_own, w_sib, lanes
    )
    top_p, low_p = grad_at([far], BF16, 2)
    ahead, behind = onward(top_p), back(low_p)
    p_ahead, p_behind = grad_at([far - 1, -(far - 1)], F32)
    rest_ds = [d for n in range(far - 2, 0, -1) for d in (n, -n)] + [0]
    ahead, behind, p_ahead, p_behind, g9 = tie(ahead, behind, p_ahead, p_behind, g9)
    rest = dict(zip(rest_ds, grad_at(rest_ds, F32)))
    hop = half // 2
    ahead = jnp.concatenate([p_ahead[:hop] + ahead.astype(F32), p_ahead[hop:]], axis=0)
    behind = jnp.concatenate([p_behind[:hop], p_behind[hop:] + behind.astype(F32)], axis=0)
    ahead, behind = onward(ahead.astype(BF16)), back(behind.astype(BF16))
    for s in range(far - 2, 0, -1):
        ahead = onward((rest[s] + ahead.astype(F32)).astype(BF16))
        behind = back((rest[-s] + behind.astype(F32)).astype(BF16))
    final = (rest[0] + ahead.astype(F32) + behind.astype(F32)).astype(BF16)
    keep = lax.dynamic_slice_in_dim(final, core * part, part, 1)
    other = sibling(lax.dynamic_slice_in_dim(final, (1 - core) * part, part, 1))
    join = lambda a, b: jnp.transpose(
        jnp.where(core == 0, jnp.concatenate([a, b], axis=0), jnp.concatenate([b, a], axis=0))
    )
    input_grad = join(keep, other)
    activated = join(act_own, sibling(act_sib))

    block[far] = jnp.concatenate([top, low], axis=0)
    gs = [g_own, sibling(g_sib)]
    groups = []
    for d in offsets:
        group = [block[d], sibling(block[d])]
        if pair:
            far_x = across(block[d])
            group += [far_x, sibling(far_x)]
        groups.append(group)
    if pair:
        gs += [across(g) for g in gs]
    g9t, bias_grad = displaced_call(gs, scale)
    total = None
    step = chips // 4
    for n in range(0, chips, step):
        ids = list(range(n, n + step))
        total = weight_grad_call(q, ids, g9t, [groups[i] for i in ids], total, scale, channels)
    bias_grad = bias_grad[0]
    if not pair:
        total, bias_grad = lax.psum((total, bias_grad), "case")
    weight_grad = total.reshape(9, part, channels)
    return activated, input_grad, weight_grad, bias_grad


def solution(mesh):
    in_specs = (P("filt", "case"), P(None, "filt", None), P("filt"), P("filt", "case"))
    out_specs = (P("filt", "case"), P("filt", "case"), P(None, "filt", None), P("filt"))
    return jax.shard_map(body, mesh=mesh, in_specs=in_specs, out_specs=out_specs, check_vma=False)
```

profile of v0, /device:TPU:0, one launch (start us, length us, event | category | flops | bytes accessed | tf_op | source)
XLA Modules:
  0.0 131.9 jit_solution(2672554763961876188)
XLA Ops:
  0.7 1.2 constant_dynamic-slice_fusion.2
  2.0 0.5 collective-permute-start
  2.5 1.0 collective-permute-done
  4.1 2.7 %collective-permute-start.4 = (bf16[576,256]{1,0:T(8,128)(2,1)S(1)}, bf16[576,256]{1,0:T(8,128)(2,1)S(1)}, u32[]{:S(2)}, u32[]{:S(2)}) collective-permute-start(bf16[576,256]{1,0:T(8,128)(2,1)S(1)} %maximum_select_fusion.refs_0_), channel_id=1, source_target_pairs={{0,2},{1,3},{4,0},{5,1},{8,4},{9,5},{12,8},{13,9},{14,12},{15,13},... | collective-permute-start | bytes 884744 | tf_op jit(solution)/shard_map/ppermute | solution.py:292
  7.0 7.5 %collective-permute-done.4.refs_2_.refs_0_ = bf16[576,256]{1,0:T(8,128)(2,1)S(1)} collective-permute-done((bf16[576,256]{1,0:T(8,128)(2,1)S(1)}, bf16[576,256]{1,0:T(8,128)(2,1)S(1)}, u32[]{:S(2)}, u32[]{:S(2)}) %collective-permute-start.4) | collective-permute-done | bytes 294944 | tf_op jit(solution)/shard_map/ppermute | solution.py:292
  14.4 1.7 %collective-permute-start.5 = (bf16[576,256]{1,0:T(8,128)(2,1)S(1)}, bf16[576,256]{1,0:T(8,128)(2,1)S(1)}, u32[]{:S(2)}, u32[]{:S(2)}) collective-permute-start(bf16[576,256]{1,0:T(8,128)(2,1)S(1)} %collective-permute-done.4.refs_2_.refs_0_), channel_id=1, source_target_pairs={{0,2},{1,3},{4,0},{5,1},{8,4},{9,5},{12,8},{13,9},{14,12},{15,13},... | collective-permute-start | bytes 884744 | tf_op jit(solution)/shard_map/ppermute | solution.py:292
  16.5 0.7 fusion.2.q_ref
  17.2 2.3 %copy-done = bf16[9,128,2048]{2,1,0:T(8,128)(2,1)S(1)} copy-done((bf16[9,128,2048]{2,1,0:T(8,128)(2,1)S(1)}, bf16[9,128,2048]{2,1,0:T(8,128)(2,1)}, u32[]{:S(2)}) %copy-start) | copy-done | bytes 4718616
  19.5 4.6 %forward.3.refs_0_ = f32[3,576,256]{2,1,0:T(8,128)S(1)} custom-call(s32[8]{0:T(128)S(1)} %fusion.2.q_ref, bf16[9,128,2048]{2,1,0:T(8,128)(2,1)S(1)} %copy-done, bf16[9,128,2048]{2,1,0:T(8,128)(2,1)} %collective-permute-done.1.w_sib, bf16[576,256]{1,0:T(8,128)(2,1)S(1)} %maximum_select_fusion.refs_0_, ...), custom_call_target="tpu_custom_call" | custom-call | flops 2038431744 | bytes 8388608 | tf_op jit(solution)/shard_map/forward/pallas_call | solution.py:93
  24.4 1.6 %collective-permute-start.6 = (bf16[576,256]{1,0:T(8,128)(2,1)}, bf16[576,256]{1,0:T(8,128)(2,1)S(1)}, u32[]{:S(2)}, u32[]{:S(2)}) collective-permute-start(bf16[576,256]{1,0:T(8,128)(2,1)} %collective-permute-done.3.refs_1_.refs_4_), channel_id=1, source_target_pairs={{0,4},{1,5},{4,8},{5,9},{8,12},{9,13},{12,14},{13,15},{14,10},{15,... | collective-permute-start | bytes 884744 | tf_op jit(solution)/shard_map/ppermute | solution.py:291
  26.4 1.5 %collective-permute-start.44 = (bf16[576,256]{1,0:T(8,128)(2,1)S(1)}, bf16[576,256]{1,0:T(8,128)(2,1)}, u32[]{:S(2)}, u32[]{:S(2)}) collective-permute-start(bf16[576,256]{1,0:T(8,128)(2,1)S(1)} %maximum_select_fusion.refs_0_), channel_id=1, source_target_pairs={{0,16},{16,0},{1,17},{17,1},{2,18},{18,2},{3,19},{19,3},{4,20},{20... | collective-permute-start | bytes 884744 | tf_op jit(solution)/shard_map/ppermute | solution.py:295
  28.4 1.8 %copy.14 = bf16[128,1152]{0,1:T(8,128)(2,1)} copy(bf16[128,1152]{1,0:T(8,128)(2,1)} %param.8) | data formatting | bytes 589824 | tf_op jit(solution)/shard_map/optimization_barrier | solution.py:296
  30.3 1.0 dynamic-slice_bitcast_fusion
  31.3 2.3 %copy-done.1 = bf16[9,128,2048]{2,1,0:T(8,128)(2,1)S(1)} copy-done((bf16[9,128,2048]{2,1,0:T(8,128)(2,1)S(1)}, bf16[9,128,2048]{2,1,0:T(8,128)(2,1)}, u32[]{:S(2)}) %copy-start.1) | copy-done | bytes 4718616
  33.6 4.0 %forward.4.refs_0_ = f32[3,576,256]{2,1,0:T(8,128)S(1)} custom-call(s32[8]{0:T(128)S(1)} %fusion.2.q_ref, bf16[9,128,2048]{2,1,0:T(8,128)(2,1)S(1)} %copy-done.1, bf16[9,128,2048]{2,1,0:T(8,128)(2,1)} %collective-permute-done.1.w_sib, f32[3,576,256]{2,1,0:T(8,128)S(1)} %forward.3.refs_0_, bf16[576,256]{1,0:T(8,128)(2,1)} %collective-permute-done.3.refs_1_.refs_4_, ...), custom_call_target="tpu_custom_call" | custom-call | flops 1358954496 | bytes 8388608 | tf_op jit(solution)/shard_map/forward/pallas_call | solution.py:93
  37.8 1.6 %collective-permute-start.9 = (bf16[288,256]{1,0:T(8,128)(2,1)S(1)}, bf16[288,256]{1,0:T(8,128)(2,1)S(1)}, u32[]{:S(2)}, u32[]{:S(2)}) collective-permute-start(bf16[288,256]{1,0:T(8,128)(2,1)S(1)} %slice.21), channel_id=1, source_target_pairs={{0,2},{1,3},{4,0},{5,1},{8,4},{9,5},{12,8},{13,9},{14,12},{15,13},... | collective-permute-start | bytes 442376 | tf_op jit(solution)/shard_map/ppermute | solution.py:292
  39.9 4.0 %forward.5.carry = f32[3,576,256]{2,1,0:T(8,128)S(1)} custom-call(s32[8]{0:T(128)S(1)} %fusion.2.q_ref, bf16[9,128,2048]{2,1,0:T(8,128)(2,1)S(1)} %copy-done.1, bf16[9,128,2048]{2,1,0:T(8,128)(2,1)} %collective-permute-done.1.w_sib, f32[3,576,256]{2,1,0:T(8,128)S(1)} %forward.4.refs_0_, bf16[576,256]{1,0:T(8,128)(2,1)S(1)} %collective-permute-done.6.refs_1_.refs_4_, ...), custom_call_target="tpu_custom_call" | custom-call | flops 1358954496 | bytes 8388608 | tf_op jit(solution)/shard_map/forward/pallas_call | solution.py:93
  44.6 0.8 collective-permute-done.8.refs_0_
  45.4 3.8 %gate.1 = (bf16[576,128]{1,0:T(8,128)(2,1)S(1)}, bf16[576,128]{1,0:T(8,128)(2,1)S(1)}, bf16[576,128]{1,0:T(8,128)(2,1)S(1)}, bf16[576,128]{1,0:T(8,128)(2,1)S(1)}, bf16[576,2304]{1,0:T(8,128)(2,1)S(1)}) custom-call(s32[8]{0:T(128)S(1)} %fusion.2.q_ref, bf16[9,128,2048]{2,1,0:T(8,128)(2,1)S(1)} %bitcast.16, ...), custom_call_target="tpu_custom_call" | custom-call | flops 679477248 | bytes 8388608 | tf_op jit(solution)/shard_map/gate/pallas_call | solution.py:140
  49.3 3.3 %input_grad.3 = (bf16[288,256]{1,0:T(8,128)(2,1)S(1)}, bf16[288,256]{1,0:T(8,128)(2,1)S(1)}) custom-call(s32[8]{0:T(128)S(1)} %fusion.2.q_ref, bf16[9,128,2048]{2,1,0:T(8,128)(2,1)S(1)} %bitcast.16, bf16[9,128,2048]{2,1,0:T(8,128)(2,1)} %collective-permute-done.1.w_sib, bf16[576,2304]{1,0:T(8,128)(2,1)S(1)} %get-tuple-element.56.g9), custom_call_target="tpu_custom_call" | custom-call | flops 679477248 | bytes 8388608 | tf_op jit(solution)/shard_map/input_grad/pallas_call | solution.py:172
  52.5 0.9 collective-permute-start.13
  53.4 1.2 collective-permute-start.14
  54.6 3.9 %input_grad.4 = (f32[576,256]{1,0:T(8,128)S(1)}, f32[576,256]{1,0:T(8,128)S(1)}) custom-call(s32[8]{0:T(128)S(1)} %fusion.2.q_ref, bf16[9,128,2048]{2,1,0:T(8,128)(2,1)S(1)} %bitcast.16, bf16[9,128,2048]{2,1,0:T(8,128)(2,1)} %collective-permute-done.1.w_sib, bf16[576,2304]{1,0:T(8,128)(2,1)S(1)} %get-tuple-element.56.g9), custom_call_target="tpu_custom_call" | custom-call | flops 1358954496 | bytes 8388608 | tf_op jit(solution)/shard_map/input_grad/pallas_call | solution.py:172
  58.6 0.8 collective-permute-start.47
  59.6 6.0 %input_grad.5 = (f32[576,256]{1,0:T(8,128)S(1)}, f32[576,256]{1,0:T(8,128)S(1)}, f32[576,256]{1,0:T(8,128)S(1)}, f32[576,256]{1,0:T(8,128)S(1)}, f32[576,256]{1,0:T(8,128)S(1)}) custom-call(s32[8]{0:T(128)S(1)} %fusion.2.q_ref, bf16[9,128,2048]{2,1,0:T(8,128)(2,1)S(1)} %bitcast.16, bf16[9,128,2048]{2,1,0:T(8,128)(2,1)} %collective-permute-done.1.w_sib, ...), custom_call_target="tpu_custom_call" | custom-call | flops 3397386240 | bytes 8388608 | tf_op jit(solution)/shard_map/input_grad/pallas_call | solution.py:172
  66.4 1.3 collective-permute-start.23
  67.7 0.7 collective-permute-start.24
  68.4 0.7 pad_maximum_fusion.1
  69.2 1.6 %collective-permute-start.18 = (bf16[576,256]{1,0:T(8,128)(2,1)}, bf16[576,256]{1,0:T(8,128)(2,1)}, u32[]{:S(2)}, u32[]{:S(2)}) collective-permute-start(bf16[576,256]{1,0:T(8,128)(2,1)} %pad_maximum_fusion.1), channel_id=1, source_target_pairs={{0,2},{1,3},{4,0},{5,1},{8,4},{9,5},{12,8},{13,9},{14,12},{15,13},... | collective-permute-start | bytes 884744 | tf_op jit(solution)/shard_map/ppermute | solution.py:292
  70.8 0.7 pad_maximum_fusion
  71.6 0.6 collective-permute-start.39
  72.1 0.9 collective-permute-done.23.refs_2_
  73.0 0.6 copy-done.14
  73.7 1.9 %collective-permute-done.24.refs_3_ = bf16[576,128]{1,0:T(8,128)(2,1)S(1)} collective-permute-done((bf16[576,128]{1,0:T(8,128)(2,1)S(1)}, bf16[576,128]{1,0:T(8,128)(2,1)S(1)}, u32[]{:S(2)}, u32[]{:S(2)}) %collective-permute-start.24) | collective-permute-done | bytes 147488 | tf_op jit(solution)/shard_map/ppermute | solution.py:295
  75.6 0.6 copy-done.16
  76.3 1.6 %collective-permute-start.15 = (bf16[576,256]{1,0:T(8,128)(2,1)}, bf16[576,256]{1,0:T(8,128)(2,1)}, u32[]{:S(2)}, u32[]{:S(2)}) collective-permute-start(bf16[576,256]{1,0:T(8,128)(2,1)} %pad_maximum_fusion), channel_id=1, source_target_pairs={{0,4},{1,5},{4,8},{5,9},{8,12},{9,13},{12,14},{13,15},{14,10},{15,... | collective-permute-start | bytes 884744 | tf_op jit(solution)/shard_map/ppermute | solution.py:291
  77.9 0.8 fusion
  78.7 1.8 %copy.16 = bf16[128,1152]{1,0:T(8,128)(2,1)} copy(bf16[128,1152]{0,1:T(8,128)(2,1)} %fusion) | data formatting | bytes 589824
  80.5 0.9 copy-done.11
  81.4 0.9 copy-done.13
  82.4 0.9 copy-done.15
  83.3 0.9 copy-done.17
  84.2 2.3 %displaced.1 = (bf16[1152,2304]{1,0:T(8,128)(2,1)S(1)}, f32[1,128]{1,0:T(1,128)}) custom-call(bf16[576,128]{1,0:T(8,128)(2,1)S(1)} %copy-done.11, bf16[576,128]{1,0:T(8,128)(2,1)S(1)} %copy-done.13, bf16[576,128]{1,0:T(8,128)(2,1)S(1)} %copy-done.15, bf16[576,128]{1,0:T(8,128)(2,1)S(1)} %copy-done.17), custom_call_target="tpu_custom_call" | custom-call | flops 2654208 | bytes 8388608 | tf_op jit(solution)/shard_map/displaced/pallas_call | solution.py:205
  86.5 0.6 collective-permute-start.41
  87.1 1.2 add_convert_fusion.2
  88.4 1.5 %collective-permute-start.32 = (bf16[576,256]{1,0:T(8,128)(2,1)S(1)}, bf16[576,256]{1,0:T(8,128)(2,1)S(1)}, u32[]{:S(2)}, u32[]{:S(2)}) collective-permute-start(bf16[576,256]{1,0:T(8,128)(2,1)S(1)} %collective-permute-done.5.refs_2_.refs_0_), channel_id=1, source_target_pairs={{0,16},{16,0},{1,17},{17,1},{2,18},{18,2},{3,19},{19,3},{4,20},{20... | collective-permute-start | bytes 884744 | tf_op jit(solution)/shard_map/ppermute | solution.py:295
  89.9 0.6 collective-permute-start.35
  90.5 1.1 collective-permute-start.19
  91.6 1.2 add_convert_fusion.4
  92.8 3.8 %collective-permute-done.41.refs_6_ = bf16[576,256]{1,0:T(8,128)(2,1)S(1)} collective-permute-done((bf16[576,256]{1,0:T(8,128)(2,1)}, bf16[576,256]{1,0:T(8,128)(2,1)S(1)}, u32[]{:S(2)}, u32[]{:S(2)}) %collective-permute-start.41) | collective-permute-done | bytes 294944 | tf_op jit(solution)/shard_map/ppermute | solution.py:295
  96.6 1.6 %collective-permute-start.16 = (bf16[576,256]{1,0:T(8,128)(2,1)S(1)}, bf16[576,256]{1,0:T(8,128)(2,1)S(1)}, u32[]{:S(2)}, u32[]{:S(2)}) collective-permute-start(bf16[576,256]{1,0:T(8,128)(2,1)S(1)} %add_convert_fusion.4), channel_id=1, source_target_pairs={{0,4},{1,5},{4,8},{5,9},{8,12},{9,13},{12,14},{13,15},{14,10},{15,... | collective-permute-start | bytes 884744 | tf_op jit(solution)/shard_map/ppermute | solution.py:291
  98.2 1.0 copy-done.9
  99.1 6.0 %weight_grad.4.refs_8_ = f32[1152,2048]{1,0:T(8,128)} custom-call(s32[8]{0:T(128)S(1)} %fusion.2.q_ref, bf16[1152,2304]{1,0:T(8,128)(2,1)S(1)} %get-tuple-element.68.g9t, bf16[576,256]{1,0:T(8,128)(2,1)S(1)} %maximum_select_fusion.refs_0_, bf16[576,256]{1,0:T(8,128)(2,1)} %collective-permute-done.43.refs_1_, ...), custom_call_target="tpu_custom_call" | custom-call | flops 2717908992 | bytes 10027008 | tf_op jit(solution)/shard_map/weight_grad/pallas_call | solution.py:238
  105.7 1.9 %collective-permute-done.35.refs_6_ = bf16[576,256]{1,0:T(8,128)(2,1)S(1)} collective-permute-done((bf16[576,256]{1,0:T(8,128)(2,1)S(1)}, bf16[576,256]{1,0:T(8,128)(2,1)S(1)}, u32[]{:S(2)}, u32[]{:S(2)}) %collective-permute-start.35) | collective-permute-done | bytes 294944 | tf_op jit(solution)/shard_map/ppermute | solution.py:295
  108.4 0.8 collective-permute-start.26
  109.2 1.3 collective-permute-start.29
  110.9 1.6 %collective-permute-start.17 = (bf16[576,256]{1,0:T(8,128)(2,1)S(1)}, bf16[576,256]{1,0:T(8,128)(2,1)S(1)}, u32[]{:S(2)}, u32[]{:S(2)}) collective-permute-start(bf16[576,256]{1,0:T(8,128)(2,1)S(1)} %add_convert_fusion.3), channel_id=1, source_target_pairs={{0,4},{1,5},{4,8},{5,9},{8,12},{9,13},{12,14},{13,15},{14,10},{15,... | collective-permute-start | bytes 884744 | tf_op jit(solution)/shard_map/ppermute | solution.py:291
  112.5 5.8 %weight_grad.5.refs_8_ = f32[1152,2048]{1,0:T(8,128)} custom-call(s32[8]{0:T(128)S(1)} %fusion.2.q_ref, bf16[1152,2304]{1,0:T(8,128)(2,1)S(1)} %get-tuple-element.68.g9t, bf16[576,256]{1,0:T(8,128)(2,1)S(1)} %collective-permute-done.4.refs_2_.refs_0_, bf16[576,256]{1,0:T(8,128)(2,1)S(1)} %copy-done.7, ...), custom_call_target="tpu_custom_call", output_to_operand_aliasing={{}: (10, {})} | custom-call | flops 2717908992 | bytes 10027008 | tf_op jit(solution)/shard_map/weight_grad/pallas_call | solution.py:238
  118.3 4.7 %weight_grad.6.refs_8_ = f32[1152,2048]{1,0:T(8,128)} custom-call(s32[8]{0:T(128)S(1)} %fusion.2.q_ref, bf16[1152,2304]{1,0:T(8,128)(2,1)S(1)} %get-tuple-element.68.g9t, bf16[576,256]{1,0:T(8,128)(2,1)S(1)} %collective-permute-done.5.refs_2_.refs_0_, bf16[576,256]{1,0:T(8,128)(2,1)S(1)} %collective-permute-done.31.refs_1_, ...), custom_call_target="tpu_custom_call", output_to_operand_aliasing={{}: (10, {})} | custom-call | flops 2717908992 | bytes 10027008 | tf_op jit(solution)/shard_map/weight_grad/pallas_call | solution.py:238
  123.5 0.7 collective-permute-done.29.refs_6_
  124.2 0.5 collective-permute-start.30
  124.9 0.8 collective-permute-done.27.refs_3_
  126.2 4.7 %weight_grad.7 = f32[1152,2048]{1,0:T(8,128)} custom-call(s32[8]{0:T(128)S(1)} %fusion.2.q_ref, bf16[1152,2304]{1,0:T(8,128)(2,1)S(1)} %get-tuple-element.68.g9t, bf16[576,256]{1,0:T(8,128)(2,1)S(1)} %collective-permute-done.7.refs_2_.refs_0_, bf16[576,256]{1,0:T(8,128)(2,1)S(1)} %collective-permute-done.25.refs_1_, ...), custom_call_target="tpu_custom_call", output_to_operand_aliasing={{}: (10, {})} | custom-call | flops 2717908992 | bytes 10027008 | tf_op jit(solution)/shard_map/weight_grad/pallas_call | solution.py:238
  131.0 0.9 copy.17
  (117 shorter events, 7.8 us)
Async XLA Ops:
  2.0 1.5 %collective-permute-start = (bf16[576,128]{1,0:T(8,128)(2,1)S(1)}, bf16[576,128]{1,0:T(8,128)(2,1)S(1)}, u32[]{:S(2)}, u32[]{:S(2)}) collective-permute-start(bf16[576,128]{1,0:T(8,128)(2,1)S(1)} %bitcast.19), channel_id=1, source_target_pairs={{0,1},{1,0},{2,3},{3,2},{4,5},{5,4},{6,7},{7,6},{8,9},{9,8},{10,11... | collective-permute-start | bytes 442376 | tf_op jit(solution)/shard_map/ppermute | solution.py:293
  3.5 13.7 %collective-permute-start.1 = (bf16[9,128,2048]{2,1,0:T(8,128)(2,1)}, bf16[9,128,2048]{2,1,0:T(8,128)(2,1)}, u32[]{:S(2)}, u32[]{:S(2)}) collective-permute-start(bf16[9,128,2048]{2,1,0:T(8,128)(2,1)} %w_own.6), channel_id=1, source_target_pairs={{0,1},{1,0},{2,3},{3,2},{4,5},{5,4},{6,7},{7,6},{8,9},{9,8},{10,11... | collective-permute-start | bytes 14155784 | tf_op jit(solution)/shard_map/ppermute | solution.py:293
  4.1 10.3 %collective-permute-start.4 = (bf16[576,256]{1,0:T(8,128)(2,1)S(1)}, bf16[576,256]{1,0:T(8,128)(2,1)S(1)}, u32[]{:S(2)}, u32[]{:S(2)}) collective-permute-start(bf16[576,256]{1,0:T(8,128)(2,1)S(1)} %maximum_select_fusion.refs_0_), channel_id=1, source_target_pairs={{0,2},{1,3},{4,0},{5,1},{8,4},{9,5},{12,8},{13,9},{14,12},{15,13},... | collective-permute-start | bytes 884744 | tf_op jit(solution)/shard_map/ppermute | solution.py:292
  6.8 9.3 %collective-permute-start.2 = (bf16[576,256]{1,0:T(8,128)(2,1)S(1)}, bf16[576,256]{1,0:T(8,128)(2,1)S(1)}, u32[]{:S(2)}, u32[]{:S(2)}) collective-permute-start(bf16[576,256]{1,0:T(8,128)(2,1)S(1)} %maximum_select_fusion.refs_0_), channel_id=1, source_target_pairs={{0,4},{1,5},{4,8},{5,9},{8,12},{9,13},{12,14},{13,15},{14,10},{15,... | collective-permute-start | bytes 884744 | tf_op jit(solution)/shard_map/ppermute | solution.py:291
  14.4 9.7 %collective-permute-start.5 = (bf16[576,256]{1,0:T(8,128)(2,1)S(1)}, bf16[576,256]{1,0:T(8,128)(2,1)S(1)}, u32[]{:S(2)}, u32[]{:S(2)}) collective-permute-start(bf16[576,256]{1,0:T(8,128)(2,1)S(1)} %collective-permute-done.4.refs_2_.refs_0_), channel_id=1, source_target_pairs={{0,2},{1,3},{4,0},{5,1},{8,4},{9,5},{12,8},{13,9},{14,12},{15,13},... | collective-permute-start | bytes 884744 | tf_op jit(solution)/shard_map/ppermute | solution.py:292
  16.1 8.3 %collective-permute-start.3 = (bf16[576,256]{1,0:T(8,128)(2,1)S(1)}, bf16[576,256]{1,0:T(8,128)(2,1)}, u32[]{:S(2)}, u32[]{:S(2)}) collective-permute-start(bf16[576,256]{1,0:T(8,128)(2,1)S(1)} %collective-permute-done.2.refs_1_.refs_4_), channel_id=1, source_target_pairs={{0,4},{1,5},{4,8},{5,9},{8,12},{9,13},{12,14},{13,15},{14,10},{15,... | collective-permute-start | bytes 884744 | tf_op jit(solution)/shard_map/ppermute | solution.py:291
  17.2 2.3 %copy-start = (bf16[9,128,2048]{2,1,0:T(8,128)(2,1)S(1)}, bf16[9,128,2048]{2,1,0:T(8,128)(2,1)}, u32[]{:S(2)}) copy-start(bf16[9,128,2048]{2,1,0:T(8,128)(2,1)} %w_own.6) | copy-start | bytes 14155780
  19.5 8.4 %copy-start.18 = (f32[128]{0:T(128)S(1)}, f32[128]{0:T(128)}, u32[]{:S(2)}) copy-start(f32[128]{0:T(128)} %param.7) | copy-start | bytes 1540
  24.4 13.3 %collective-permute-start.6 = (bf16[576,256]{1,0:T(8,128)(2,1)}, bf16[576,256]{1,0:T(8,128)(2,1)S(1)}, u32[]{:S(2)}, u32[]{:S(2)}) collective-permute-start(bf16[576,256]{1,0:T(8,128)(2,1)} %collective-permute-done.3.refs_1_.refs_4_), channel_id=1, source_target_pairs={{0,4},{1,5},{4,8},{5,9},{8,12},{9,13},{12,14},{13,15},{14,10},{15,... | collective-permute-start | bytes 884744 | tf_op jit(solution)/shard_map/ppermute | solution.py:291
  26.0 11.8 %collective-permute-start.7 = (bf16[576,256]{1,0:T(8,128)(2,1)S(1)}, bf16[576,256]{1,0:T(8,128)(2,1)S(1)}, u32[]{:S(2)}, u32[]{:S(2)}) collective-permute-start(bf16[576,256]{1,0:T(8,128)(2,1)S(1)} %collective-permute-done.5.refs_2_.refs_0_), channel_id=1, source_target_pairs={{0,2},{1,3},{4,0},{5,1},{8,4},{9,5},{12,8},{13,9},{14,12},{15,13},... | collective-permute-start | bytes 884744 | tf_op jit(solution)/shard_map/ppermute | solution.py:292
  26.4 32.1 %collective-permute-start.44 = (bf16[576,256]{1,0:T(8,128)(2,1)S(1)}, bf16[576,256]{1,0:T(8,128)(2,1)}, u32[]{:S(2)}, u32[]{:S(2)}) collective-permute-start(bf16[576,256]{1,0:T(8,128)(2,1)S(1)} %maximum_select_fusion.refs_0_), channel_id=1, source_target_pairs={{0,16},{16,0},{1,17},{17,1},{2,18},{18,2},{3,19},{19,3},{4,20},{20... | collective-permute-start | bytes 884744 | tf_op jit(solution)/shard_map/ppermute | solution.py:295
  27.9 37.7 %collective-permute-start.43 = (bf16[576,256]{1,0:T(8,128)(2,1)S(1)}, bf16[576,256]{1,0:T(8,128)(2,1)}, u32[]{:S(2)}, u32[]{:S(2)}) collective-permute-start(bf16[576,256]{1,0:T(8,128)(2,1)S(1)} %maximum_select_fusion.refs_0_), channel_id=1, source_target_pairs={{0,1},{1,0},{2,3},{3,2},{4,5},{5,4},{6,7},{7,6},{8,9},{9,8},{10,11... | collective-permute-start | bytes 884744 | tf_op jit(solution)/shard_map/ppermute | solution.py:293
  27.9 11.5 %collective-permute-start.10 = (f32[1,128]{1,0:T(1,128)S(1)}, f32[1,128]{1,0:T(1,128)S(1)}, u32[]{:S(2)}, u32[]{:S(2)}) collective-permute-start(f32[1,128]{1,0:T(1,128)S(1)} %bitcast.20), channel_id=1, source_target_pairs={{0,1},{1,0},{2,3},{3,2},{4,5},{5,4},{6,7},{7,6},{8,9},{9,8},{10,11... | collective-permute-start | bytes 1544 | tf_op jit(solution)/shard_map/ppermute | solution.py:293
  31.3 2.3 %copy-start.1 = (bf16[9,128,2048]{2,1,0:T(8,128)(2,1)S(1)}, bf16[9,128,2048]{2,1,0:T(8,128)(2,1)}, u32[]{:S(2)}) copy-start(bf16[9,128,2048]{2,1,0:T(8,128)(2,1)} %w_own.6) | copy-start | bytes 14155780
  37.7 7.7 %collective-permute-start.11 = (bf16[576,128]{1,0:T(8,128)(2,1)S(1)}, bf16[576,128]{1,0:T(8,128)(2,1)S(1)}, u32[]{:S(2)}, u32[]{:S(2)}) collective-permute-start(bf16[576,128]{1,0:T(8,128)(2,1)S(1)} %get-tuple-element.76), channel_id=1, source_target_pairs={{0,1},{1,0},{2,3},{3,2},{4,5},{5,4},{6,7},{7,6},{8,9},{9,8},{10,11... | collective-permute-start | bytes 442376 | tf_op jit(solution)/shard_map/ppermute | solution.py:293
  37.7 7.7 %slice-start = ((s8[4718592]{0:T(1024)(128)(4,1)}), s8[4194304]{0:T(1024)(128)(4,1)S(1)}, s32[]{:S(2)}) async-start(s8[4718592]{0:T(1024)(128)(4,1)} %bitcast.15), calls=%async_computation | async-start | bytes 8388608
  37.8 6.3 %collective-permute-start.9 = (bf16[288,256]{1,0:T(8,128)(2,1)S(1)}, bf16[288,256]{1,0:T(8,128)(2,1)S(1)}, u32[]{:S(2)}, u32[]{:S(2)}) collective-permute-start(bf16[288,256]{1,0:T(8,128)(2,1)S(1)} %slice.21), channel_id=1, source_target_pairs={{0,2},{1,3},{4,0},{5,1},{8,4},{9,5},{12,8},{13,9},{14,12},{15,13},... | collective-permute-start | bytes 442376 | tf_op jit(solution)/shard_map/ppermute | solution.py:292
  39.4 5.9 %collective-permute-start.8 = (bf16[288,256]{1,0:T(8,128)(2,1)S(1)}, bf16[288,256]{1,0:T(8,128)(2,1)S(1)}, u32[]{:S(2)}, u32[]{:S(2)}) collective-permute-start(bf16[288,256]{1,0:T(8,128)(2,1)S(1)} %slice.20), channel_id=1, source_target_pairs={{0,4},{1,5},{4,8},{5,9},{8,12},{9,13},{12,14},{13,15},{14,10},{15,... | collective-permute-start | bytes 442376 | tf_op jit(solution)/shard_map/ppermute | solution.py:291
  39.9 5.5 %slice-start.1 = ((s8[4718592]{0:T(1024)(128)(4,1)}), s8[524288]{0:T(1024)(128)(4,1)S(1)}, s32[]{:S(2)}) async-start(s8[4718592]{0:T(1024)(128)(4,1)} %bitcast.15), calls=%async_computation.1 | async-start | bytes 1048576
  44.1 22.3 %collective-permute-start.38 = (bf16[576,256]{1,0:T(8,128)(2,1)S(1)}, bf16[576,256]{1,0:T(8,128)(2,1)S(1)}, u32[]{:S(2)}, u32[]{:S(2)}) collective-permute-start(bf16[576,256]{1,0:T(8,128)(2,1)S(1)} %collective-permute-done.4.refs_2_.refs_0_), channel_id=1, source_target_pairs={{0,16},{16,0},{1,17},{17,1},{2,18},{18,2},{3,19},{19,3},{4,20},{20... | collective-permute-start | bytes 884744 | tf_op jit(solution)/shard_map/ppermute | solution.py:295
  49.2 17.1 %copy-start.10 = (bf16[576,128]{1,0:T(8,128)(2,1)}, bf16[576,128]{1,0:T(8,128)(2,1)S(1)}, u32[]{:S(2)}) copy-start(bf16[576,128]{1,0:T(8,128)(2,1)S(1)} %get-tuple-element.66.refs_0_) | copy-start | bytes 442372
  52.5 6.1 %collective-permute-start.13 = (bf16[288,256]{1,0:T(8,128)(2,1)S(1)}, bf16[288,256]{1,0:T(8,128)(2,1)S(1)}, u32[]{:S(2)}, u32[]{:S(2)}) collective-permute-start(bf16[288,256]{1,0:T(8,128)(2,1)S(1)} %get-tuple-element.52), channel_id=1, source_target_pairs={{0,4},{1,5},{4,8},{5,9},{8,12},{9,13},{12,14},{13,15},{14,10},{15,... | collective-permute-start | bytes 442376 | tf_op jit(solution)/shard_map/ppermute | solution.py:291
  53.4 6.0 %collective-permute-start.14 = (bf16[288,256]{1,0:T(8,128)(2,1)S(1)}, bf16[288,256]{1,0:T(8,128)(2,1)S(1)}, u32[]{:S(2)}, u32[]{:S(2)}) collective-permute-start(bf16[288,256]{1,0:T(8,128)(2,1)S(1)} %get-tuple-element.53), channel_id=1, source_target_pairs={{0,2},{1,3},{4,0},{5,1},{8,4},{9,5},{12,8},{13,9},{14,12},{15,13},... | collective-permute-start | bytes 442376 | tf_op jit(solution)/shard_map/ppermute | solution.py:292
  58.5 10.6 %collective-permute-start.37 = (bf16[576,256]{1,0:T(8,128)(2,1)S(1)}, bf16[576,256]{1,0:T(8,128)(2,1)S(1)}, u32[]{:S(2)}, u32[]{:S(2)}) collective-permute-start(bf16[576,256]{1,0:T(8,128)(2,1)S(1)} %collective-permute-done.4.refs_2_.refs_0_), channel_id=1, source_target_pairs={{0,1},{1,0},{2,3},{3,2},{4,5},{5,4},{6,7},{7,6},{8,9},{9,8},{10,11... | collective-permute-start | bytes 884744 | tf_op jit(solution)/shard_map/ppermute | solution.py:293
  58.6 12.9 %collective-permute-start.47 = (bf16[576,256]{1,0:T(8,128)(2,1)S(1)}, bf16[576,256]{1,0:T(8,128)(2,1)}, u32[]{:S(2)}, u32[]{:S(2)}) collective-permute-start(bf16[576,256]{1,0:T(8,128)(2,1)S(1)} %collective-permute-done.2.refs_1_.refs_4_), channel_id=1, source_target_pairs={{0,16},{16,0},{1,17},{17,1},{2,18},{18,2},{3,19},{19,3},{4,20},{20... | collective-permute-start | bytes 884744 | tf_op jit(solution)/shard_map/ppermute | solution.py:295
  59.4 6.7 %collective-permute-start.45 = (bf16[576,256]{1,0:T(8,128)(2,1)}, bf16[576,256]{1,0:T(8,128)(2,1)S(1)}, u32[]{:S(2)}, u32[]{:S(2)}) collective-permute-start(bf16[576,256]{1,0:T(8,128)(2,1)} %collective-permute-done.44.refs_2_), channel_id=1, source_target_pairs={{0,1},{1,0},{2,3},{3,2},{4,5},{5,4},{6,7},{7,6},{8,9},{9,8},{10,11... | collective-permute-start | bytes 884744 | tf_op jit(solution)/shard_map/ppermute | solution.py:293
  65.6 6.0 %copy-start.2 = (f32[576,256]{1,0:T(8,128)}, f32[576,256]{1,0:T(8,128)S(1)}, u32[]{:S(2)}) copy-start(f32[576,256]{1,0:T(8,128)S(1)} %get-tuple-element.59) | copy-start | bytes 1769476
  65.6 6.0 %copy-start.3 = (f32[576,256]{1,0:T(8,128)}, f32[576,256]{1,0:T(8,128)S(1)}, u32[]{:S(2)}) copy-start(f32[576,256]{1,0:T(8,128)S(1)} %get-tuple-element.63) | copy-start | bytes 1769476
  65.6 6.0 %copy-start.4 = (f32[576,256]{1,0:T(8,128)}, f32[576,256]{1,0:T(8,128)S(1)}, u32[]{:S(2)}) copy-start(f32[576,256]{1,0:T(8,128)S(1)} %get-tuple-element.57) | copy-start | bytes 1769476
  65.6 2.0 %collective-permute-start.22 = (bf16[576,128]{1,0:T(8,128)(2,1)S(1)}, bf16[576,128]{1,0:T(8,128)(2,1)S(1)}, u32[]{:S(2)}, u32[]{:S(2)}) collective-permute-start(bf16[576,128]{1,0:T(8,128)(2,1)S(1)} %get-tuple-element.67), channel_id=1, source_target_pairs={{0,1},{1,0},{2,3},{3,2},{4,5},{5,4},{6,7},{7,6},{8,9},{9,8},{10,11... | collective-permute-start | bytes 442376 | tf_op jit(solution)/shard_map/ppermute | solution.py:293
  66.1 6.9 %copy-start.8 = (bf16[576,256]{1,0:T(8,128)(2,1)}, bf16[576,256]{1,0:T(8,128)(2,1)S(1)}, u32[]{:S(2)}) copy-start(bf16[576,256]{1,0:T(8,128)(2,1)S(1)} %collective-permute-done.45.refs_3_) | copy-start | bytes 884740
  66.1 5.4 %collective-permute-start.12 = (bf16[576,128]{1,0:T(8,128)(2,1)S(1)}, bf16[576,128]{1,0:T(8,128)(2,1)S(1)}, u32[]{:S(2)}, u32[]{:S(2)}) collective-permute-start(bf16[576,128]{1,0:T(8,128)(2,1)S(1)} %get-tuple-element.50), channel_id=1, source_target_pairs={{0,1},{1,0},{2,3},{3,2},{4,5},{5,4},{6,7},{7,6},{8,9},{9,8},{10,11... | collective-permute-start | bytes 442376 | tf_op jit(solution)/shard_map/ppermute | solution.py:293
  66.4 6.7 %collective-permute-start.23 = (bf16[576,128]{1,0:T(8,128)(2,1)S(1)}, bf16[576,128]{1,0:T(8,128)(2,1)S(1)}, u32[]{:S(2)}, u32[]{:S(2)}) collective-permute-start(bf16[576,128]{1,0:T(8,128)(2,1)S(1)} %get-tuple-element.66.refs_0_), channel_id=1, source_target_pairs={{0,16},{16,0},{1,17},{17,1},{2,18},{18,2},{3,19},{19,3},{4,20},{20... | collective-permute-start | bytes 442376 | tf_op jit(solution)/shard_map/ppermute | solution.py:295
  67.7 6.0 %copy-start.12 = (bf16[576,128]{1,0:T(8,128)(2,1)}, bf16[576,128]{1,0:T(8,128)(2,1)S(1)}, u32[]{:S(2)}) copy-start(bf16[576,128]{1,0:T(8,128)(2,1)S(1)} %collective-permute-done.22.refs_1_) | copy-start | bytes 442372
  67.7 8.0 %collective-permute-start.24 = (bf16[576,128]{1,0:T(8,128)(2,1)S(1)}, bf16[576,128]{1,0:T(8,128)(2,1)S(1)}, u32[]{:S(2)}, u32[]{:S(2)}) collective-permute-start(bf16[576,128]{1,0:T(8,128)(2,1)S(1)} %collective-permute-done.22.refs_1_), channel_id=1, source_target_pairs={{0,16},{16,0},{1,17},{17,1},{2,18},{18,2},{3,19},{19,3},{4,20},{20... | collective-permute-start | bytes 442376 | tf_op jit(solution)/shard_map/ppermute | solution.py:295
  69.2 3.0 %copy-start.6 = (bf16[576,256]{1,0:T(8,128)(2,1)}, bf16[576,256]{1,0:T(8,128)(2,1)S(1)}, u32[]{:S(2)}) copy-start(bf16[576,256]{1,0:T(8,128)(2,1)S(1)} %collective-permute-done.37.refs_1_) | copy-start | bytes 884740
  69.2 17.3 %collective-permute-start.18 = (bf16[576,256]{1,0:T(8,128)(2,1)}, bf16[576,256]{1,0:T(8,128)(2,1)}, u32[]{:S(2)}, u32[]{:S(2)}) collective-permute-start(bf16[576,256]{1,0:T(8,128)(2,1)} %pad_maximum_fusion.1), channel_id=1, source_target_pairs={{0,2},{1,3},{4,0},{5,1},{8,4},{9,5},{12,8},{13,9},{14,12},{15,13},... | collective-permute-start | bytes 884744 | tf_op jit(solution)/shard_map/ppermute | solution.py:292
  71.5 16.7 %collective-permute-start.46 = (bf16[576,256]{1,0:T(8,128)(2,1)S(1)}, bf16[576,256]{1,0:T(8,128)(2,1)}, u32[]{:S(2)}, u32[]{:S(2)}) collective-permute-start(bf16[576,256]{1,0:T(8,128)(2,1)S(1)} %collective-permute-done.2.refs_1_.refs_4_), channel_id=1, source_target_pairs={{0,1},{1,0},{2,3},{3,2},{4,5},{5,4},{6,7},{7,6},{8,9},{9,8},{10,11... | collective-permute-start | bytes 884744 | tf_op jit(solution)/shard_map/ppermute | solution.py:293
  71.6 16.8 %collective-permute-start.39 = (bf16[576,256]{1,0:T(8,128)(2,1)S(1)}, bf16[576,256]{1,0:T(8,128)(2,1)}, u32[]{:S(2)}, u32[]{:S(2)}) collective-permute-start(bf16[576,256]{1,0:T(8,128)(2,1)S(1)} %collective-permute-done.38.refs_2_), channel_id=1, source_target_pairs={{0,1},{1,0},{2,3},{3,2},{4,5},{5,4},{6,7},{7,6},{8,9},{9,8},{10,11... | collective-permute-start | bytes 884744 | tf_op jit(solution)/shard_map/ppermute | solution.py:293
  73.7 16.2 %collective-permute-start.48 = (bf16[576,256]{1,0:T(8,128)(2,1)}, bf16[576,256]{1,0:T(8,128)(2,1)}, u32[]{:S(2)}, u32[]{:S(2)}) collective-permute-start(bf16[576,256]{1,0:T(8,128)(2,1)} %collective-permute-done.47.refs_6_), channel_id=1, source_target_pairs={{0,1},{1,0},{2,3},{3,2},{4,5},{5,4},{6,7},{7,6},{8,9},{9,8},{10,11... | collective-permute-start | bytes 884744 | tf_op jit(solution)/shard_map/ppermute | solution.py:293
  76.3 14.2 %collective-permute-start.15 = (bf16[576,256]{1,0:T(8,128)(2,1)}, bf16[576,256]{1,0:T(8,128)(2,1)}, u32[]{:S(2)}, u32[]{:S(2)}) collective-permute-start(bf16[576,256]{1,0:T(8,128)(2,1)} %pad_maximum_fusion), channel_id=1, source_target_pairs={{0,4},{1,5},{4,8},{5,9},{8,12},{9,13},{12,14},{13,15},{14,10},{15,... | collective-permute-start | bytes 884744 | tf_op jit(solution)/shard_map/ppermute | solution.py:291
  86.5 10.2 %collective-permute-start.41 = (bf16[576,256]{1,0:T(8,128)(2,1)}, bf16[576,256]{1,0:T(8,128)(2,1)S(1)}, u32[]{:S(2)}, u32[]{:S(2)}) collective-permute-start(bf16[576,256]{1,0:T(8,128)(2,1)} %collective-permute-done.3.refs_1_.refs_4_), channel_id=1, source_target_pairs={{0,16},{16,0},{1,17},{17,1},{2,18},{18,2},{3,19},{19,3},{4,20},{20... | collective-permute-start | bytes 884744 | tf_op jit(solution)/shard_map/ppermute | solution.py:295
  88.3 16.9 %collective-permute-start.40 = (bf16[576,256]{1,0:T(8,128)(2,1)}, bf16[576,256]{1,0:T(8,128)(2,1)S(1)}, u32[]{:S(2)}, u32[]{:S(2)}) collective-permute-start(bf16[576,256]{1,0:T(8,128)(2,1)} %collective-permute-done.3.refs_1_.refs_4_), channel_id=1, source_target_pairs={{0,1},{1,0},{2,3},{3,2},{4,5},{5,4},{6,7},{7,6},{8,9},{9,8},{10,11... | collective-permute-start | bytes 884744 | tf_op jit(solution)/shard_map/ppermute | solution.py:293
  88.4 16.8 %collective-permute-start.32 = (bf16[576,256]{1,0:T(8,128)(2,1)S(1)}, bf16[576,256]{1,0:T(8,128)(2,1)S(1)}, u32[]{:S(2)}, u32[]{:S(2)}) collective-permute-start(bf16[576,256]{1,0:T(8,128)(2,1)S(1)} %collective-permute-done.5.refs_2_.refs_0_), channel_id=1, source_target_pairs={{0,16},{16,0},{1,17},{17,1},{2,18},{18,2},{3,19},{19,3},{4,20},{20... | collective-permute-start | bytes 884744 | tf_op jit(solution)/shard_map/ppermute | solution.py:295
  89.9 17.7 %collective-permute-start.35 = (bf16[576,256]{1,0:T(8,128)(2,1)S(1)}, bf16[576,256]{1,0:T(8,128)(2,1)S(1)}, u32[]{:S(2)}, u32[]{:S(2)}) collective-permute-start(bf16[576,256]{1,0:T(8,128)(2,1)S(1)} %collective-permute-done.6.refs_1_.refs_4_), channel_id=1, source_target_pairs={{0,16},{16,0},{1,17},{17,1},{2,18},{18,2},{3,19},{19,3},{4,20},{20... | collective-permute-start | bytes 884744 | tf_op jit(solution)/shard_map/ppermute | solution.py:295
  90.5 17.1 %collective-permute-start.19 = (bf16[576,256]{1,0:T(8,128)(2,1)S(1)}, bf16[576,256]{1,0:T(8,128)(2,1)S(1)}, u32[]{:S(2)}, u32[]{:S(2)}) collective-permute-start(bf16[576,256]{1,0:T(8,128)(2,1)S(1)} %add_convert_fusion.2), channel_id=1, source_target_pairs={{0,2},{1,3},{4,0},{5,1},{8,4},{9,5},{12,8},{13,9},{14,12},{15,13},... | collective-permute-start | bytes 884744 | tf_op jit(solution)/shard_map/ppermute | solution.py:292
  96.6 11.6 %collective-permute-start.16 = (bf16[576,256]{1,0:T(8,128)(2,1)S(1)}, bf16[576,256]{1,0:T(8,128)(2,1)S(1)}, u32[]{:S(2)}, u32[]{:S(2)}) collective-permute-start(bf16[576,256]{1,0:T(8,128)(2,1)S(1)} %add_convert_fusion.4), channel_id=1, source_target_pairs={{0,4},{1,5},{4,8},{5,9},{8,12},{9,13},{12,14},{13,15},{14,10},{15,... | collective-permute-start | bytes 884744 | tf_op jit(solution)/shard_map/ppermute | solution.py:291
  98.2 1.0 copy-start.9
  99.1 13.4 %copy-start.7 = (bf16[576,256]{1,0:T(8,128)(2,1)S(1)}, bf16[576,256]{1,0:T(8,128)(2,1)}, u32[]{:S(2)}) copy-start(bf16[576,256]{1,0:T(8,128)(2,1)} %copy-done.6) | copy-start | bytes 884740
  105.2 3.2 %collective-permute-start.31 = (bf16[576,256]{1,0:T(8,128)(2,1)S(1)}, bf16[576,256]{1,0:T(8,128)(2,1)S(1)}, u32[]{:S(2)}, u32[]{:S(2)}) collective-permute-start(bf16[576,256]{1,0:T(8,128)(2,1)S(1)} %collective-permute-done.5.refs_2_.refs_0_), channel_id=1, source_target_pairs={{0,1},{1,0},{2,3},{3,2},{4,5},{5,4},{6,7},{7,6},{8,9},{9,8},{10,11... | collective-permute-start | bytes 884744 | tf_op jit(solution)/shard_map/ppermute | solution.py:293
  105.2 5.7 %collective-permute-start.34 = (bf16[576,256]{1,0:T(8,128)(2,1)S(1)}, bf16[576,256]{1,0:T(8,128)(2,1)S(1)}, u32[]{:S(2)}, u32[]{:S(2)}) collective-permute-start(bf16[576,256]{1,0:T(8,128)(2,1)S(1)} %collective-permute-done.6.refs_1_.refs_4_), channel_id=1, source_target_pairs={{0,1},{1,0},{2,3},{3,2},{4,5},{5,4},{6,7},{7,6},{8,9},{9,8},{10,11... | collective-permute-start | bytes 884744 | tf_op jit(solution)/shard_map/ppermute | solution.py:293
  107.6 1.6 %collective-permute-start.42 = (bf16[576,256]{1,0:T(8,128)(2,1)S(1)}, bf16[576,256]{1,0:T(8,128)(2,1)S(1)}, u32[]{:S(2)}, u32[]{:S(2)}) collective-permute-start(bf16[576,256]{1,0:T(8,128)(2,1)S(1)} %collective-permute-done.41.refs_6_), channel_id=1, source_target_pairs={{0,1},{1,0},{2,3},{3,2},{4,5},{5,4},{6,7},{7,6},{8,9},{9,8},{10,11... | collective-permute-start | bytes 884744 | tf_op jit(solution)/shard_map/ppermute | solution.py:293
  107.6 2.9 %collective-permute-start.33 = (bf16[576,256]{1,0:T(8,128)(2,1)S(1)}, bf16[576,256]{1,0:T(8,128)(2,1)S(1)}, u32[]{:S(2)}, u32[]{:S(2)}) collective-permute-start(bf16[576,256]{1,0:T(8,128)(2,1)S(1)} %collective-permute-done.32.refs_2_), channel_id=1, source_target_pairs={{0,1},{1,0},{2,3},{3,2},{4,5},{5,4},{6,7},{7,6},{8,9},{9,8},{10,11... | collective-permute-start | bytes 884744 | tf_op jit(solution)/shard_map/ppermute | solution.py:293
  108.2 10.1 %collective-permute-start.36 = (bf16[576,256]{1,0:T(8,128)(2,1)S(1)}, bf16[576,256]{1,0:T(8,128)(2,1)S(1)}, u32[]{:S(2)}, u32[]{:S(2)}) collective-permute-start(bf16[576,256]{1,0:T(8,128)(2,1)S(1)} %collective-permute-done.35.refs_6_), channel_id=1, source_target_pairs={{0,1},{1,0},{2,3},{3,2},{4,5},{5,4},{6,7},{7,6},{8,9},{9,8},{10,11... | collective-permute-start | bytes 884744 | tf_op jit(solution)/shard_map/ppermute | solution.py:293
  108.4 14.6 %collective-permute-start.26 = (bf16[576,256]{1,0:T(8,128)(2,1)S(1)}, bf16[576,256]{1,0:T(8,128)(2,1)S(1)}, u32[]{:S(2)}, u32[]{:S(2)}) collective-permute-start(bf16[576,256]{1,0:T(8,128)(2,1)S(1)} %collective-permute-done.7.refs_2_.refs_0_), channel_id=1, source_target_pairs={{0,16},{16,0},{1,17},{17,1},{2,18},{18,2},{3,19},{19,3},{4,20},{20... | collective-permute-start | bytes 884744 | tf_op jit(solution)/shard_map/ppermute | solution.py:295
  109.2 15.0 %collective-permute-start.29 = (bf16[576,256]{1,0:T(8,128)(2,1)S(1)}, bf16[576,256]{1,0:T(8,128)(2,1)S(1)}, u32[]{:S(2)}, u32[]{:S(2)}) collective-permute-start(bf16[576,256]{1,0:T(8,128)(2,1)S(1)} %constant_dynamic-update-slice_fusion.refs_4_), channel_id=1, source_target_pairs={{0,16},{16,0},{1,17},{17,1},{2,18},{18,2},{3,19},{19,3},{4,20},{20... | collective-permute-start | bytes 884744 | tf_op jit(solution)/shard_map/ppermute | solution.py:295
  110.5 13.7 %collective-permute-start.20 = (bf16[576,256]{1,0:T(8,128)(2,1)S(1)}, bf16[576,256]{1,0:T(8,128)(2,1)S(1)}, u32[]{:S(2)}, u32[]{:S(2)}) collective-permute-start(bf16[576,256]{1,0:T(8,128)(2,1)S(1)} %add_convert_fusion.1), channel_id=1, source_target_pairs={{0,2},{1,3},{4,0},{5,1},{8,4},{9,5},{12,8},{13,9},{14,12},{15,13},... | collective-permute-start | bytes 884744 | tf_op jit(solution)/shard_map/ppermute | solution.py:292
  110.9 13.8 %collective-permute-start.17 = (bf16[576,256]{1,0:T(8,128)(2,1)S(1)}, bf16[576,256]{1,0:T(8,128)(2,1)S(1)}, u32[]{:S(2)}, u32[]{:S(2)}) collective-permute-start(bf16[576,256]{1,0:T(8,128)(2,1)S(1)} %add_convert_fusion.3), channel_id=1, source_target_pairs={{0,4},{1,5},{4,8},{5,9},{8,12},{9,13},{12,14},{13,15},{14,10},{15,... | collective-permute-start | bytes 884744 | tf_op jit(solution)/shard_map/ppermute | solution.py:291
  118.3 6.4 %copy-start.5 = (f32[576,256]{1,0:T(8,128)S(1)}, f32[576,256]{1,0:T(8,128)}, u32[]{:S(2)}) copy-start(f32[576,256]{1,0:T(8,128)} %copy-done.4) | copy-start | bytes 1769476
  118.3 6.6 %collective-permute-start.25 = (bf16[576,256]{1,0:T(8,128)(2,1)S(1)}, bf16[576,256]{1,0:T(8,128)(2,1)S(1)}, u32[]{:S(2)}, u32[]{:S(2)}) collective-permute-start(bf16[576,256]{1,0:T(8,128)(2,1)S(1)} %collective-permute-done.7.refs_2_.refs_0_), channel_id=1, source_target_pairs={{0,1},{1,0},{2,3},{3,2},{4,5},{5,4},{6,7},{7,6},{8,9},{9,8},{10,11... | collective-permute-start | bytes 884744 | tf_op jit(solution)/shard_map/ppermute | solution.py:293
  123.0 1.9 %collective-permute-start.28 = (bf16[576,256]{1,0:T(8,128)(2,1)S(1)}, bf16[576,256]{1,0:T(8,128)(2,1)S(1)}, u32[]{:S(2)}, u32[]{:S(2)}) collective-permute-start(bf16[576,256]{1,0:T(8,128)(2,1)S(1)} %constant_dynamic-update-slice_fusion.refs_4_), channel_id=1, source_target_pairs={{0,1},{1,0},{2,3},{3,2},{4,5},{5,4},{6,7},{7,6},{8,9},{9,8},{10,11... | collective-permute-start | bytes 884744 | tf_op jit(solution)/shard_map/ppermute | solution.py:293
  124.2 1.6 %collective-permute-start.27 = (bf16[576,256]{1,0:T(8,128)(2,1)S(1)}, bf16[576,256]{1,0:T(8,128)(2,1)S(1)}, u32[]{:S(2)}, u32[]{:S(2)}) collective-permute-start(bf16[576,256]{1,0:T(8,128)(2,1)S(1)} %collective-permute-done.26.refs_2_), channel_id=1, source_target_pairs={{0,1},{1,0},{2,3},{3,2},{4,5},{5,4},{6,7},{7,6},{8,9},{9,8},{10,11... | collective-permute-start | bytes 884744 | tf_op jit(solution)/shard_map/ppermute | solution.py:293
  124.2 2.0 %collective-permute-start.30 = (bf16[576,256]{1,0:T(8,128)(2,1)S(1)}, bf16[576,256]{1,0:T(8,128)(2,1)S(1)}, u32[]{:S(2)}, u32[]{:S(2)}) collective-permute-start(bf16[576,256]{1,0:T(8,128)(2,1)S(1)} %collective-permute-done.29.refs_6_), channel_id=1, source_target_pairs={{0,1},{1,0},{2,3},{3,2},{4,5},{5,4},{6,7},{7,6},{8,9},{9,8},{10,11... | collective-permute-start | bytes 884744 | tf_op jit(solution)/shard_map/ppermute | solution.py:293
  124.8 6.1 %collective-permute-start.21 = (bf16[576,128]{1,0:T(8,128)(2,1)S(1)}, bf16[576,128]{1,0:T(8,128)(2,1)S(1)}, u32[]{:S(2)}, u32[]{:S(2)}) collective-permute-start(bf16[576,128]{1,0:T(8,128)(2,1)S(1)} %get-tuple-element.75), channel_id=1, source_target_pairs={{0,1},{1,0},{2,3},{3,2},{4,5},{5,4},{6,7},{7,6},{8,9},{9,8},{10,11... | collective-permute-start | bytes 442376 | tf_op jit(solution)/shard_map/ppermute | solution.py:293
  (6 other events, 4.9 us)
where the time goes:
time: 133 us; the launch traced here: 132 us
  Pallas kernels  53.1 us (40%)
  starting transfers between devices  33.7 us (25%)
  waiting for transfers between devices  20.2 us (15%)
  local copies, waits for them, and re-layouts  18.5 us (14%)
  other arithmetic  5.21 us (4%)
    pallas_call x4, Pallas kernels, weight_grad_call(): pl.pallas_call(functools.partial(weight_grad_kernel, blocks, pieces, scal...  21.2 us
    unnamed x47, local copies, waits for them, and re-layouts  13.7 us
    pallas_call x3, Pallas kernels, input_grad_call(): pl.pallas_call(functools.partial(input_grad_kernel, slots, pieces), out_s...  13.1 us
    pallas_call x3, Pallas kernels, forward_call(): pl.pallas_call(functools.partial(forward_kernel, slots, carry is not None...  12.7 us
    ppermute x8, starting transfers between devices, body(): back = lambda v: lax.ppermute(v, 'filt', backwards)  10.8 us
    ppermute x10, starting transfers between devices, body(): across = lambda v: lax.ppermute(v, 'case', [(0, 1), (1, 0)])  9.58 us
    ppermute x10, waiting for transfers between devices, body(): across = lambda v: lax.ppermute(v, 'case', [(0, 1), (1, 0)])  9.22 us
    ppermute x8, starting transfers between devices, body(): onward = lambda v: lax.ppermute(v, 'filt', forwards)  8.17 us
  transfers between devices with their start and end apart: 49, of which 12 were waited for; matrix products, arithmetic and copies ran while one was open for 8% of the time, Pallas kernels for 40%

commit v1 on v0

v1 whole, which is shorter than its diff:
```python
import functools

import jax
import jax.numpy as jnp
import numpy as np
from jax import lax
from jax.experimental import pallas as pl
from jax.experimental.pallas import tpu as pltpu
from jax.sharding import PartitionSpec as P

GRID = 24
FIELD = GRID * GRID
STEPS = (-1, 0, 1)
EDGE = 8
F32 = jnp.float32
BF16 = jnp.bfloat16
MIB = 1024 * 1024
LIGHT = pl.CostEstimate(flops=1000, transcendentals=0, bytes_accessed=1000)
VMEM = pl.BlockSpec(memory_space=pltpu.VMEM)
SMEM = pl.BlockSpec(memory_space=pltpu.SMEM)
ANY = pl.BlockSpec(memory_space=pl.ANY)
TOKEN = jax.ShapeDtypeStruct((8, 128), F32)


def chip_cycle(chips):
    rows = 4
    cols = chips // rows
    walk = [(r, 0) for r in range(rows)]
    for r in reversed(range(rows)):
        across = range(1, cols) if (rows - 1 - r) % 2 == 0 else reversed(range(1, cols))
        walk += [(r, c) for c in across]
    return [r * cols + c for r, c in walk]


def rows_moved(v, a):
    if a == 0:
        return v
    gap = jnp.zeros((GRID, v.shape[1]), v.dtype)
    pieces = []
    for s in range(0, v.shape[0], FIELD):
        pieces += [v[s + GRID : s + FIELD], gap] if a > 0 else [gap, v[s : s + FIELD - GRID]]
    return jnp.concatenate(pieces, axis=0)


def grid_columns(cells, lanes):
    r = lax.broadcasted_iota(jnp.int32, (cells, lanes), 0)
    return lax.rem(r, GRID)


def columns_moved(field, v, b, col):
    if b == 0:
        return v
    cells, lanes = v.shape
    field[EDGE : EDGE + cells, :lanes] = v
    moved = field[EDGE + b : EDGE + b + cells, :lanes]
    ok = col >= 1 if b < 0 else col < GRID - 1
    return jnp.where(ok, moved, 0.0)


def clear_edges(field):
    rows, lanes = field.shape
    field[0:EDGE, :] = jnp.zeros((EDGE, lanes), field.dtype)
    field[rows - EDGE : rows, :] = jnp.zeros((EDGE, lanes), field.dtype)


def hold_kernel(w_own, w_sib, out, token, sems):
    part = w_own.shape[1]
    token[...] = jnp.zeros(token.shape, F32)
    copies = [
        pltpu.make_async_copy(w, out.at[:, n * part : (n + 1) * part], sems.at[n])
        for n, w in enumerate((w_own, w_sib))
    ]
    for copy in copies:
        copy.start()
    for copy in copies:
        copy.wait()


def hold_call(w_own, w_sib):
    taps, part, channels = w_own.shape
    return pl.pallas_call(
        hold_kernel,
        out_shape=[jax.ShapeDtypeStruct((taps, 2 * part, channels), BF16), TOKEN],
        in_specs=[pl.BlockSpec(memory_space=pltpu.HBM)] * 2,
        out_specs=[VMEM] * 2,
        scratch_shapes=[pltpu.SemaphoreType.DMA((2,))],
        compiler_params=pltpu.CompilerParams(vmem_limit_bytes=12 * MIB),
        cost_estimate=LIGHT,
        name="hold",
    )(w_own, w_sib)


def forward_sums(q_ref, slots, xs, w_all, carry, b):
    lanes = xs[0][0].shape[1] if isinstance(xs[0], (list, tuple)) else xs[0].shape[1]
    total = None if carry is None else carry
    for a in STEPS:
        tap = (a + 1) * 3 + b + 1
        part = None
        for n, x in zip(slots, xs):
            cols = pl.ds(pl.multiple_of(q_ref[n] * lanes, lanes), lanes)
            w = w_all[tap, :, cols]
            v = jnp.concatenate([p[...] for p in x], axis=0) if isinstance(x, (list, tuple)) else x[...]
            y = lax.dot_general(v, w, (((1,), (1,)), ((), ())), preferred_element_type=F32)
            part = y if part is None else part + y
        part = rows_moved(part, a)
        total = part if total is None else total + part
    return total


def forward_kernel(slots, has_carry, q_ref, after, w_all, *refs):
    refs = list(refs)
    carry = refs.pop(0) if has_carry else None
    xs, out, token = refs[:-2], refs[-2], refs[-1]
    token[...] = jnp.zeros(token.shape, F32)
    for b in STEPS:
        before = carry[b + 1] if has_carry else None
        out[b + 1] = forward_sums(q_ref, slots, xs, w_all, before, b)


def forward_call(q, after, slots, xs, w_all, carry):
    cells, lanes = xs[0].shape
    outs = w_all.shape[1]
    args = ([] if carry is None else [carry]) + list(xs)
    return pl.pallas_call(
        functools.partial(forward_kernel, slots, carry is not None),
        out_shape=[jax.ShapeDtypeStruct((3, cells, outs), F32), TOKEN],
        in_specs=[SMEM, ANY] + [VMEM] * (1 + len(args)),
        out_specs=[VMEM] * 2,
        compiler_params=pltpu.CompilerParams(vmem_limit_bytes=8 * MIB),
        cost_estimate=LIGHT,
        name="forward",
    )(q, after, w_all, *args)


def gate_kernel(slots, halves, q_ref, after, w_all, carry, bias, cot_own, cot_sib, *refs):
    xs = refs[: len(slots) * halves]
    act_own, act_sib, g_own, g_sib, g9, field = refs[len(slots) * halves :]
    xs = [xs[n : n + halves] for n in range(0, len(xs), halves)]
    cells = act_own.shape[0]
    part = act_own.shape[1]
    lanes = 2 * part
    col = grid_columns(cells, lanes)
    clear_edges(field)
    preact = bias[0:1, :]
    for b in (0, -1, 1):
        sums = forward_sums(q_ref, slots, xs, w_all, carry[b + 1], b)
        preact = preact + columns_moved(field, sums, b, col)
    gate = jax.nn.sigmoid(preact)
    act = (preact * gate).astype(BF16)
    act_own[...], act_sib[...] = act[:, :part], act[:, part:]
    cot = jnp.concatenate([cot_own[...], cot_sib[...]], axis=1).astype(F32)
    grad = (cot * gate * (1.0 + preact * (1.0 - gate))).astype(BF16)
    g_own[...], g_sib[...] = grad[:, :part], grad[:, part:]
    grad = grad.astype(F32)
    for b in STEPS:
        side = columns_moved(field, grad, -b, col)
        for a in STEPS:
            tap = (a + 1) * 3 + b + 1
            g9[:, tap * lanes : (tap + 1) * lanes] = rows_moved(side, -a).astype(BF16)


def gate_call(q, after, slots, xs, w_all, carry, bias, cot_own, cot_sib):
    cells = carry.shape[1]
    outs = carry.shape[2]
    part = outs // 2
    halves = len(xs[0])
    flat = [p for x in xs for p in x]
    piece = jax.ShapeDtypeStruct((cells, part), BF16)
    return pl.pallas_call(
        functools.partial(gate_kernel, slots, halves),
        out_shape=[piece] * 4 + [jax.ShapeDtypeStruct((cells, 9 * outs), BF16)],
        in_specs=[SMEM, ANY] + [VMEM] * (5 + len(flat)),
        out_specs=[VMEM] * 5,
        scratch_shapes=[pltpu.VMEM((cells + 2 * EDGE, outs), F32)],
        compiler_params=pltpu.CompilerParams(vmem_limit_bytes=10 * MIB),
        cost_estimate=LIGHT,
        name="gate",
    )(q, after, w_all, carry, bias, cot_own, cot_sib, *flat)


def input_grad_kernel(slots, pieces, q_ref, after, w_all, g9, *outs):
    lanes = outs[0].shape[1]
    outs = list(outs)
    token = outs.pop()
    token[...] = jnp.zeros(token.shape, F32)
    for n in slots:
        cols = pl.ds(pl.multiple_of(q_ref[n] * lanes, lanes), lanes)
        w = w_all[:, :, cols].reshape(-1, lanes)
        total = jnp.dot(g9[...], w, preferred_element_type=F32)
        rows = total.shape[0] // pieces
        for p in range(pieces):
            out = outs.pop(0)
            out[...] = total[p * rows : (p + 1) * rows].astype(out.dtype)


def input_grad_call(q, after, slots, dtype, pieces, g9, w_all, lanes):
    cells, depth = g9.shape
    count = len(slots) * pieces
    return pl.pallas_call(
        functools.partial(input_grad_kernel, slots, pieces),
        out_shape=[jax.ShapeDtypeStruct((cells // pieces, lanes), dtype)] * count + [TOKEN],
        in_specs=[SMEM, ANY] + [VMEM] * 2,
        out_specs=[VMEM] * (count + 1),
        compiler_params=pltpu.CompilerParams(vmem_limit_bytes=8 * MIB),
        cost_estimate=LIGHT,
        name="input_grad",
    )(q, after, w_all, g9)


def displaced_kernel(scale, core, after, act_own, act_sib, *refs):
    gs = refs[:-4]
    out, bias_out, act_out, field = refs[-4:]
    for c, order in enumerate(((act_own, act_sib), (act_sib, act_own))):

        @pl.when(core[0] == c)
        def _(order=order):
            act_out[...] = jnp.transpose(jnp.concatenate([v[...] for v in order], axis=0))

    cells = out.shape[1]
    part = out.shape[0] // 9
    clear_edges(field)
    grad = jnp.concatenate([g[...] for g in gs], axis=0).astype(F32)
    bias_out[...] = jnp.sum(grad, axis=0, keepdims=True) * scale
    col = grid_columns(cells, part)
    for b in STEPS:
        side = columns_moved(field, grad, -b, col)
        for a in STEPS:
            tap = (a + 1) * 3 + b + 1
            moved = rows_moved(side, -a).astype(BF16)
            out[tap * part : (tap + 1) * part, :] = jnp.transpose(moved)


def displaced_call(core, after, act_own, act_sib, gs, scale):
    cells = sum(g.shape[0] for g in gs)
    part = gs[0].shape[1]
    return pl.pallas_call(
        functools.partial(displaced_kernel, scale),
        out_shape=[
            jax.ShapeDtypeStruct((9 * part, cells), BF16),
            jax.ShapeDtypeStruct((1, part), F32),
            jax.ShapeDtypeStruct((part, 2 * act_own.shape[0]), BF16),
        ],
        in_specs=[SMEM, ANY] + [VMEM] * (2 + len(gs)),
        out_specs=[VMEM] * 3,
        scratch_shapes=[pltpu.VMEM((cells + 2 * EDGE, part), F32)],
        compiler_params=pltpu.CompilerParams(vmem_limit_bytes=10 * MIB),
        cost_estimate=LIGHT,
        name="displaced",
    )(core, after, act_own, act_sib, *gs)


def weight_grad_kernel(places, scale, q_ref, after, g9t, *refs):
    x = jnp.concatenate([x[...] for x in refs[:places]], axis=0)
    out, token = refs[-2:]
    token[...] = jnp.zeros(token.shape, F32)
    out[...] = jnp.dot(g9t[...], x, preferred_element_type=F32) * scale


def weight_grad_call(q, after, slots, g9t, xs, total, scale, channels):
    blocks = len(slots)
    rows, cells = g9t.shape
    lanes = xs[0].shape[1]
    first = slots[0]
    aliased = [] if total is None else [total]
    return pl.pallas_call(
        functools.partial(weight_grad_kernel, len(xs), scale),
        out_shape=[jax.ShapeDtypeStruct((rows, channels), F32), TOKEN],
        grid_spec=pltpu.PrefetchScalarGridSpec(
            num_scalar_prefetch=1,
            grid=(blocks,),
            in_specs=[ANY, VMEM]
            + [pl.BlockSpec((xs[0].shape[0] // blocks, lanes), lambda k, q: (k, 0))] * len(xs)
            + [ANY] * len(aliased),
            out_specs=[pl.BlockSpec((rows, lanes), lambda k, q: (0, q[first + k])), VMEM],
        ),
        input_output_aliases={3 + len(xs): 0} if aliased else {},
        compiler_params=pltpu.CompilerParams(
            dimension_semantics=("arbitrary",), vmem_limit_bytes=12 * MIB
        ),
        cost_estimate=LIGHT,
        name="weight_grad",
    )(q, after, g9t, *xs, *aliased)


def body(inputs, weight, bias_vector, cotangent):
    part, cells = inputs.shape
    devices = lax.axis_size("filt")
    case_rows = lax.axis_size("case")
    channels = part * devices
    chips = devices // 2
    half = cells // 2
    lanes = 2 * part
    far = chips // 2
    scale = 1.0 / (cells // FIELD * case_rows)

    cycle = chip_cycle(chips)
    offsets = [0]
    for d in range(1, far):
        offsets += [-d, d]
    offsets.append(far)
    slot = {d: n for n, d in enumerate(offsets)}
    place = {chip: n for n, chip in enumerate(cycle)}
    table = np.array(
        [[cycle[(place[chip] + d) % chips] for d in offsets] for chip in range(chips)], np.int32
    )
    me = lax.axis_index("filt")
    core = me % 2
    q = lax.dynamic_index_in_dim(jnp.asarray(table), me // 2, 0, keepdims=False)

    forwards, backwards = [], []
    for n, chip in enumerate(cycle):
        for c in range(2):
            forwards.append((2 * chip + c, 2 * cycle[(n + 1) % chips] + c))
            backwards.append((2 * chip + c, 2 * cycle[(n - 1) % chips] + c))
    swap = [(n, n ^ 1) for n in range(devices)]
    onward = lambda v: lax.ppermute(v, "filt", forwards)
    back = lambda v: lax.ppermute(v, "filt", backwards)
    sibling = lambda v: lax.ppermute(v, "filt", swap)
    pair = case_rows == 2
    across = lambda v: lax.ppermute(v, "case", [(0, 1), (1, 0)])
    tie = lambda *v: lax.optimization_barrier(v)

    x_t = jnp.transpose(inputs)
    mine = lax.dynamic_slice_in_dim(x_t, core * half, half, 0)
    theirs = sibling(lax.dynamic_slice_in_dim(x_t, (1 - core) * half, half, 0))
    own_block = jnp.where(
        core == 0,
        jnp.concatenate([mine, theirs], axis=1),
        jnp.concatenate([theirs, mine], axis=1),
    )
    block = {0: own_block, -1: onward(own_block), 1: back(own_block)}
    theirs, weight, cotangent, bias_vector = tie(theirs, weight, cotangent, bias_vector)
    w_own, w_sib = weight, sibling(weight)
    cot_t = jnp.transpose(cotangent)
    cot_own = lax.dynamic_slice_in_dim(cot_t, core * half, half, 0)
    cot_sib = sibling(lax.dynamic_slice_in_dim(cot_t, (1 - core) * half, half, 0))
    bias_row = bias_vector[None, :]
    bias_sib = sibling(bias_row)
    block[-1], block[1], cot_sib, bias_sib = tie(block[-1], block[1], cot_sib, bias_sib)
    bias_row = jnp.concatenate([bias_row, bias_sib], axis=1)

    stacks = []

    def stack(ds, parts):
        x = jnp.concatenate(parts, axis=0)
        stacks.append(([slot[d] for d in ds], x, across(x) if pair else None))

    w_all, token = hold_call(w_own, w_sib)
    for s in range(1, far):
        if s > 1:
            block[-s], block[s] = onward(block[-s + 1]), back(block[s - 1])
            if s == far - 1:
                early = offsets[: 2 * far - 3]
                carry, token = forward_call(
                    q, token, [slot[d] for d in early], [block[d] for d in early], w_all, None
                )
            block[-s], block[s], token = tie(block[-s], block[s], token)
        if s < far - 1:
            ds = [0, -1, 1] if s == 1 else [-s, s]
            stack(ds, [block[d] for d in ds])
    s = far - 1
    top, low = onward(block[-s][: half // 2]), back(block[s][half // 2 :])
    carry, token = forward_call(q, token, [slot[-s], slot[s]], [block[-s], block[s]], w_all, carry)
    tops = [top, low, token] + [x for _, _, x in stacks[:1] if pair]
    top, low, token, *done = tie(*tops)
    others = done
    act_own, act_sib, g_own, g_sib, g9 = gate_call(
        q, token, [slot[far]], [[top, low]], w_all, carry, bias_row, cot_own, cot_sib
    )

    grad_at = lambda after, ds, dtype, pieces=1: input_grad_call(
        q, after, [slot[d] for d in ds], dtype, pieces, g9, w_all, lanes
    )
    top_p, low_p, after_top = grad_at(token, [far], BF16, 2)
    ahead, behind = onward(top_p), back(low_p)
    act_recv, g_recv = sibling(act_sib), sibling(g_sib)
    p_ahead, p_behind, token = grad_at(after_top, [far - 1, -(far - 1)], F32)
    gs = [jnp.concatenate([g_own, g_recv], axis=0)]
    waits = [act_recv, gs[0]] + [x for _, _, x in stacks[1:] if pair]
    ahead, behind, token, act_recv, gs[0], *done = tie(ahead, behind, token, *waits)
    others += done
    if pair:
        gs.append(across(gs[0]))
    stack(
        [-(far - 1), far - 1, far], [block[-(far - 1)], block[far - 1], top, low]
    )
    hop = half // 2
    ahead = jnp.concatenate([p_ahead[:hop] + ahead.astype(F32), p_ahead[hop:]], axis=0)
    behind = jnp.concatenate([p_behind[:hop], p_behind[hop:] + behind.astype(F32)], axis=0)
    ahead, behind = tie(ahead.astype(BF16), behind.astype(BF16))
    ahead, behind = onward(ahead), back(behind)
    rest_ds = [d for n in range(far - 2, 0, -1) for d in (n, -n)] + [0]
    *rest, token = grad_at(token, rest_ds, F32)
    rest = dict(zip(rest_ds, rest))
    ahead, behind, token, *gs = tie(ahead, behind, token, *gs)

    g9t, bias_grad, activated = displaced_call(core[None], token, act_own, act_recv, gs, scale)
    state = {"total": None, "next": 0, "token": token}

    def weight_grads():
        n = state["next"]
        ids, x, _ = stacks[n]
        xs = [x, sibling(x)]
        if pair:
            xs += [others[n], sibling(others[n])]
        state["total"], state["token"] = weight_grad_call(
            q, state["token"], ids, g9t, xs, state["total"], scale, channels
        )
        state["next"] = n + 1
        return state["token"]

    for s in range(far - 2, 0, -1):
        ahead = (rest[s] + ahead.astype(F32)).astype(BF16)
        behind = (rest[-s] + behind.astype(F32)).astype(BF16)
        ahead, behind = tie(ahead, behind)
        ahead, behind = onward(ahead), back(behind)
        waits = [ahead, behind]
        if state["next"] < len(stacks) - 1:
            waits.append(weight_grads())
        else:
            waits.append(state["token"])
        if s == 1 and pair:
            waits.append(stacks[-1][2])
        ahead, behind, state["token"], *last = tie(*waits)
        others += last
    final = (rest[0] + ahead.astype(F32) + behind.astype(F32)).astype(BF16)
    keep = lax.dynamic_slice_in_dim(final, core * part, part, 1)
    other = sibling(lax.dynamic_slice_in_dim(final, (1 - core) * part, part, 1))
    while state["next"] < len(stacks):
        weight_grads()
    total = state["total"]
    input_grad = jnp.transpose(
        jnp.where(
            core == 0,
            jnp.concatenate([keep, other], axis=0),
            jnp.concatenate([other, keep], axis=0),
        )
    )
    bias_grad = bias_grad[0]
    if not pair:
        total, bias_grad = lax.psum((total, bias_grad), "case")
    weight_grad = total.reshape(9, part, channels)
    return activated, input_grad, weight_grad, bias_grad


def solution(mesh):
    in_specs = (P("filt", "case"), P(None, "filt", None), P("filt"), P("filt", "case"))
    out_specs = (P("filt", "case"), P("filt", "case"), P(None, "filt", None), P("filt"))
    return jax.shard_map(body, mesh=mesh, in_specs=in_specs, out_specs=out_specs, check_vma=False)
```

time: 133 us -> 103 us (0.77)
  Pallas kernels: 53.1 us -> 39.6 us
  starting transfers between devices: 33.7 us -> 25.7 us
  local copies, waits for them, and re-layouts: 18.5 us -> 11.5 us
  other arithmetic: 5.21 us -> 1.88 us
  waiting for transfers between devices: 20.2 us -> 22.5 us
    ppermute x8, waiting for transfers between devices: 1.03 us -> 8.56 us  [body(): onward = lambda v: lax.ppermute(v, 'filt', forwards)]
    pallas_call x3 -> x2, Pallas kernels: 12.7 us -> 6.38 us  [forward_call(): pl.pallas_call(functools.partial(forward_kernel, slots, carry is not None...]
    ppermute x10 -> x4, waiting for transfers between devices: 9.22 us -> 3.26 us  [body(): across = lambda v: lax.ppermute(v, 'case', [(0, 1), (1, 0)])]
    pallas_call x3, Pallas kernels: 13.1 us -> 7.69 us  [input_grad_call(): pl.pallas_call(functools.partial(input_grad_kernel, slots, pieces), out_s...]
    unnamed x47 -> x23, local copies, waits for them, and re-layouts: 13.7 us -> 8.34 us
    ppermute x10 -> x4, starting transfers between devices: 9.58 us -> 5.24 us  [body(): across = lambda v: lax.ppermute(v, 'case', [(0, 1), (1, 0)])]
    ppermute x8, starting transfers between devices: 10.8 us -> 6.88 us  [body(): back = lambda v: lax.ppermute(v, 'filt', backwards)]
    ppermute x23 -> x13, waiting for transfers between devices: 2.35 us -> 4.97 us  [body(): sibling = lambda v: lax.ppermute(v, 'filt', swap)]
  transfers between devices with their start and end apart: 49 -> 33, of which waited for: 12 -> 14; matrix products, arithmetic and copies ran while one was open for 8% -> 5% of each run, Pallas kernels for 40% -> 32%
where the time goes in v1:
time: 103 us; the launch traced here: 102 us
  Pallas kernels  39.6 us (38%)
  starting transfers between devices  25.7 us (25%)
  waiting for transfers between devices  22.5 us (22%)
  local copies, waits for them, and re-layouts  11.5 us (11%)
  other arithmetic  1.88 us (2%)
    pallas_call x3, Pallas kernels, weight_grad_call(): pl.pallas_call(functools.partial(weight_grad_kernel, len(xs), scale), out...  18.4 us
    ppermute x8, starting transfers between devices, body(): onward = lambda v: lax.ppermute(v, 'filt', forwards)  10.4 us
    ppermute x8, waiting for transfers between devices, body(): onward = lambda v: lax.ppermute(v, 'filt', forwards)  8.56 us
    unnamed x23, local copies, waits for them, and re-layouts  8.34 us
    pallas_call x3, Pallas kernels, input_grad_call(): pl.pallas_call(functools.partial(input_grad_kernel, slots, pieces), out_s...  7.69 us
    ppermute x8, starting transfers between devices, body(): back = lambda v: lax.ppermute(v, 'filt', backwards)  6.88 us
    pallas_call x2, Pallas kernels, forward_call(): pl.pallas_call(functools.partial(forward_kernel, slots, carry is not None...  6.38 us
    ppermute x8, waiting for transfers between devices, body(): back = lambda v: lax.ppermute(v, 'filt', backwards)  5.7 us
  transfers between devices with their start and end apart: 33, of which 14 were waited for; matrix products, arithmetic and copies ran while one was open for 5% of the time, Pallas kernels for 32%

profile of v1, /device:TPU:0, one launch (start us, length us, event | category | flops | bytes accessed | tf_op | source)
XLA Modules:
  0.0 102.2 jit_solution(2473137808121699758)
XLA Ops:
  0.7 1.2 %constant_dynamic-slice_fusion.3 = (bf16[128,576]{1,0:T(8,128)(2,1)S(1)}, bf16[128,576]{1,0:T(8,128)(2,1)S(1)}) fusion(bf16[128,1152]{1,0:T(8,128)(2,1)} %param.5, s32[]{:T(128)S(6)} %select_n.49, s32[]{:T(128)S(6)} %select_n.50), kind=kLoop, calls=%fused_computation.27 | loop fusion | bytes 589832 | tf_op jit(solution)/shard_map/dynamic-slice
  1.9 0.1 copy.17
  2.0 0.5 collective-permute-start
  2.5 1.0 collective-permute-done
  3.5 0.4 collective-permute-start.7
  3.9 0.1 copy.16
  4.0 0.1 maximum_select_fusion.refs_0_
  4.1 2.8 %collective-permute-start.1 = (bf16[576,256]{1,0:T(8,128)(2,1)S(1)}, bf16[576,256]{1,0:T(8,128)(2,1)S(1)}, u32[]{:S(2)}, u32[]{:S(2)}) collective-permute-start(bf16[576,256]{1,0:T(8,128)(2,1)S(1)} %maximum_select_fusion.refs_0_), channel_id=1, source_target_pairs={{0,4},{1,5},{4,8},{5,9},{8,12},{9,13},{12,14},{13,15},{14,10},{15,... | collective-permute-start | bytes 884744 | tf_op jit(solution)/shard_map/ppermute | solution.py:316
  6.9 1.2 %copy.13 = bf16[128,1152]{0,1:T(8,128)(2,1)S(1)} copy(bf16[128,1152]{1,0:T(8,128)(2,1)} %param.8) | data formatting | bytes 589824 | tf_op jit(solution)/shard_map/optimization_barrier | solution.py:321
  8.1 0.1 collective-permute-start.3
  8.3 0.4 collective-permute-start.4
  8.7 2.9 %collective-permute-done.4 = f32[1,128]{1,0:T(1,128)S(1)} collective-permute-done((f32[1,128]{1,0:T(1,128)S(1)}, f32[1,128]{1,0:T(1,128)S(1)}, u32[]{:S(2)}, u32[]{:S(2)}) %collective-permute-start.4) | collective-permute-done | bytes 544 | tf_op jit(solution)/shard_map/ppermute | solution.py:318
  11.6 2.7 %collective-permute-done.1.refs_1_ = bf16[576,256]{1,0:T(8,128)(2,1)S(1)} collective-permute-done((bf16[576,256]{1,0:T(8,128)(2,1)S(1)}, bf16[576,256]{1,0:T(8,128)(2,1)S(1)}, u32[]{:S(2)}, u32[]{:S(2)}) %collective-permute-start.1) | collective-permute-done | bytes 294944 | tf_op jit(solution)/shard_map/ppermute | solution.py:316
  14.4 1.5 %collective-permute-done.2.refs_2_ = bf16[576,256]{1,0:T(8,128)(2,1)S(1)} collective-permute-done((bf16[576,256]{1,0:T(8,128)(2,1)S(1)}, bf16[576,256]{1,0:T(8,128)(2,1)S(1)}, u32[]{:S(2)}, u32[]{:S(2)}) %collective-permute-start.2) | collective-permute-done | bytes 294944 | tf_op jit(solution)/shard_map/ppermute | solution.py:317
  16.0 1.6 %collective-permute-start.12 = (bf16[1728,256]{1,0:T(8,128)(2,1)S(1)}, bf16[1728,256]{1,0:T(8,128)(2,1)S(1)}, u32[]{:S(2)}, u32[]{:S(2)}) collective-permute-start(bf16[1728,256]{1,0:T(8,128)(2,1)S(1)} %pad_maximum_fusion.refs_0_), channel_id=1, source_target_pairs={{0,16},{16,0},{1,17},{17,1},{2,18},{18,2},{3,19},{19,3},{4,20},{20... | collective-permute-start | bytes 2654216 | tf_op jit(solution)/shard_map/ppermute | solution.py:320
  17.6 1.6 %collective-permute-start.5 = (bf16[576,256]{1,0:T(8,128)(2,1)S(1)}, bf16[576,256]{1,0:T(8,128)(2,1)S(1)}, u32[]{:S(2)}, u32[]{:S(2)}) collective-permute-start(bf16[576,256]{1,0:T(8,128)(2,1)S(1)} %collective-permute-done.1.refs_1_), channel_id=1, source_target_pairs={{0,4},{1,5},{4,8},{5,9},{8,12},{9,13},{12,14},{13,15},{14,10},{15,... | collective-permute-start | bytes 884744 | tf_op jit(solution)/shard_map/ppermute | solution.py:316
  19.1 0.4 collective-permute-start.6
  19.6 2.3 %copy-done.2 = bf16[9,128,2048]{2,1,0:T(8,128)(2,1)S(1)} copy-done((bf16[9,128,2048]{2,1,0:T(8,128)(2,1)S(1)}, bf16[9,128,2048]{2,1,0:T(8,128)(2,1)}, u32[]{:S(2)}) %copy-start.2) | copy-done | bytes 4718616
  21.9 2.7 %hold.1 = (bf16[9,256,2048]{2,1,0:T(8,128)(2,1)S(1)}, f32[8,128]{1,0:T(8,128)S(1)}) custom-call(bf16[9,128,2048]{2,1,0:T(8,128)(2,1)S(1)} %copy-done.2, bf16[9,128,2048]{2,1,0:T(8,128)(2,1)} %collective-permute-done.7.w_sib), custom_call_target="tpu_custom_call" | custom-call | flops 1000 | bytes 1000 | tf_op jit(solution)/shard_map/hold/pallas_call | solution.py:81
  24.6 0.8 collective-permute-done.5.refs_3_
  25.4 1.3 %collective-permute-done.6.refs_4_ = bf16[576,256]{1,0:T(8,128)(2,1)S(1)} collective-permute-done((bf16[576,256]{1,0:T(8,128)(2,1)S(1)}, bf16[576,256]{1,0:T(8,128)(2,1)S(1)}, u32[]{:S(2)}, u32[]{:S(2)}) %collective-permute-start.6) | collective-permute-done | bytes 294944 | tf_op jit(solution)/shard_map/ppermute | solution.py:317
  26.7 1.6 %collective-permute-start.8 = (bf16[576,256]{1,0:T(8,128)(2,1)S(1)}, bf16[576,256]{1,0:T(8,128)(2,1)S(1)}, u32[]{:S(2)}, u32[]{:S(2)}) collective-permute-start(bf16[576,256]{1,0:T(8,128)(2,1)S(1)} %collective-permute-done.5.refs_3_), channel_id=1, source_target_pairs={{0,4},{1,5},{4,8},{5,9},{8,12},{9,13},{12,14},{13,15},{14,10},{15,... | collective-permute-start | bytes 884744 | tf_op jit(solution)/shard_map/ppermute | solution.py:316
  28.3 0.4 collective-permute-start.9
  28.8 0.6 collective-permute-start.17
  29.4 0.7 fusion.1.q_ref
  30.1 4.2 %forward.2 = (f32[3,576,256]{2,1,0:T(8,128)S(1)}, f32[8,128]{1,0:T(8,128)S(1)}) custom-call(s32[8]{0:T(128)S(1)} %fusion.1.q_ref, f32[8,128]{1,0:T(8,128)S(1)} %get-tuple-element.84.after, bf16[9,256,2048]{2,1,0:T(8,128)(2,1)S(1)} %get-tuple-element.85.w_all, bf16[576,256]{1,0:T(8,128)(2,1)S(1)} %maximum_select_fusion.refs_0_, ...), custom_call_target="tpu_custom_call" | custom-call | flops 1000 | bytes 1000 | tf_op jit(solution)/shard_map/forward/pallas_call | solution.py:124
  34.3 0.7 collective-permute-done.9.refs_2_
  35.0 1.5 %collective-permute-start.10 = (bf16[288,256]{1,0:T(8,128)(2,1)S(1)}, bf16[288,256]{1,0:T(8,128)(2,1)S(1)}, u32[]{:S(2)}, u32[]{:S(2)}) collective-permute-start(bf16[288,256]{1,0:T(8,128)(2,1)S(1)} %slice.20), channel_id=1, source_target_pairs={{0,4},{1,5},{4,8},{5,9},{8,12},{9,13},{12,14},{13,15},{14,10},{15,... | collective-permute-start | bytes 442376 | tf_op jit(solution)/shard_map/ppermute | solution.py:316
  36.6 0.6 collective-permute-start.11
  37.2 2.2 %forward.3 = (f32[3,576,256]{2,1,0:T(8,128)S(1)}, f32[8,128]{1,0:T(8,128)S(1)}) custom-call(s32[8]{0:T(128)S(1)} %fusion.1.q_ref, f32[8,128]{1,0:T(8,128)S(1)} %get-tuple-element.89.after, bf16[9,256,2048]{2,1,0:T(8,128)(2,1)S(1)} %get-tuple-element.85.w_all, f32[3,576,256]{2,1,0:T(8,128)S(1)} %get-tuple-element.90.refs_0_, ...), custom_call_target="tpu_custom_call" | custom-call | flops 1000 | bytes 1000 | tf_op jit(solution)/shard_map/forward/pallas_call | solution.py:124
  39.4 0.9 collective-permute-done.10.refs_0_
  40.2 1.6 %collective-permute-done.11.refs_1_ = bf16[288,256]{1,0:T(8,128)(2,1)S(1)} collective-permute-done((bf16[288,256]{1,0:T(8,128)(2,1)S(1)}, bf16[288,256]{1,0:T(8,128)(2,1)S(1)}, u32[]{:S(2)}, u32[]{:S(2)}) %collective-permute-start.11) | collective-permute-done | bytes 147488 | tf_op jit(solution)/shard_map/ppermute | solution.py:317
  41.8 2.1 %gate.1 = (bf16[576,128]{1,0:T(8,128)(2,1)S(1)}, bf16[576,128]{1,0:T(8,128)(2,1)S(1)}, bf16[576,128]{1,0:T(8,128)(2,1)S(1)}, bf16[576,128]{1,0:T(8,128)(2,1)S(1)}, bf16[576,2304]{1,0:T(8,128)(2,1)S(1)}) custom-call(s32[8]{0:T(128)S(1)} %fusion.1.q_ref, f32[8,128]{1,0:T(8,128)S(1)} %get-tuple-element.92.after, ...), custom_call_target="tpu_custom_call" | custom-call | flops 1000 | bytes 1000 | tf_op jit(solution)/shard_map/gate/pallas_call | solution.py:169
  43.9 1.4 %input_grad.3 = (bf16[288,256]{1,0:T(8,128)(2,1)S(1)}, bf16[288,256]{1,0:T(8,128)(2,1)S(1)}, f32[8,128]{1,0:T(8,128)S(1)}) custom-call(s32[8]{0:T(128)S(1)} %fusion.1.q_ref, f32[8,128]{1,0:T(8,128)S(1)} %get-tuple-element.92.after, bf16[9,256,2048]{2,1,0:T(8,128)(2,1)S(1)} %get-tuple-element.85.w_all, bf16[576,2304]{1,0:T(8,128)(2,1)S(1)} %get-tuple-element.98.g9), custom_call_target="tpu_custom_call" | custom-call | flops 1000 | bytes 1000 | tf_op jit(solution)/shard_map/input_grad/pallas_call | solution.py:199
  45.3 2.1 %input_grad.4 = (f32[576,256]{1,0:T(8,128)S(1)}, f32[576,256]{1,0:T(8,128)S(1)}, f32[8,128]{1,0:T(8,128)S(1)}) custom-call(s32[8]{0:T(128)S(1)} %fusion.1.q_ref, f32[8,128]{1,0:T(8,128)S(1)} %get-tuple-element.99.after, bf16[9,256,2048]{2,1,0:T(8,128)(2,1)S(1)} %get-tuple-element.85.w_all, bf16[576,2304]{1,0:T(8,128)(2,1)S(1)} %get-tuple-element.98.g9), custom_call_target="tpu_custom_call" | custom-call | flops 1000 | bytes 1000 | tf_op jit(solution)/shard_map/input_grad/pallas_call | solution.py:199
  47.5 0.9 collective-permute-start.13
  48.4 1.2 %collective-permute-start.14 = (bf16[288,256]{1,0:T(8,128)(2,1)S(1)}, bf16[288,256]{1,0:T(8,128)(2,1)S(1)}, u32[]{:S(2)}, u32[]{:S(2)}) collective-permute-start(bf16[288,256]{1,0:T(8,128)(2,1)S(1)} %get-tuple-element.102), channel_id=1, source_target_pairs={{0,2},{1,3},{4,0},{5,1},{8,4},{9,5},{12,8},{13,9},{14,12},{15,13},... | collective-permute-start | bytes 442376 | tf_op jit(solution)/shard_map/ppermute | solution.py:317
  49.6 4.2 %collective-permute-done.13 = bf16[288,256]{1,0:T(8,128)(2,1)S(1)} collective-permute-done((bf16[288,256]{1,0:T(8,128)(2,1)S(1)}, bf16[288,256]{1,0:T(8,128)(2,1)S(1)}, u32[]{:S(2)}, u32[]{:S(2)}) %collective-permute-start.13) | collective-permute-done | bytes 147488 | tf_op jit(solution)/shard_map/ppermute | solution.py:316
  53.8 0.6 collective-permute-done.14
  54.5 0.7 collective-permute-start.18
  55.2 1.4 %collective-permute-start.19 = (bf16[576,256]{1,0:T(8,128)(2,1)S(1)}, bf16[576,256]{1,0:T(8,128)(2,1)S(1)}, u32[]{:S(2)}, u32[]{:S(2)}) collective-permute-start(bf16[576,256]{1,0:T(8,128)(2,1)S(1)} %pad_maximum_fusion.3), channel_id=1, source_target_pairs={{0,2},{1,3},{4,0},{5,1},{8,4},{9,5},{12,8},{13,9},{14,12},{15,13},... | collective-permute-start | bytes 884744 | tf_op jit(solution)/shard_map/ppermute | solution.py:317
  56.6 1.5 %collective-permute-start.20 = (bf16[1152,128]{1,0:T(8,128)(2,1)S(1)}, bf16[1152,128]{1,0:T(8,128)(2,1)S(1)}, u32[]{:S(2)}, u32[]{:S(2)}) collective-permute-start(bf16[1152,128]{1,0:T(8,128)(2,1)S(1)} %pad_maximum_fusion.1.refs_0_), channel_id=1, source_target_pairs={{0,16},{16,0},{1,17},{17,1},{2,18},{18,2},{3,19},{19,3},{4,20},{20... | collective-permute-start | bytes 884744 | tf_op jit(solution)/shard_map/ppermute | solution.py:320
  58.1 0.6 collective-permute-start.24
  58.7 4.2 %input_grad.5 = (f32[576,256]{1,0:T(8,128)S(1)}, f32[576,256]{1,0:T(8,128)S(1)}, f32[576,256]{1,0:T(8,128)S(1)}, f32[576,256]{1,0:T(8,128)S(1)}, f32[576,256]{1,0:T(8,128)S(1)}, /*index=5*/f32[8,128]{1,0:T(8,128)S(1)}) custom-call(s32[8]{0:T(128)S(1)} %fusion.1.q_ref, f32[8,128]{1,0:T(8,128)S(1)} %get-tuple-element.112.after, ...), custom_call_target="tpu_custom_call" | custom-call | flops 1000 | bytes 1000 | tf_op jit(solution)/shard_map/input_grad/pallas_call | solution.py:199
  62.9 0.8 copy-done.3
  63.7 0.6 collective-permute-done.20.refs_1_
  64.4 0.7 collective-permute-start.21
  65.1 1.4 %collective-permute-start.22 = (bf16[576,256]{1,0:T(8,128)(2,1)S(1)}, bf16[576,256]{1,0:T(8,128)(2,1)S(1)}, u32[]{:S(2)}, u32[]{:S(2)}) collective-permute-start(bf16[576,256]{1,0:T(8,128)(2,1)S(1)} %add_convert_fusion.3), channel_id=1, source_target_pairs={{0,2},{1,3},{4,0},{5,1},{8,4},{9,5},{12,8},{13,9},{14,12},{15,13},... | collective-permute-start | bytes 884744 | tf_op jit(solution)/shard_map/ppermute | solution.py:317
  66.6 1.6 %collective-permute-start.29 = (bf16[1728,256]{1,0:T(8,128)(2,1)S(1)}, bf16[1728,256]{1,0:T(8,128)(2,1)}, u32[]{:S(2)}, u32[]{:S(2)}) collective-permute-start(bf16[1728,256]{1,0:T(8,128)(2,1)S(1)} %constant_dynamic-update-slice_fusion.2.refs_0_), channel_id=1, source_target_pairs={{0,16},{16,0},{1,17},{17,1},{2,18},{18,2},{3,19},{19,3},{4,20},{20... | collective-permute-start | bytes 2654216 | tf_op jit(solution)/shard_map/ppermute | solution.py:320
  68.1 2.4 %displaced.1 = (bf16[1152,2304]{1,0:T(8,128)(2,1)S(1)}, f32[1,128]{1,0:T(1,128)}, bf16[128,1152]{1,0:T(8,128)(2,1)}) custom-call(s32[1]{0:T(128)} %bitcast.core, f32[8,128]{1,0:T(8,128)S(1)} %get-tuple-element.115.after, bf16[576,128]{1,0:T(8,128)(2,1)S(1)} %get-tuple-element.116.act_own, bf16[576,128]{1,0:T(8,128)(2,1)S(1)} %collective-permute-done.15.act_sib, ...), custom_call_target="tpu_custom_call" | custom-call | flops 1000 | bytes 1000 | tf_op jit(solution)/shard_map/displaced/pallas_call | solution.py:236
  70.6 0.5 collective-permute-start.28
  71.1 6.4 %weight_grad.3 = (f32[1152,2048]{1,0:T(8,128)}, f32[8,128]{1,0:T(8,128)S(1)}) custom-call(s32[8]{0:T(128)S(1)} %fusion.1.q_ref, f32[8,128]{1,0:T(8,128)S(1)} %get-tuple-element.115.after, bf16[1152,2304]{1,0:T(8,128)(2,1)S(1)} %get-tuple-element.129.g9t, bf16[1728,256]{1,0:T(8,128)(2,1)S(1)} %pad_maximum_fusion.refs_0_, ...), custom_call_target="tpu_custom_call" | custom-call | flops 1000 | bytes 1000 | tf_op jit(solution)/shard_map/weight_grad/pallas_call | solution.py:265
  77.6 0.7 collective-permute-start.25
  78.3 1.4 %collective-permute-start.26 = (bf16[576,256]{1,0:T(8,128)(2,1)S(1)}, bf16[576,256]{1,0:T(8,128)(2,1)S(1)}, u32[]{:S(2)}, u32[]{:S(2)}) collective-permute-start(bf16[576,256]{1,0:T(8,128)(2,1)S(1)} %add_convert_fusion.1), channel_id=1, source_target_pairs={{0,2},{1,3},{4,0},{5,1},{8,4},{9,5},{12,8},{13,9},{14,12},{15,13},... | collective-permute-start | bytes 884744 | tf_op jit(solution)/shard_map/ppermute | solution.py:317
  79.7 4.8 %weight_grad.4 = (f32[1152,2048]{1,0:T(8,128)}, f32[8,128]{1,0:T(8,128)S(1)}) custom-call(s32[8]{0:T(128)S(1)} %fusion.1.q_ref, f32[8,128]{1,0:T(8,128)S(1)} %get-tuple-element.137.after, bf16[1152,2304]{1,0:T(8,128)(2,1)S(1)} %get-tuple-element.129.g9t, ...), custom_call_target="tpu_custom_call", output_to_operand_aliasing={{0}: (7, {})} | custom-call | flops 1000 | bytes 1000 | tf_op jit(solution)/shard_map/weight_grad/pallas_call | solution.py:265
  84.5 2.6 %collective-permute-done.29.refs_2_ = bf16[1728,256]{1,0:T(8,128)(2,1)} collective-permute-done((bf16[1728,256]{1,0:T(8,128)(2,1)S(1)}, bf16[1728,256]{1,0:T(8,128)(2,1)}, u32[]{:S(2)}, u32[]{:S(2)}) %collective-permute-start.29) | collective-permute-done | bytes 884768 | tf_op jit(solution)/shard_map/ppermute | solution.py:320
  87.1 0.7 copy-done.5
  87.8 0.7 copy-done.6
  88.6 1.2 %add_convert_fusion = bf16[576,256]{1,0:T(8,128)(2,1)S(1)} fusion(bf16[576,256]{1,0:T(8,128)(2,1)} %copy-done.6, f32[576,256]{1,0:T(8,128)S(1)} %copy-done.4, bf16[576,256]{1,0:T(8,128)(2,1)} %copy-done.5), kind=kLoop, calls=%fused_computation.1 | loop fusion | flops 737280 | bytes 1474560 | tf_op jit(solution)/shard_map/convert_element_type | solution.py:426
  89.8 0.6 collective-permute-start.30
  90.4 1.0 collective-permute-done.30
  91.5 0.9 copy.15
  92.4 2.5 %copy-done.1 = bf16[1152,2304]{1,0:T(8,128)(2,1)S(1)} copy-done((bf16[1152,2304]{1,0:T(8,128)(2,1)S(1)}, bf16[1152,2304]{1,0:T(8,128)(2,1)}, u32[]{:S(2)}) %copy-start.1) | copy-done | bytes 5308440
  94.9 7.3 %weight_grad.5 = (f32[1152,2048]{1,0:T(8,128)}, f32[8,128]{1,0:T(8,128)}) custom-call(s32[8]{0:T(128)S(1)} %fusion.1.q_ref, f32[8,128]{1,0:T(8,128)S(1)} %get-tuple-element.143.after, bf16[1152,2304]{1,0:T(8,128)(2,1)S(1)} %copy-done.1, bf16[1728,256]{1,0:T(8,128)(2,1)S(1)} %constant_dynamic-update-slice_fusion.2.refs_0_, ...), custom_call_target="tpu_custom_call", output_to_operand_aliasing={{0}: (7, {})} | custom-call | flops 1000 | bytes 1000 | tf_op jit(solution)/shard_map/weight_grad/pallas_call | solution.py:265
  (60 shorter events, 1.0 us)
Async XLA Ops:
  0.6 7.6 %copy-start.7 = (f32[128]{0:T(128)S(1)}, f32[128]{0:T(128)}, u32[]{:S(2)}) copy-start(f32[128]{0:T(128)} %param.7) | copy-start | bytes 1540
  2.0 1.5 %collective-permute-start = (bf16[576,128]{1,0:T(8,128)(2,1)S(1)}, bf16[576,128]{1,0:T(8,128)(2,1)S(1)}, u32[]{:S(2)}, u32[]{:S(2)}) collective-permute-start(bf16[576,128]{1,0:T(8,128)(2,1)S(1)} %bitcast.16), channel_id=1, source_target_pairs={{0,1},{1,0},{2,3},{3,2},{4,5},{5,4},{6,7},{7,6},{8,9},{9,8},{10,11... | collective-permute-start | bytes 442376 | tf_op jit(solution)/shard_map/ppermute | solution.py:318
  3.5 16.1 %collective-permute-start.7 = (bf16[9,128,2048]{2,1,0:T(8,128)(2,1)}, bf16[9,128,2048]{2,1,0:T(8,128)(2,1)}, u32[]{:S(2)}, u32[]{:S(2)}) collective-permute-start(bf16[9,128,2048]{2,1,0:T(8,128)(2,1)} %w_own), channel_id=1, source_target_pairs={{0,1},{1,0},{2,3},{3,2},{4,5},{5,4},{6,7},{7,6},{8,9},{9,8},{10,11... | collective-permute-start | bytes 14155784 | tf_op jit(solution)/shard_map/ppermute | solution.py:318
  4.1 10.2 %collective-permute-start.1 = (bf16[576,256]{1,0:T(8,128)(2,1)S(1)}, bf16[576,256]{1,0:T(8,128)(2,1)S(1)}, u32[]{:S(2)}, u32[]{:S(2)}) collective-permute-start(bf16[576,256]{1,0:T(8,128)(2,1)S(1)} %maximum_select_fusion.refs_0_), channel_id=1, source_target_pairs={{0,4},{1,5},{4,8},{5,9},{8,12},{9,13},{12,14},{13,15},{14,10},{15,... | collective-permute-start | bytes 884744 | tf_op jit(solution)/shard_map/ppermute | solution.py:316
  6.9 9.0 %collective-permute-start.2 = (bf16[576,256]{1,0:T(8,128)(2,1)S(1)}, bf16[576,256]{1,0:T(8,128)(2,1)S(1)}, u32[]{:S(2)}, u32[]{:S(2)}) collective-permute-start(bf16[576,256]{1,0:T(8,128)(2,1)S(1)} %maximum_select_fusion.refs_0_), channel_id=1, source_target_pairs={{0,2},{1,3},{4,0},{5,1},{8,4},{9,5},{12,8},{13,9},{14,12},{15,13},... | collective-permute-start | bytes 884744 | tf_op jit(solution)/shard_map/ppermute | solution.py:317
  8.1 3.5 %collective-permute-start.3 = (bf16[576,128]{1,0:T(8,128)(2,1)S(1)}, bf16[576,128]{1,0:T(8,128)(2,1)S(1)}, u32[]{:S(2)}, u32[]{:S(2)}) collective-permute-start(bf16[576,128]{1,0:T(8,128)(2,1)S(1)} %get-tuple-element.155), channel_id=1, source_target_pairs={{0,1},{1,0},{2,3},{3,2},{4,5},{5,4},{6,7},{7,6},{8,9},{9,8},{10,11... | collective-permute-start | bytes 442376 | tf_op jit(solution)/shard_map/ppermute | solution.py:318
  8.3 3.4 %collective-permute-start.4 = (f32[1,128]{1,0:T(1,128)S(1)}, f32[1,128]{1,0:T(1,128)S(1)}, u32[]{:S(2)}, u32[]{:S(2)}) collective-permute-start(f32[1,128]{1,0:T(1,128)S(1)} %bitcast.17), channel_id=1, source_target_pairs={{0,1},{1,0},{2,3},{3,2},{4,5},{5,4},{6,7},{7,6},{8,9},{9,8},{10,11... | collective-permute-start | bytes 1544 | tf_op jit(solution)/shard_map/ppermute | solution.py:318
  16.0 23.4 %collective-permute-start.12 = (bf16[1728,256]{1,0:T(8,128)(2,1)S(1)}, bf16[1728,256]{1,0:T(8,128)(2,1)S(1)}, u32[]{:S(2)}, u32[]{:S(2)}) collective-permute-start(bf16[1728,256]{1,0:T(8,128)(2,1)S(1)} %pad_maximum_fusion.refs_0_), channel_id=1, source_target_pairs={{0,16},{16,0},{1,17},{17,1},{2,18},{18,2},{3,19},{19,3},{4,20},{20... | collective-permute-start | bytes 2654216 | tf_op jit(solution)/shard_map/ppermute | solution.py:320
  17.6 7.9 %collective-permute-start.5 = (bf16[576,256]{1,0:T(8,128)(2,1)S(1)}, bf16[576,256]{1,0:T(8,128)(2,1)S(1)}, u32[]{:S(2)}, u32[]{:S(2)}) collective-permute-start(bf16[576,256]{1,0:T(8,128)(2,1)S(1)} %collective-permute-done.1.refs_1_), channel_id=1, source_target_pairs={{0,4},{1,5},{4,8},{5,9},{8,12},{9,13},{12,14},{13,15},{14,10},{15,... | collective-permute-start | bytes 884744 | tf_op jit(solution)/shard_map/ppermute | solution.py:316
  19.1 7.6 %collective-permute-start.6 = (bf16[576,256]{1,0:T(8,128)(2,1)S(1)}, bf16[576,256]{1,0:T(8,128)(2,1)S(1)}, u32[]{:S(2)}, u32[]{:S(2)}) collective-permute-start(bf16[576,256]{1,0:T(8,128)(2,1)S(1)} %collective-permute-done.2.refs_2_), channel_id=1, source_target_pairs={{0,2},{1,3},{4,0},{5,1},{8,4},{9,5},{12,8},{13,9},{14,12},{15,13},... | collective-permute-start | bytes 884744 | tf_op jit(solution)/shard_map/ppermute | solution.py:317
  19.6 2.3 %copy-start.2 = (bf16[9,128,2048]{2,1,0:T(8,128)(2,1)S(1)}, bf16[9,128,2048]{2,1,0:T(8,128)(2,1)}, u32[]{:S(2)}) copy-start(bf16[9,128,2048]{2,1,0:T(8,128)(2,1)} %w_own) | copy-start | bytes 14155780
  26.7 7.6 %collective-permute-start.8 = (bf16[576,256]{1,0:T(8,128)(2,1)S(1)}, bf16[576,256]{1,0:T(8,128)(2,1)S(1)}, u32[]{:S(2)}, u32[]{:S(2)}) collective-permute-start(bf16[576,256]{1,0:T(8,128)(2,1)S(1)} %collective-permute-done.5.refs_3_), channel_id=1, source_target_pairs={{0,4},{1,5},{4,8},{5,9},{8,12},{9,13},{12,14},{13,15},{14,10},{15,... | collective-permute-start | bytes 884744 | tf_op jit(solution)/shard_map/ppermute | solution.py:316
  28.3 6.7 %collective-permute-start.9 = (bf16[576,256]{1,0:T(8,128)(2,1)S(1)}, bf16[576,256]{1,0:T(8,128)(2,1)S(1)}, u32[]{:S(2)}, u32[]{:S(2)}) collective-permute-start(bf16[576,256]{1,0:T(8,128)(2,1)S(1)} %collective-permute-done.6.refs_4_), channel_id=1, source_target_pairs={{0,2},{1,3},{4,0},{5,1},{8,4},{9,5},{12,8},{13,9},{14,12},{15,13},... | collective-permute-start | bytes 884744 | tf_op jit(solution)/shard_map/ppermute | solution.py:317
  28.8 25.6 %collective-permute-start.17 = (bf16[1152,256]{1,0:T(8,128)(2,1)S(1)}, bf16[1152,256]{1,0:T(8,128)(2,1)S(1)}, u32[]{:S(2)}, u32[]{:S(2)}) collective-permute-start(bf16[1152,256]{1,0:T(8,128)(2,1)S(1)} %constant_dynamic-update-slice_fusion.refs_0_), channel_id=1, source_target_pairs={{0,16},{16,0},{1,17},{17,1},{2,18},{18,2},{3,19},{19,3},{4,20},{20... | collective-permute-start | bytes 1769480 | tf_op jit(solution)/shard_map/ppermute | solution.py:320
  35.0 5.2 %collective-permute-start.10 = (bf16[288,256]{1,0:T(8,128)(2,1)S(1)}, bf16[288,256]{1,0:T(8,128)(2,1)S(1)}, u32[]{:S(2)}, u32[]{:S(2)}) collective-permute-start(bf16[288,256]{1,0:T(8,128)(2,1)S(1)} %slice.20), channel_id=1, source_target_pairs={{0,4},{1,5},{4,8},{5,9},{8,12},{9,13},{12,14},{13,15},{14,10},{15,... | collective-permute-start | bytes 442376 | tf_op jit(solution)/shard_map/ppermute | solution.py:316
  36.6 5.2 %collective-permute-start.11 = (bf16[288,256]{1,0:T(8,128)(2,1)S(1)}, bf16[288,256]{1,0:T(8,128)(2,1)S(1)}, u32[]{:S(2)}, u32[]{:S(2)}) collective-permute-start(bf16[288,256]{1,0:T(8,128)(2,1)S(1)} %slice.21), channel_id=1, source_target_pairs={{0,2},{1,3},{4,0},{5,1},{8,4},{9,5},{12,8},{13,9},{14,12},{15,13},... | collective-permute-start | bytes 442376 | tf_op jit(solution)/shard_map/ppermute | solution.py:317
  43.8 5.7 %collective-permute-start.16 = (bf16[576,128]{1,0:T(8,128)(2,1)S(1)}, bf16[576,128]{1,0:T(8,128)(2,1)S(1)}, u32[]{:S(2)}, u32[]{:S(2)}) collective-permute-start(bf16[576,128]{1,0:T(8,128)(2,1)S(1)} %get-tuple-element.106), channel_id=1, source_target_pairs={{0,1},{1,0},{2,3},{3,2},{4,5},{5,4},{6,7},{7,6},{8,9},{9,8},{10,11... | collective-permute-start | bytes 442376 | tf_op jit(solution)/shard_map/ppermute | solution.py:318
  47.5 6.3 %collective-permute-start.13 = (bf16[288,256]{1,0:T(8,128)(2,1)S(1)}, bf16[288,256]{1,0:T(8,128)(2,1)S(1)}, u32[]{:S(2)}, u32[]{:S(2)}) collective-permute-start(bf16[288,256]{1,0:T(8,128)(2,1)S(1)} %get-tuple-element.101), channel_id=1, source_target_pairs={{0,4},{1,5},{4,8},{5,9},{8,12},{9,13},{12,14},{13,15},{14,10},{15,... | collective-permute-start | bytes 442376 | tf_op jit(solution)/shard_map/ppermute | solution.py:316
  48.4 6.0 %collective-permute-start.14 = (bf16[288,256]{1,0:T(8,128)(2,1)S(1)}, bf16[288,256]{1,0:T(8,128)(2,1)S(1)}, u32[]{:S(2)}, u32[]{:S(2)}) collective-permute-start(bf16[288,256]{1,0:T(8,128)(2,1)S(1)} %get-tuple-element.102), channel_id=1, source_target_pairs={{0,2},{1,3},{4,0},{5,1},{8,4},{9,5},{12,8},{13,9},{14,12},{15,13},... | collective-permute-start | bytes 442376 | tf_op jit(solution)/shard_map/ppermute | solution.py:317
  49.6 4.8 %collective-permute-start.15 = (bf16[576,128]{1,0:T(8,128)(2,1)S(1)}, bf16[576,128]{1,0:T(8,128)(2,1)S(1)}, u32[]{:S(2)}, u32[]{:S(2)}) collective-permute-start(bf16[576,128]{1,0:T(8,128)(2,1)S(1)} %get-tuple-element.104), channel_id=1, source_target_pairs={{0,1},{1,0},{2,3},{3,2},{4,5},{5,4},{6,7},{7,6},{8,9},{9,8},{10,11... | collective-permute-start | bytes 442376 | tf_op jit(solution)/shard_map/ppermute | solution.py:318
  54.5 9.2 %collective-permute-start.18 = (bf16[576,256]{1,0:T(8,128)(2,1)S(1)}, bf16[576,256]{1,0:T(8,128)(2,1)S(1)}, u32[]{:S(2)}, u32[]{:S(2)}) collective-permute-start(bf16[576,256]{1,0:T(8,128)(2,1)S(1)} %pad_maximum_fusion.2), channel_id=1, source_target_pairs={{0,4},{1,5},{4,8},{5,9},{8,12},{9,13},{12,14},{13,15},{14,10},{15,... | collective-permute-start | bytes 884744 | tf_op jit(solution)/shard_map/ppermute | solution.py:316
  55.2 8.5 %collective-permute-start.19 = (bf16[576,256]{1,0:T(8,128)(2,1)S(1)}, bf16[576,256]{1,0:T(8,128)(2,1)S(1)}, u32[]{:S(2)}, u32[]{:S(2)}) collective-permute-start(bf16[576,256]{1,0:T(8,128)(2,1)S(1)} %pad_maximum_fusion.3), channel_id=1, source_target_pairs={{0,2},{1,3},{4,0},{5,1},{8,4},{9,5},{12,8},{13,9},{14,12},{15,13},... | collective-permute-start | bytes 884744 | tf_op jit(solution)/shard_map/ppermute | solution.py:317
  56.6 7.8 %collective-permute-start.20 = (bf16[1152,128]{1,0:T(8,128)(2,1)S(1)}, bf16[1152,128]{1,0:T(8,128)(2,1)S(1)}, u32[]{:S(2)}, u32[]{:S(2)}) collective-permute-start(bf16[1152,128]{1,0:T(8,128)(2,1)S(1)} %pad_maximum_fusion.1.refs_0_), channel_id=1, source_target_pairs={{0,16},{16,0},{1,17},{17,1},{2,18},{18,2},{3,19},{19,3},{4,20},{20... | collective-permute-start | bytes 884744 | tf_op jit(solution)/shard_map/ppermute | solution.py:320
  58.1 12.5 %collective-permute-start.23 = (bf16[1728,256]{1,0:T(8,128)(2,1)S(1)}, bf16[1728,256]{1,0:T(8,128)(2,1)S(1)}, u32[]{:S(2)}, u32[]{:S(2)}) collective-permute-start(bf16[1728,256]{1,0:T(8,128)(2,1)S(1)} %pad_maximum_fusion.refs_0_), channel_id=1, source_target_pairs={{0,1},{1,0},{2,3},{3,2},{4,5},{5,4},{6,7},{7,6},{8,9},{9,8},{10,11... | collective-permute-start | bytes 2654216 | tf_op jit(solution)/shard_map/ppermute | solution.py:318
  58.1 12.5 %collective-permute-start.24 = (bf16[1728,256]{1,0:T(8,128)(2,1)S(1)}, bf16[1728,256]{1,0:T(8,128)(2,1)S(1)}, u32[]{:S(2)}, u32[]{:S(2)}) collective-permute-start(bf16[1728,256]{1,0:T(8,128)(2,1)S(1)} %collective-permute-done.12.refs_2_), channel_id=1, source_target_pairs={{0,1},{1,0},{2,3},{3,2},{4,5},{5,4},{6,7},{7,6},{8,9},{9,8},{10,11... | collective-permute-start | bytes 2654216 | tf_op jit(solution)/shard_map/ppermute | solution.py:318
  62.9 0.8 copy-start.3
  64.4 13.0 %collective-permute-start.21 = (bf16[576,256]{1,0:T(8,128)(2,1)S(1)}, bf16[576,256]{1,0:T(8,128)(2,1)S(1)}, u32[]{:S(2)}, u32[]{:S(2)}) collective-permute-start(bf16[576,256]{1,0:T(8,128)(2,1)S(1)} %add_convert_fusion.4), channel_id=1, source_target_pairs={{0,4},{1,5},{4,8},{5,9},{8,12},{9,13},{12,14},{13,15},{14,10},{15,... | collective-permute-start | bytes 884744 | tf_op jit(solution)/shard_map/ppermute | solution.py:316
  65.1 12.3 %collective-permute-start.22 = (bf16[576,256]{1,0:T(8,128)(2,1)S(1)}, bf16[576,256]{1,0:T(8,128)(2,1)S(1)}, u32[]{:S(2)}, u32[]{:S(2)}) collective-permute-start(bf16[576,256]{1,0:T(8,128)(2,1)S(1)} %add_convert_fusion.3), channel_id=1, source_target_pairs={{0,2},{1,3},{4,0},{5,1},{8,4},{9,5},{12,8},{13,9},{14,12},{15,13},... | collective-permute-start | bytes 884744 | tf_op jit(solution)/shard_map/ppermute | solution.py:317
  66.6 20.6 %collective-permute-start.29 = (bf16[1728,256]{1,0:T(8,128)(2,1)S(1)}, bf16[1728,256]{1,0:T(8,128)(2,1)}, u32[]{:S(2)}, u32[]{:S(2)}) collective-permute-start(bf16[1728,256]{1,0:T(8,128)(2,1)S(1)} %constant_dynamic-update-slice_fusion.2.refs_0_), channel_id=1, source_target_pairs={{0,16},{16,0},{1,17},{17,1},{2,18},{18,2},{3,19},{19,3},{4,20},{20... | collective-permute-start | bytes 2654216 | tf_op jit(solution)/shard_map/ppermute | solution.py:320
  70.6 9.2 %copy-start = (bf16[1152,2304]{1,0:T(8,128)(2,1)}, bf16[1152,2304]{1,0:T(8,128)(2,1)S(1)}, u32[]{:S(2)}) copy-start(bf16[1152,2304]{1,0:T(8,128)(2,1)S(1)} %get-tuple-element.129.g9t) | copy-start | bytes 15925252
  70.6 9.1 %collective-permute-start.27 = (bf16[1152,256]{1,0:T(8,128)(2,1)S(1)}, bf16[1152,256]{1,0:T(8,128)(2,1)S(1)}, u32[]{:S(2)}, u32[]{:S(2)}) collective-permute-start(bf16[1152,256]{1,0:T(8,128)(2,1)S(1)} %constant_dynamic-update-slice_fusion.refs_0_), channel_id=1, source_target_pairs={{0,1},{1,0},{2,3},{3,2},{4,5},{5,4},{6,7},{7,6},{8,9},{9,8},{10,11... | collective-permute-start | bytes 1769480 | tf_op jit(solution)/shard_map/ppermute | solution.py:318
  70.6 9.1 %collective-permute-start.28 = (bf16[1152,256]{1,0:T(8,128)(2,1)S(1)}, bf16[1152,256]{1,0:T(8,128)(2,1)S(1)}, u32[]{:S(2)}, u32[]{:S(2)}) collective-permute-start(bf16[1152,256]{1,0:T(8,128)(2,1)S(1)} %collective-permute-done.17.refs_2_), channel_id=1, source_target_pairs={{0,1},{1,0},{2,3},{3,2},{4,5},{5,4},{6,7},{7,6},{8,9},{9,8},{10,11... | collective-permute-start | bytes 1769480 | tf_op jit(solution)/shard_map/ppermute | solution.py:318
  77.6 9.5 %collective-permute-start.25 = (bf16[576,256]{1,0:T(8,128)(2,1)S(1)}, bf16[576,256]{1,0:T(8,128)(2,1)S(1)}, u32[]{:S(2)}, u32[]{:S(2)}) collective-permute-start(bf16[576,256]{1,0:T(8,128)(2,1)S(1)} %add_convert_fusion.2), channel_id=1, source_target_pairs={{0,4},{1,5},{4,8},{5,9},{8,12},{9,13},{12,14},{13,15},{14,10},{15,... | collective-permute-start | bytes 884744 | tf_op jit(solution)/shard_map/ppermute | solution.py:316
  78.3 8.8 %collective-permute-start.26 = (bf16[576,256]{1,0:T(8,128)(2,1)S(1)}, bf16[576,256]{1,0:T(8,128)(2,1)S(1)}, u32[]{:S(2)}, u32[]{:S(2)}) collective-permute-start(bf16[576,256]{1,0:T(8,128)(2,1)S(1)} %add_convert_fusion.1), channel_id=1, source_target_pairs={{0,2},{1,3},{4,0},{5,1},{8,4},{9,5},{12,8},{13,9},{14,12},{15,13},... | collective-permute-start | bytes 884744 | tf_op jit(solution)/shard_map/ppermute | solution.py:317
  79.7 12.7 %collective-permute-start.31 = (bf16[1728,256]{1,0:T(8,128)(2,1)S(1)}, bf16[1728,256]{1,0:T(8,128)(2,1)S(1)}, u32[]{:S(2)}, u32[]{:S(2)}) collective-permute-start(bf16[1728,256]{1,0:T(8,128)(2,1)S(1)} %constant_dynamic-update-slice_fusion.2.refs_0_), channel_id=1, source_target_pairs={{0,1},{1,0},{2,3},{3,2},{4,5},{5,4},{6,7},{7,6},{8,9},{9,8},{10,11... | collective-permute-start | bytes 2654216 | tf_op jit(solution)/shard_map/ppermute | solution.py:318
  79.7 8.8 %copy-start.4 = (f32[576,256]{1,0:T(8,128)S(1)}, f32[576,256]{1,0:T(8,128)}, u32[]{:S(2)}) copy-start(f32[576,256]{1,0:T(8,128)} %copy-done.3) | copy-start | bytes 1769476
  87.1 0.7 copy-start.5
  87.8 0.7 copy-start.6
  88.6 3.8 %collective-permute-start.32 = (bf16[1728,256]{1,0:T(8,128)(2,1)}, bf16[1728,256]{1,0:T(8,128)(2,1)S(1)}, u32[]{:S(2)}, u32[]{:S(2)}) collective-permute-start(bf16[1728,256]{1,0:T(8,128)(2,1)} %collective-permute-done.29.refs_2_), channel_id=1, source_target_pairs={{0,1},{1,0},{2,3},{3,2},{4,5},{5,4},{6,7},{7,6},{8,9},{9,8},{10,11... | collective-permute-start | bytes 2654216 | tf_op jit(solution)/shard_map/ppermute | solution.py:318
  89.8 1.6 %collective-permute-start.30 = (bf16[576,128]{1,0:T(8,128)(2,1)S(1)}, bf16[576,128]{1,0:T(8,128)(2,1)S(1)}, u32[]{:S(2)}, u32[]{:S(2)}) collective-permute-start(bf16[576,128]{1,0:T(8,128)(2,1)S(1)} %get-tuple-element.153), channel_id=1, source_target_pairs={{0,1},{1,0},{2,3},{3,2},{4,5},{5,4},{6,7},{7,6},{8,9},{9,8},{10,11... | collective-permute-start | bytes 442376 | tf_op jit(solution)/shard_map/ppermute | solution.py:318
  92.4 2.5 %copy-start.1 = (bf16[1152,2304]{1,0:T(8,128)(2,1)S(1)}, bf16[1152,2304]{1,0:T(8,128)(2,1)}, u32[]{:S(2)}) copy-start(bf16[1152,2304]{1,0:T(8,128)(2,1)} %copy-done) | copy-start | bytes 15925252

commit v2 on v1

--- a/solution.py
+++ b/solution.py
@@ -282,6 +282,51 @@
     )(q, after, g9t, *xs, *aliased)
 
 
+def last_sum_kernel(core, product, ahead, behind, keep, send):
+    part = keep.shape[1]
+    total = (product[...] + ahead[...].astype(F32) + behind[...].astype(F32)).astype(BF16)
+    for c, (first, second) in enumerate(((keep, send), (send, keep))):
+
+        @pl.when(core[0] == c)
+        def _(first=first, second=second):
+            first[...] = total[:, :part]
+            second[...] = total[:, part:]
+
+
+def last_sum_call(core, product, ahead, behind):
+    cells, lanes = product.shape
+    return pl.pallas_call(
+        last_sum_kernel,
+        out_shape=[jax.ShapeDtypeStruct((cells, lanes // 2), BF16)] * 2,
+        in_specs=[SMEM] + [VMEM] * 3,
+        out_specs=[VMEM] * 2,
+        compiler_params=pltpu.CompilerParams(vmem_limit_bytes=4 * MIB),
+        cost_estimate=LIGHT,
+        name="last_sum",
+    )(core, product, ahead, behind)
+
+
+def join_kernel(core, after, keep, other, out):
+    for c, order in enumerate(((keep, other), (other, keep))):
+
+        @pl.when(core[0] == c)
+        def _(order=order):
+            out[...] = jnp.transpose(jnp.concatenate([v[...] for v in order], axis=0))
+
+
+def join_call(core, after, keep, other):
+    cells, part = keep.shape
+    return pl.pallas_call(
+        join_kernel,
+        out_shape=jax.ShapeDtypeStruct((part, 2 * cells), BF16),
+        in_specs=[SMEM, ANY] + [VMEM] * 2,
+        out_specs=VMEM,
+        compiler_params=pltpu.CompilerParams(vmem_limit_bytes=4 * MIB),
+        cost_estimate=LIGHT,
+        name="join",
+    )(core, after, keep, other)
+
+
 def body(inputs, weight, bias_vector, cotangent):
     part, cells = inputs.shape
     devices = lax.axis_size("filt")
@@ -354,7 +399,9 @@
                 carry, token = forward_call(
                     q, token, [slot[d] for d in early], [block[d] for d in early], w_all, None
                 )
-            block[-s], block[s], token = tie(block[-s], block[s], token)
+            block[-s], token_a = tie(block[-s], token)
+            block[s], token_b = tie(block[s], token)
+            token = token_a
         if s < far - 1:
             ds = [0, -1, 1] if s == 1 else [-s, s]
             stack(ds, [block[d] for d in ds])
@@ -374,6 +421,7 @@
     top_p, low_p, after_top = grad_at(token, [far], BF16, 2)
     ahead, behind = onward(top_p), back(low_p)
     act_recv, g_recv = sibling(act_sib), sibling(g_sib)
+    after_top, g_recv = tie(after_top, g_recv)
     p_ahead, p_behind, token = grad_at(after_top, [far - 1, -(far - 1)], F32)
     gs = [jnp.concatenate([g_own, g_recv], axis=0)]
     waits = [act_recv, gs[0]] + [x for _, _, x in stacks[1:] if pair]
@@ -423,19 +471,12 @@
             waits.append(stacks[-1][2])
         ahead, behind, state["token"], *last = tie(*waits)
         others += last
-    final = (rest[0] + ahead.astype(F32) + behind.astype(F32)).astype(BF16)
-    keep = lax.dynamic_slice_in_dim(final, core * part, part, 1)
-    other = sibling(lax.dynamic_slice_in_dim(final, (1 - core) * part, part, 1))
+    keep, send = last_sum_call(core[None], rest[0], ahead, behind)
+    other = sibling(send)
     while state["next"] < len(stacks):
         weight_grads()
     total = state["total"]
-    input_grad = jnp.transpose(
-        jnp.where(
-            core == 0,
-            jnp.concatenate([keep, other], axis=0),
-            jnp.concatenate([other, keep], axis=0),
-        )
-    )
+    input_grad = join_call(core[None], state["token"], keep, other)
     bias_grad = bias_grad[0]
     if not pair:
         total, bias_grad = lax.psum((total, bias_grad), "case")

time: 103 us -> 94.4 us (0.917)
  local copies, waits for them, and re-layouts: 11.5 us -> 5.85 us
  other arithmetic: 1.88 us -> 0.64 us
    unnamed x23 -> x10, local copies, waits for them, and re-layouts: 8.34 us -> 2.7 us
    ppermute x8, starting transfers between devices: 6.88 us -> 3.42 us  [body(): back = lambda v: lax.ppermute(v, 'filt', backwards)]
    ppermute x8, starting transfers between devices: 10.4 us -> 13.9 us  [body(): onward = lambda v: lax.ppermute(v, 'filt', forwards)]
    ppermute x8, waiting for transfers between devices: 8.56 us -> 6 us  [body(): onward = lambda v: lax.ppermute(v, 'filt', forwards)]
    convert_element_type x1 -> x0, other arithmetic: 1.19 us -> none  [body(): final = (rest[0] + ahead.astype(F32) + behind.astype(F32)).astype(BF16)]
    pallas_call x3, Pallas kernels: 18.4 us -> 17.3 us  [weight_grad_call(): pl.pallas_call(functools.partial(weight_grad_kernel, len(xs), scale), out...]
  transfers between devices with their start and end apart: 33 -> 33, of which waited for: 14 -> 15; matrix products, arithmetic and copies ran while one was open for 5% -> 3% of each run, Pallas kernels for 32% -> 41%
where the time goes in v2:
time: 94.4 us; the launch traced here: 94.1 us
  Pallas kernels  39.5 us (42%)
  starting transfers between devices  25.7 us (27%)
  waiting for transfers between devices  21.5 us (23%)
  local copies, waits for them, and re-layouts  5.85 us (6%)
    pallas_call x3, Pallas kernels, weight_grad_call(): pl.pallas_call(functools.partial(weight_grad_kernel, len(xs), scale), out...  17.3 us
    ppermute x8, starting transfers between devices, body(): onward = lambda v: lax.ppermute(v, 'filt', forwards)  13.9 us
    pallas_call x3, Pallas kernels, input_grad_call(): pl.pallas_call(functools.partial(input_grad_kernel, slots, pieces), out_s...  7.69 us
    ppermute x8, waiting for transfers between devices, body(): back = lambda v: lax.ppermute(v, 'filt', backwards)  6.49 us
    pallas_call x2, Pallas kernels, forward_call(): pl.pallas_call(functools.partial(forward_kernel, slots, carry is not None...  6.38 us
    ppermute x8, waiting for transfers between devices, body(): onward = lambda v: lax.ppermute(v, 'filt', forwards)  6 us
    ppermute x13, waiting for transfers between devices, body(): sibling = lambda v: lax.ppermute(v, 'filt', swap)  5.64 us
    ppermute x4, starting transfers between devices, body(): across = lambda v: lax.ppermute(v, 'case', [(0, 1), (1, 0)])  5.26 us
  transfers between devices with their start and end apart: 33, of which 15 were waited for; matrix products, arithmetic and copies ran while one was open for 3% of the time, Pallas kernels for 41%

profile of v2, /device:TPU:0, one launch (start us, length us, event | category | flops | bytes accessed | tf_op | source)
XLA Modules:
  0.0 94.1 jit_solution(12943161319262359647)
XLA Ops:
  0.7 1.2 %constant_dynamic-slice_fusion.1 = (bf16[128,576]{1,0:T(8,128)(2,1)S(1)}, bf16[128,576]{1,0:T(8,128)(2,1)S(1)}) fusion(bf16[128,1152]{1,0:T(8,128)(2,1)} %param.5, s32[]{:T(128)S(6)} %select_n.35, s32[]{:T(128)S(6)} %select_n.36), kind=kLoop, calls=%fused_computation.22 | loop fusion | bytes 589832 | tf_op jit(solution)/shard_map/dynamic-slice
  1.8 0.1 copy.16
  2.0 0.5 collective-permute-start
  2.5 1.0 %collective-permute-done = bf16[576,128]{1,0:T(8,128)(2,1)S(1)} collective-permute-done((bf16[576,128]{1,0:T(8,128)(2,1)S(1)}, bf16[576,128]{1,0:T(8,128)(2,1)S(1)}, u32[]{:S(2)}, u32[]{:S(2)}) %collective-permute-start) | collective-permute-done | bytes 147488 | tf_op jit(solution)/shard_map/ppermute | solution.py:363
  3.5 0.4 collective-permute-start.6
  3.9 0.1 copy.15
  4.0 0.1 maximum_select_fusion.refs_0_
  4.1 2.8 %collective-permute-start.1 = (bf16[576,256]{1,0:T(8,128)(2,1)S(1)}, bf16[576,256]{1,0:T(8,128)(2,1)S(1)}, u32[]{:S(2)}, u32[]{:S(2)}) collective-permute-start(bf16[576,256]{1,0:T(8,128)(2,1)S(1)} %maximum_select_fusion.refs_0_), channel_id=1, source_target_pairs={{0,4},{1,5},{4,8},{5,9},{8,12},{9,13},{12,14},{13,15},{14,10},{15,... | collective-permute-start | bytes 884744 | tf_op jit(solution)/shard_map/ppermute | solution.py:361
  6.9 1.2 %copy.13 = bf16[128,1152]{0,1:T(8,128)(2,1)S(1)} copy(bf16[128,1152]{1,0:T(8,128)(2,1)} %param.8) | data formatting | bytes 589824 | tf_op jit(solution)/shard_map/optimization_barrier | solution.py:366
  8.1 0.1 collective-permute-start.3
  8.3 0.4 collective-permute-start.4
  8.7 2.9 %collective-permute-done.4 = f32[1,128]{1,0:T(1,128)S(1)} collective-permute-done((f32[1,128]{1,0:T(1,128)S(1)}, f32[1,128]{1,0:T(1,128)S(1)}, u32[]{:S(2)}, u32[]{:S(2)}) %collective-permute-start.4) | collective-permute-done | bytes 544 | tf_op jit(solution)/shard_map/ppermute | solution.py:363
  11.6 2.7 %collective-permute-done.1.refs_1_ = bf16[576,256]{1,0:T(8,128)(2,1)S(1)} collective-permute-done((bf16[576,256]{1,0:T(8,128)(2,1)S(1)}, bf16[576,256]{1,0:T(8,128)(2,1)S(1)}, u32[]{:S(2)}, u32[]{:S(2)}) %collective-permute-start.1) | collective-permute-done | bytes 294944 | tf_op jit(solution)/shard_map/ppermute | solution.py:361
  14.4 1.5 %collective-permute-done.2.refs_2_ = bf16[576,256]{1,0:T(8,128)(2,1)S(1)} collective-permute-done((bf16[576,256]{1,0:T(8,128)(2,1)S(1)}, bf16[576,256]{1,0:T(8,128)(2,1)S(1)}, u32[]{:S(2)}, u32[]{:S(2)}) %collective-permute-start.2) | collective-permute-done | bytes 294944 | tf_op jit(solution)/shard_map/ppermute | solution.py:362
  16.0 1.6 %collective-permute-start.12 = (bf16[1728,256]{1,0:T(8,128)(2,1)S(1)}, bf16[1728,256]{1,0:T(8,128)(2,1)S(1)}, u32[]{:S(2)}, u32[]{:S(2)}) collective-permute-start(bf16[1728,256]{1,0:T(8,128)(2,1)S(1)} %pad_maximum_fusion.refs_0_), channel_id=1, source_target_pairs={{0,16},{16,0},{1,17},{17,1},{2,18},{18,2},{3,19},{19,3},{4,20},{20... | collective-permute-start | bytes 2654216 | tf_op jit(solution)/shard_map/ppermute | solution.py:365
  17.6 1.6 %collective-permute-start.5 = (bf16[576,256]{1,0:T(8,128)(2,1)S(1)}, bf16[576,256]{1,0:T(8,128)(2,1)S(1)}, u32[]{:S(2)}, u32[]{:S(2)}) collective-permute-start(bf16[576,256]{1,0:T(8,128)(2,1)S(1)} %collective-permute-done.1.refs_1_), channel_id=1, source_target_pairs={{0,4},{1,5},{4,8},{5,9},{8,12},{9,13},{12,14},{13,15},{14,10},{15,... | collective-permute-start | bytes 884744 | tf_op jit(solution)/shard_map/ppermute | solution.py:361
  19.1 0.4 collective-permute-start.8
  19.6 2.3 %copy-done = bf16[9,128,2048]{2,1,0:T(8,128)(2,1)S(1)} copy-done((bf16[9,128,2048]{2,1,0:T(8,128)(2,1)S(1)}, bf16[9,128,2048]{2,1,0:T(8,128)(2,1)}, u32[]{:S(2)}) %copy-start) | copy-done | bytes 4718616
  21.9 2.7 %hold.1 = (bf16[9,256,2048]{2,1,0:T(8,128)(2,1)S(1)}, f32[8,128]{1,0:T(8,128)S(1)}) custom-call(bf16[9,128,2048]{2,1,0:T(8,128)(2,1)S(1)} %copy-done, bf16[9,128,2048]{2,1,0:T(8,128)(2,1)} %collective-permute-done.6.w_sib), custom_call_target="tpu_custom_call" | custom-call | flops 1000 | bytes 1000 | tf_op jit(solution)/shard_map/hold/pallas_call | solution.py:81
  24.6 0.8 collective-permute-done.5.refs_3_
  25.4 1.6 %collective-permute-start.7 = (bf16[576,256]{1,0:T(8,128)(2,1)S(1)}, bf16[576,256]{1,0:T(8,128)(2,1)S(1)}, u32[]{:S(2)}, u32[]{:S(2)}) collective-permute-start(bf16[576,256]{1,0:T(8,128)(2,1)S(1)} %collective-permute-done.5.refs_3_), channel_id=1, source_target_pairs={{0,4},{1,5},{4,8},{5,9},{8,12},{9,13},{12,14},{13,15},{14,10},{15,... | collective-permute-start | bytes 884744 | tf_op jit(solution)/shard_map/ppermute | solution.py:361
  27.0 0.4 collective-permute-start.10
  27.5 0.6 collective-permute-start.17
  28.1 0.7 fusion.q_ref
  28.8 4.2 %forward.2 = (f32[3,576,256]{2,1,0:T(8,128)S(1)}, f32[8,128]{1,0:T(8,128)S(1)}) custom-call(s32[8]{0:T(128)S(1)} %fusion.q_ref, f32[8,128]{1,0:T(8,128)S(1)} %get-tuple-element.87.after, bf16[9,256,2048]{2,1,0:T(8,128)(2,1)S(1)} %get-tuple-element.88.w_all, bf16[576,256]{1,0:T(8,128)(2,1)S(1)} %maximum_select_fusion.refs_0_, ...), custom_call_target="tpu_custom_call" | custom-call | flops 1000 | bytes 1000 | tf_op jit(solution)/shard_map/forward/pallas_call | solution.py:124
  33.0 1.6 %collective-permute-start.9 = (bf16[288,256]{1,0:T(8,128)(2,1)S(1)}, bf16[288,256]{1,0:T(8,128)(2,1)S(1)}, u32[]{:S(2)}, u32[]{:S(2)}) collective-permute-start(bf16[288,256]{1,0:T(8,128)(2,1)S(1)} %slice.20), channel_id=1, source_target_pairs={{0,4},{1,5},{4,8},{5,9},{8,12},{9,13},{12,14},{13,15},{14,10},{15,... | collective-permute-start | bytes 442376 | tf_op jit(solution)/shard_map/ppermute | solution.py:361
  34.7 0.5 collective-permute-start.11
  35.2 2.2 %forward.3 = (f32[3,576,256]{2,1,0:T(8,128)S(1)}, f32[8,128]{1,0:T(8,128)S(1)}) custom-call(s32[8]{0:T(128)S(1)} %fusion.q_ref, f32[8,128]{1,0:T(8,128)S(1)} %get-tuple-element.94.after, bf16[9,256,2048]{2,1,0:T(8,128)(2,1)S(1)} %get-tuple-element.88.w_all, f32[3,576,256]{2,1,0:T(8,128)S(1)} %get-tuple-element.95.refs_0_, ...), custom_call_target="tpu_custom_call" | custom-call | flops 1000 | bytes 1000 | tf_op jit(solution)/shard_map/forward/pallas_call | solution.py:124
  37.3 1.3 %collective-permute-done.12.refs_2_ = bf16[1728,256]{1,0:T(8,128)(2,1)S(1)} collective-permute-done((bf16[1728,256]{1,0:T(8,128)(2,1)S(1)}, bf16[1728,256]{1,0:T(8,128)(2,1)S(1)}, u32[]{:S(2)}, u32[]{:S(2)}) %collective-permute-start.12) | collective-permute-done | bytes 884768 | tf_op jit(solution)/shard_map/ppermute | solution.py:365
  38.6 1.2 %collective-permute-done.11.refs_1_ = bf16[288,256]{1,0:T(8,128)(2,1)S(1)} collective-permute-done((bf16[288,256]{1,0:T(8,128)(2,1)S(1)}, bf16[288,256]{1,0:T(8,128)(2,1)S(1)}, u32[]{:S(2)}, u32[]{:S(2)}) %collective-permute-start.11) | collective-permute-done | bytes 147488 | tf_op jit(solution)/shard_map/ppermute | solution.py:362
  39.9 2.0 %gate.1 = (bf16[576,128]{1,0:T(8,128)(2,1)S(1)}, bf16[576,128]{1,0:T(8,128)(2,1)S(1)}, bf16[576,128]{1,0:T(8,128)(2,1)S(1)}, bf16[576,128]{1,0:T(8,128)(2,1)S(1)}, bf16[576,2304]{1,0:T(8,128)(2,1)S(1)}) custom-call(s32[8]{0:T(128)S(1)} %fusion.q_ref, f32[8,128]{1,0:T(8,128)S(1)} %get-tuple-element.97.after, ...), custom_call_target="tpu_custom_call" | custom-call | flops 1000 | bytes 1000 | tf_op jit(solution)/shard_map/gate/pallas_call | solution.py:169
  41.9 1.4 %input_grad.3 = (bf16[288,256]{1,0:T(8,128)(2,1)S(1)}, bf16[288,256]{1,0:T(8,128)(2,1)S(1)}, f32[8,128]{1,0:T(8,128)S(1)}) custom-call(s32[8]{0:T(128)S(1)} %fusion.q_ref, f32[8,128]{1,0:T(8,128)S(1)} %get-tuple-element.97.after, bf16[9,256,2048]{2,1,0:T(8,128)(2,1)S(1)} %get-tuple-element.88.w_all, bf16[576,2304]{1,0:T(8,128)(2,1)S(1)} %get-tuple-element.103.g9), custom_call_target="tpu_custom_call" | custom-call | flops 1000 | bytes 1000 | tf_op jit(solution)/shard_map/input_grad/pallas_call | solution.py:199
  43.4 1.6 %collective-permute-start.14 = (bf16[288,256]{1,0:T(8,128)(2,1)S(1)}, bf16[288,256]{1,0:T(8,128)(2,1)S(1)}, u32[]{:S(2)}, u32[]{:S(2)}) collective-permute-start(bf16[288,256]{1,0:T(8,128)(2,1)S(1)} %get-tuple-element.108), channel_id=1, source_target_pairs={{0,4},{1,5},{4,8},{5,9},{8,12},{9,13},{12,14},{13,15},{14,10},{15,... | collective-permute-start | bytes 442376 | tf_op jit(solution)/shard_map/ppermute | solution.py:361
  45.0 0.5 collective-permute-start.15
  45.4 2.1 %input_grad.4 = (f32[576,256]{1,0:T(8,128)S(1)}, f32[576,256]{1,0:T(8,128)S(1)}, f32[8,128]{1,0:T(8,128)S(1)}) custom-call(s32[8]{0:T(128)S(1)} %fusion.q_ref, f32[8,128]{1,0:T(8,128)S(1)} %get-tuple-element.106.after, bf16[9,256,2048]{2,1,0:T(8,128)(2,1)S(1)} %get-tuple-element.88.w_all, bf16[576,2304]{1,0:T(8,128)(2,1)S(1)} %get-tuple-element.103.g9), custom_call_target="tpu_custom_call" | custom-call | flops 1000 | bytes 1000 | tf_op jit(solution)/shard_map/input_grad/pallas_call | solution.py:199
  47.6 2.0 %collective-permute-done.14 = bf16[288,256]{1,0:T(8,128)(2,1)S(1)} collective-permute-done((bf16[288,256]{1,0:T(8,128)(2,1)S(1)}, bf16[288,256]{1,0:T(8,128)(2,1)S(1)}, u32[]{:S(2)}, u32[]{:S(2)}) %collective-permute-start.14) | collective-permute-done | bytes 147488 | tf_op jit(solution)/shard_map/ppermute | solution.py:361
  49.7 1.3 %collective-permute-done.15 = bf16[288,256]{1,0:T(8,128)(2,1)S(1)} collective-permute-done((bf16[288,256]{1,0:T(8,128)(2,1)S(1)}, bf16[288,256]{1,0:T(8,128)(2,1)S(1)}, u32[]{:S(2)}, u32[]{:S(2)}) %collective-permute-start.15) | collective-permute-done | bytes 147488 | tf_op jit(solution)/shard_map/ppermute | solution.py:362
  51.1 1.5 %collective-permute-start.18 = (bf16[576,256]{1,0:T(8,128)(2,1)S(1)}, bf16[576,256]{1,0:T(8,128)(2,1)S(1)}, u32[]{:S(2)}, u32[]{:S(2)}) collective-permute-start(bf16[576,256]{1,0:T(8,128)(2,1)S(1)} %pad_maximum_fusion.2), channel_id=1, source_target_pairs={{0,4},{1,5},{4,8},{5,9},{8,12},{9,13},{12,14},{13,15},{14,10},{15,... | collective-permute-start | bytes 884744 | tf_op jit(solution)/shard_map/ppermute | solution.py:361
  52.7 0.5 collective-permute-start.19
  53.2 1.5 %collective-permute-start.20 = (bf16[1152,128]{1,0:T(8,128)(2,1)S(1)}, bf16[1152,128]{1,0:T(8,128)(2,1)S(1)}, u32[]{:S(2)}, u32[]{:S(2)}) collective-permute-start(bf16[1152,128]{1,0:T(8,128)(2,1)S(1)} %pad_maximum_fusion.1.refs_0_), channel_id=1, source_target_pairs={{0,16},{16,0},{1,17},{17,1},{2,18},{18,2},{3,19},{19,3},{4,20},{20... | collective-permute-start | bytes 884744 | tf_op jit(solution)/shard_map/ppermute | solution.py:365
  54.7 0.6 collective-permute-start.24
  55.3 4.2 %input_grad.5 = (f32[576,256]{1,0:T(8,128)S(1)}, f32[576,256]{1,0:T(8,128)S(1)}, f32[576,256]{1,0:T(8,128)S(1)}, f32[576,256]{1,0:T(8,128)S(1)}, f32[576,256]{1,0:T(8,128)S(1)}, /*index=5*/f32[8,128]{1,0:T(8,128)S(1)}) custom-call(s32[8]{0:T(128)S(1)} %fusion.q_ref, f32[8,128]{1,0:T(8,128)S(1)} %get-tuple-element.119.after, ...), custom_call_target="tpu_custom_call" | custom-call | flops 1000 | bytes 1000 | tf_op jit(solution)/shard_map/input_grad/pallas_call | solution.py:199
  59.5 1.2 %collective-permute-done.19 = bf16[576,256]{1,0:T(8,128)(2,1)S(1)} collective-permute-done((bf16[576,256]{1,0:T(8,128)(2,1)S(1)}, bf16[576,256]{1,0:T(8,128)(2,1)S(1)}, u32[]{:S(2)}, u32[]{:S(2)}) %collective-permute-start.19) | collective-permute-done | bytes 294944 | tf_op jit(solution)/shard_map/ppermute | solution.py:362
  60.7 0.3 collective-permute-done.20.refs_1_
  61.0 0.1 add_convert_fusion.2
  61.1 1.5 %collective-permute-start.21 = (bf16[576,256]{1,0:T(8,128)(2,1)S(1)}, bf16[576,256]{1,0:T(8,128)(2,1)S(1)}, u32[]{:S(2)}, u32[]{:S(2)}) collective-permute-start(bf16[576,256]{1,0:T(8,128)(2,1)S(1)} %add_convert_fusion.3), channel_id=1, source_target_pairs={{0,4},{1,5},{4,8},{5,9},{8,12},{9,13},{12,14},{13,15},{14,10},{15,... | collective-permute-start | bytes 884744 | tf_op jit(solution)/shard_map/ppermute | solution.py:361
  62.6 0.5 collective-permute-start.22
  63.2 1.6 %collective-permute-start.29 = (bf16[1728,256]{1,0:T(8,128)(2,1)S(1)}, bf16[1728,256]{1,0:T(8,128)(2,1)S(1)}, u32[]{:S(2)}, u32[]{:S(2)}) collective-permute-start(bf16[1728,256]{1,0:T(8,128)(2,1)S(1)} %constant_dynamic-update-slice_fusion.2.refs_0_), channel_id=1, source_target_pairs={{0,16},{16,0},{1,17},{17,1},{2,18},{18,2},{3,19},{19,3},{4,20},{20... | collective-permute-start | bytes 2654216 | tf_op jit(solution)/shard_map/ppermute | solution.py:365
  64.8 2.4 %displaced.1 = (bf16[1152,2304]{1,0:T(8,128)(2,1)S(1)}, f32[1,128]{1,0:T(1,128)}, bf16[128,1152]{1,0:T(8,128)(2,1)}) custom-call(s32[1]{0:T(128)} %bitcast.core, f32[8,128]{1,0:T(8,128)S(1)} %get-tuple-element.122.after, bf16[576,128]{1,0:T(8,128)(2,1)S(1)} %get-tuple-element.123.act_own, bf16[576,128]{1,0:T(8,128)(2,1)S(1)} %collective-permute-done.16.act_sib, ...), custom_call_target="tpu_custom_call" | custom-call | flops 1000 | bytes 1000 | tf_op jit(solution)/shard_map/displaced/pallas_call | solution.py:236
  67.2 0.5 collective-permute-start.28
  67.7 6.3 %weight_grad.3 = (f32[1152,2048]{1,0:T(8,128)}, f32[8,128]{1,0:T(8,128)S(1)}) custom-call(s32[8]{0:T(128)S(1)} %fusion.q_ref, f32[8,128]{1,0:T(8,128)S(1)} %get-tuple-element.122.after, bf16[1152,2304]{1,0:T(8,128)(2,1)S(1)} %get-tuple-element.135.g9t, bf16[1728,256]{1,0:T(8,128)(2,1)S(1)} %pad_maximum_fusion.refs_0_, ...), custom_call_target="tpu_custom_call" | custom-call | flops 1000 | bytes 1000 | tf_op jit(solution)/shard_map/weight_grad/pallas_call | solution.py:265
  74.1 0.1 add_convert_fusion.1
  74.2 0.1 add_convert_fusion
  74.3 1.6 %collective-permute-start.25 = (bf16[576,256]{1,0:T(8,128)(2,1)S(1)}, bf16[576,256]{1,0:T(8,128)(2,1)S(1)}, u32[]{:S(2)}, u32[]{:S(2)}) collective-permute-start(bf16[576,256]{1,0:T(8,128)(2,1)S(1)} %add_convert_fusion.1), channel_id=1, source_target_pairs={{0,4},{1,5},{4,8},{5,9},{8,12},{9,13},{12,14},{13,15},{14,10},{15,... | collective-permute-start | bytes 884744 | tf_op jit(solution)/shard_map/ppermute | solution.py:361
  75.8 0.5 collective-permute-start.26
  76.3 4.7 %weight_grad.4 = (f32[1152,2048]{1,0:T(8,128)}, f32[8,128]{1,0:T(8,128)S(1)}) custom-call(s32[8]{0:T(128)S(1)} %fusion.q_ref, f32[8,128]{1,0:T(8,128)S(1)} %get-tuple-element.143.after, bf16[1152,2304]{1,0:T(8,128)(2,1)S(1)} %get-tuple-element.135.g9t, ...), custom_call_target="tpu_custom_call", output_to_operand_aliasing={{0}: (7, {})} | custom-call | flops 1000 | bytes 1000 | tf_op jit(solution)/shard_map/weight_grad/pallas_call | solution.py:265
  81.1 1.8 %collective-permute-done.29.refs_2_ = bf16[1728,256]{1,0:T(8,128)(2,1)S(1)} collective-permute-done((bf16[1728,256]{1,0:T(8,128)(2,1)S(1)}, bf16[1728,256]{1,0:T(8,128)(2,1)S(1)}, u32[]{:S(2)}, u32[]{:S(2)}) %collective-permute-start.29) | collective-permute-done | bytes 884768 | tf_op jit(solution)/shard_map/ppermute | solution.py:365
  82.9 0.4 collective-permute-done.25.ahead
  83.3 1.2 %collective-permute-done.26.behind = bf16[576,256]{1,0:T(8,128)(2,1)S(1)} collective-permute-done((bf16[576,256]{1,0:T(8,128)(2,1)S(1)}, bf16[576,256]{1,0:T(8,128)(2,1)S(1)}, u32[]{:S(2)}, u32[]{:S(2)}) %collective-permute-start.26) | collective-permute-done | bytes 294944 | tf_op jit(solution)/shard_map/ppermute | solution.py:362
  84.5 0.2 last_sum.1
  84.7 0.6 collective-permute-start.32
  85.3 1.7 %collective-permute-done.31.refs_3_ = bf16[1728,256]{1,0:T(8,128)(2,1)S(1)} collective-permute-done((bf16[1728,256]{1,0:T(8,128)(2,1)S(1)}, bf16[1728,256]{1,0:T(8,128)(2,1)S(1)}, u32[]{:S(2)}, u32[]{:S(2)}) %collective-permute-start.31) | collective-permute-done | bytes 884768 | tf_op jit(solution)/shard_map/ppermute | solution.py:363
  86.9 6.3 %weight_grad.5 = (f32[1152,2048]{1,0:T(8,128)}, f32[8,128]{1,0:T(8,128)S(1)}) custom-call(s32[8]{0:T(128)S(1)} %fusion.q_ref, f32[8,128]{1,0:T(8,128)S(1)} %get-tuple-element.147.after, bf16[1152,2304]{1,0:T(8,128)(2,1)S(1)} %get-tuple-element.135.g9t, ...), custom_call_target="tpu_custom_call", output_to_operand_aliasing={{0}: (7, {})} | custom-call | flops 1000 | bytes 1000 | tf_op jit(solution)/shard_map/weight_grad/pallas_call | solution.py:265
  93.3 0.9 join.1
  (46 shorter events, 0.6 us)
Async XLA Ops:
  0.6 7.6 %copy-start.1 = (f32[128]{0:T(128)S(1)}, f32[128]{0:T(128)}, u32[]{:S(2)}) copy-start(f32[128]{0:T(128)} %param.7) | copy-start | bytes 1540
  2.0 1.5 %collective-permute-start = (bf16[576,128]{1,0:T(8,128)(2,1)S(1)}, bf16[576,128]{1,0:T(8,128)(2,1)S(1)}, u32[]{:S(2)}, u32[]{:S(2)}) collective-permute-start(bf16[576,128]{1,0:T(8,128)(2,1)S(1)} %bitcast.14), channel_id=1, source_target_pairs={{0,1},{1,0},{2,3},{3,2},{4,5},{5,4},{6,7},{7,6},{8,9},{9,8},{10,11... | collective-permute-start | bytes 442376 | tf_op jit(solution)/shard_map/ppermute | solution.py:363
  3.5 16.1 %collective-permute-start.6 = (bf16[9,128,2048]{2,1,0:T(8,128)(2,1)}, bf16[9,128,2048]{2,1,0:T(8,128)(2,1)}, u32[]{:S(2)}, u32[]{:S(2)}) collective-permute-start(bf16[9,128,2048]{2,1,0:T(8,128)(2,1)} %w_own), channel_id=1, source_target_pairs={{0,1},{1,0},{2,3},{3,2},{4,5},{5,4},{6,7},{7,6},{8,9},{9,8},{10,11... | collective-permute-start | bytes 14155784 | tf_op jit(solution)/shard_map/ppermute | solution.py:363
  4.1 10.2 %collective-permute-start.1 = (bf16[576,256]{1,0:T(8,128)(2,1)S(1)}, bf16[576,256]{1,0:T(8,128)(2,1)S(1)}, u32[]{:S(2)}, u32[]{:S(2)}) collective-permute-start(bf16[576,256]{1,0:T(8,128)(2,1)S(1)} %maximum_select_fusion.refs_0_), channel_id=1, source_target_pairs={{0,4},{1,5},{4,8},{5,9},{8,12},{9,13},{12,14},{13,15},{14,10},{15,... | collective-permute-start | bytes 884744 | tf_op jit(solution)/shard_map/ppermute | solution.py:361
  6.9 9.0 %collective-permute-start.2 = (bf16[576,256]{1,0:T(8,128)(2,1)S(1)}, bf16[576,256]{1,0:T(8,128)(2,1)S(1)}, u32[]{:S(2)}, u32[]{:S(2)}) collective-permute-start(bf16[576,256]{1,0:T(8,128)(2,1)S(1)} %maximum_select_fusion.refs_0_), channel_id=1, source_target_pairs={{0,2},{1,3},{4,0},{5,1},{8,4},{9,5},{12,8},{13,9},{14,12},{15,13},... | collective-permute-start | bytes 884744 | tf_op jit(solution)/shard_map/ppermute | solution.py:362
  8.1 3.5 %collective-permute-start.3 = (bf16[576,128]{1,0:T(8,128)(2,1)S(1)}, bf16[576,128]{1,0:T(8,128)(2,1)S(1)}, u32[]{:S(2)}, u32[]{:S(2)}) collective-permute-start(bf16[576,128]{1,0:T(8,128)(2,1)S(1)} %get-tuple-element.159), channel_id=1, source_target_pairs={{0,1},{1,0},{2,3},{3,2},{4,5},{5,4},{6,7},{7,6},{8,9},{9,8},{10,11... | collective-permute-start | bytes 442376 | tf_op jit(solution)/shard_map/ppermute | solution.py:363
  8.3 3.4 %collective-permute-start.4 = (f32[1,128]{1,0:T(1,128)S(1)}, f32[1,128]{1,0:T(1,128)S(1)}, u32[]{:S(2)}, u32[]{:S(2)}) collective-permute-start(f32[1,128]{1,0:T(1,128)S(1)} %bitcast.15), channel_id=1, source_target_pairs={{0,1},{1,0},{2,3},{3,2},{4,5},{5,4},{6,7},{7,6},{8,9},{9,8},{10,11... | collective-permute-start | bytes 1544 | tf_op jit(solution)/shard_map/ppermute | solution.py:363
  16.0 22.6 %collective-permute-start.12 = (bf16[1728,256]{1,0:T(8,128)(2,1)S(1)}, bf16[1728,256]{1,0:T(8,128)(2,1)S(1)}, u32[]{:S(2)}, u32[]{:S(2)}) collective-permute-start(bf16[1728,256]{1,0:T(8,128)(2,1)S(1)} %pad_maximum_fusion.refs_0_), channel_id=1, source_target_pairs={{0,16},{16,0},{1,17},{17,1},{2,18},{18,2},{3,19},{19,3},{4,20},{20... | collective-permute-start | bytes 2654216 | tf_op jit(solution)/shard_map/ppermute | solution.py:365
  17.6 7.9 %collective-permute-start.5 = (bf16[576,256]{1,0:T(8,128)(2,1)S(1)}, bf16[576,256]{1,0:T(8,128)(2,1)S(1)}, u32[]{:S(2)}, u32[]{:S(2)}) collective-permute-start(bf16[576,256]{1,0:T(8,128)(2,1)S(1)} %collective-permute-done.1.refs_1_), channel_id=1, source_target_pairs={{0,4},{1,5},{4,8},{5,9},{8,12},{9,13},{12,14},{13,15},{14,10},{15,... | collective-permute-start | bytes 884744 | tf_op jit(solution)/shard_map/ppermute | solution.py:361
  19.1 7.9 %collective-permute-start.8 = (bf16[576,256]{1,0:T(8,128)(2,1)S(1)}, bf16[576,256]{1,0:T(8,128)(2,1)S(1)}, u32[]{:S(2)}, u32[]{:S(2)}) collective-permute-start(bf16[576,256]{1,0:T(8,128)(2,1)S(1)} %collective-permute-done.2.refs_2_), channel_id=1, source_target_pairs={{0,2},{1,3},{4,0},{5,1},{8,4},{9,5},{12,8},{13,9},{14,12},{15,13},... | collective-permute-start | bytes 884744 | tf_op jit(solution)/shard_map/ppermute | solution.py:362
  19.6 2.3 %copy-start = (bf16[9,128,2048]{2,1,0:T(8,128)(2,1)S(1)}, bf16[9,128,2048]{2,1,0:T(8,128)(2,1)}, u32[]{:S(2)}) copy-start(bf16[9,128,2048]{2,1,0:T(8,128)(2,1)} %w_own) | copy-start | bytes 14155780
  25.4 7.6 %collective-permute-start.7 = (bf16[576,256]{1,0:T(8,128)(2,1)S(1)}, bf16[576,256]{1,0:T(8,128)(2,1)S(1)}, u32[]{:S(2)}, u32[]{:S(2)}) collective-permute-start(bf16[576,256]{1,0:T(8,128)(2,1)S(1)} %collective-permute-done.5.refs_3_), channel_id=1, source_target_pairs={{0,4},{1,5},{4,8},{5,9},{8,12},{9,13},{12,14},{13,15},{14,10},{15,... | collective-permute-start | bytes 884744 | tf_op jit(solution)/shard_map/ppermute | solution.py:361
  27.0 7.7 %collective-permute-start.10 = (bf16[576,256]{1,0:T(8,128)(2,1)S(1)}, bf16[576,256]{1,0:T(8,128)(2,1)S(1)}, u32[]{:S(2)}, u32[]{:S(2)}) collective-permute-start(bf16[576,256]{1,0:T(8,128)(2,1)S(1)} %collective-permute-done.8.refs_4_), channel_id=1, source_target_pairs={{0,2},{1,3},{4,0},{5,1},{8,4},{9,5},{12,8},{13,9},{14,12},{15,13},... | collective-permute-start | bytes 884744 | tf_op jit(solution)/shard_map/ppermute | solution.py:362
  27.5 23.5 %collective-permute-start.17 = (bf16[1152,256]{1,0:T(8,128)(2,1)S(1)}, bf16[1152,256]{1,0:T(8,128)(2,1)S(1)}, u32[]{:S(2)}, u32[]{:S(2)}) collective-permute-start(bf16[1152,256]{1,0:T(8,128)(2,1)S(1)} %constant_dynamic-update-slice_fusion.refs_0_), channel_id=1, source_target_pairs={{0,16},{16,0},{1,17},{17,1},{2,18},{18,2},{3,19},{19,3},{4,20},{20... | collective-permute-start | bytes 1769480 | tf_op jit(solution)/shard_map/ppermute | solution.py:365
  33.0 5.6 %collective-permute-start.9 = (bf16[288,256]{1,0:T(8,128)(2,1)S(1)}, bf16[288,256]{1,0:T(8,128)(2,1)S(1)}, u32[]{:S(2)}, u32[]{:S(2)}) collective-permute-start(bf16[288,256]{1,0:T(8,128)(2,1)S(1)} %slice.20), channel_id=1, source_target_pairs={{0,4},{1,5},{4,8},{5,9},{8,12},{9,13},{12,14},{13,15},{14,10},{15,... | collective-permute-start | bytes 442376 | tf_op jit(solution)/shard_map/ppermute | solution.py:361
  34.7 5.2 %collective-permute-start.11 = (bf16[288,256]{1,0:T(8,128)(2,1)S(1)}, bf16[288,256]{1,0:T(8,128)(2,1)S(1)}, u32[]{:S(2)}, u32[]{:S(2)}) collective-permute-start(bf16[288,256]{1,0:T(8,128)(2,1)S(1)} %slice.21), channel_id=1, source_target_pairs={{0,2},{1,3},{4,0},{5,1},{8,4},{9,5},{12,8},{13,9},{14,12},{15,13},... | collective-permute-start | bytes 442376 | tf_op jit(solution)/shard_map/ppermute | solution.py:362
  41.9 3.6 %collective-permute-start.13 = (bf16[576,128]{1,0:T(8,128)(2,1)S(1)}, bf16[576,128]{1,0:T(8,128)(2,1)S(1)}, u32[]{:S(2)}, u32[]{:S(2)}) collective-permute-start(bf16[576,128]{1,0:T(8,128)(2,1)S(1)} %get-tuple-element.105), channel_id=1, source_target_pairs={{0,1},{1,0},{2,3},{3,2},{4,5},{5,4},{6,7},{7,6},{8,9},{9,8},{10,11... | collective-permute-start | bytes 442376 | tf_op jit(solution)/shard_map/ppermute | solution.py:363
  43.4 6.3 %collective-permute-start.14 = (bf16[288,256]{1,0:T(8,128)(2,1)S(1)}, bf16[288,256]{1,0:T(8,128)(2,1)S(1)}, u32[]{:S(2)}, u32[]{:S(2)}) collective-permute-start(bf16[288,256]{1,0:T(8,128)(2,1)S(1)} %get-tuple-element.108), channel_id=1, source_target_pairs={{0,4},{1,5},{4,8},{5,9},{8,12},{9,13},{12,14},{13,15},{14,10},{15,... | collective-permute-start | bytes 442376 | tf_op jit(solution)/shard_map/ppermute | solution.py:361
  45.0 6.0 %collective-permute-start.15 = (bf16[288,256]{1,0:T(8,128)(2,1)S(1)}, bf16[288,256]{1,0:T(8,128)(2,1)S(1)}, u32[]{:S(2)}, u32[]{:S(2)}) collective-permute-start(bf16[288,256]{1,0:T(8,128)(2,1)S(1)} %get-tuple-element.109), channel_id=1, source_target_pairs={{0,2},{1,3},{4,0},{5,1},{8,4},{9,5},{12,8},{13,9},{14,12},{15,13},... | collective-permute-start | bytes 442376 | tf_op jit(solution)/shard_map/ppermute | solution.py:362
  45.4 5.5 %collective-permute-start.16 = (bf16[576,128]{1,0:T(8,128)(2,1)S(1)}, bf16[576,128]{1,0:T(8,128)(2,1)S(1)}, u32[]{:S(2)}, u32[]{:S(2)}) collective-permute-start(bf16[576,128]{1,0:T(8,128)(2,1)S(1)} %get-tuple-element.111), channel_id=1, source_target_pairs={{0,1},{1,0},{2,3},{3,2},{4,5},{5,4},{6,7},{7,6},{8,9},{9,8},{10,11... | collective-permute-start | bytes 442376 | tf_op jit(solution)/shard_map/ppermute | solution.py:363
  51.1 8.4 %collective-permute-start.18 = (bf16[576,256]{1,0:T(8,128)(2,1)S(1)}, bf16[576,256]{1,0:T(8,128)(2,1)S(1)}, u32[]{:S(2)}, u32[]{:S(2)}) collective-permute-start(bf16[576,256]{1,0:T(8,128)(2,1)S(1)} %pad_maximum_fusion.2), channel_id=1, source_target_pairs={{0,4},{1,5},{4,8},{5,9},{8,12},{9,13},{12,14},{13,15},{14,10},{15,... | collective-permute-start | bytes 884744 | tf_op jit(solution)/shard_map/ppermute | solution.py:361
  52.7 8.0 %collective-permute-start.19 = (bf16[576,256]{1,0:T(8,128)(2,1)S(1)}, bf16[576,256]{1,0:T(8,128)(2,1)S(1)}, u32[]{:S(2)}, u32[]{:S(2)}) collective-permute-start(bf16[576,256]{1,0:T(8,128)(2,1)S(1)} %pad_maximum_fusion.3), channel_id=1, source_target_pairs={{0,2},{1,3},{4,0},{5,1},{8,4},{9,5},{12,8},{13,9},{14,12},{15,13},... | collective-permute-start | bytes 884744 | tf_op jit(solution)/shard_map/ppermute | solution.py:362
  53.2 7.8 %collective-permute-start.20 = (bf16[1152,128]{1,0:T(8,128)(2,1)S(1)}, bf16[1152,128]{1,0:T(8,128)(2,1)S(1)}, u32[]{:S(2)}, u32[]{:S(2)}) collective-permute-start(bf16[1152,128]{1,0:T(8,128)(2,1)S(1)} %pad_maximum_fusion.1.refs_0_), channel_id=1, source_target_pairs={{0,16},{16,0},{1,17},{17,1},{2,18},{18,2},{3,19},{19,3},{4,20},{20... | collective-permute-start | bytes 884744 | tf_op jit(solution)/shard_map/ppermute | solution.py:365
  54.7 12.5 %collective-permute-start.23 = (bf16[1728,256]{1,0:T(8,128)(2,1)S(1)}, bf16[1728,256]{1,0:T(8,128)(2,1)S(1)}, u32[]{:S(2)}, u32[]{:S(2)}) collective-permute-start(bf16[1728,256]{1,0:T(8,128)(2,1)S(1)} %pad_maximum_fusion.refs_0_), channel_id=1, source_target_pairs={{0,1},{1,0},{2,3},{3,2},{4,5},{5,4},{6,7},{7,6},{8,9},{9,8},{10,11... | collective-permute-start | bytes 2654216 | tf_op jit(solution)/shard_map/ppermute | solution.py:363
  54.7 12.5 %collective-permute-start.24 = (bf16[1728,256]{1,0:T(8,128)(2,1)S(1)}, bf16[1728,256]{1,0:T(8,128)(2,1)S(1)}, u32[]{:S(2)}, u32[]{:S(2)}) collective-permute-start(bf16[1728,256]{1,0:T(8,128)(2,1)S(1)} %collective-permute-done.12.refs_2_), channel_id=1, source_target_pairs={{0,1},{1,0},{2,3},{3,2},{4,5},{5,4},{6,7},{7,6},{8,9},{9,8},{10,11... | collective-permute-start | bytes 2654216 | tf_op jit(solution)/shard_map/ppermute | solution.py:363
  61.1 13.0 %collective-permute-start.21 = (bf16[576,256]{1,0:T(8,128)(2,1)S(1)}, bf16[576,256]{1,0:T(8,128)(2,1)S(1)}, u32[]{:S(2)}, u32[]{:S(2)}) collective-permute-start(bf16[576,256]{1,0:T(8,128)(2,1)S(1)} %add_convert_fusion.3), channel_id=1, source_target_pairs={{0,4},{1,5},{4,8},{5,9},{8,12},{9,13},{12,14},{13,15},{14,10},{15,... | collective-permute-start | bytes 884744 | tf_op jit(solution)/shard_map/ppermute | solution.py:361
  62.6 11.4 %collective-permute-start.22 = (bf16[576,256]{1,0:T(8,128)(2,1)S(1)}, bf16[576,256]{1,0:T(8,128)(2,1)S(1)}, u32[]{:S(2)}, u32[]{:S(2)}) collective-permute-start(bf16[576,256]{1,0:T(8,128)(2,1)S(1)} %add_convert_fusion.2), channel_id=1, source_target_pairs={{0,2},{1,3},{4,0},{5,1},{8,4},{9,5},{12,8},{13,9},{14,12},{15,13},... | collective-permute-start | bytes 884744 | tf_op jit(solution)/shard_map/ppermute | solution.py:362
  63.2 19.7 %collective-permute-start.29 = (bf16[1728,256]{1,0:T(8,128)(2,1)S(1)}, bf16[1728,256]{1,0:T(8,128)(2,1)S(1)}, u32[]{:S(2)}, u32[]{:S(2)}) collective-permute-start(bf16[1728,256]{1,0:T(8,128)(2,1)S(1)} %constant_dynamic-update-slice_fusion.2.refs_0_), channel_id=1, source_target_pairs={{0,16},{16,0},{1,17},{17,1},{2,18},{18,2},{3,19},{19,3},{4,20},{20... | collective-permute-start | bytes 2654216 | tf_op jit(solution)/shard_map/ppermute | solution.py:365
  67.2 9.1 %collective-permute-start.27 = (bf16[1152,256]{1,0:T(8,128)(2,1)S(1)}, bf16[1152,256]{1,0:T(8,128)(2,1)S(1)}, u32[]{:S(2)}, u32[]{:S(2)}) collective-permute-start(bf16[1152,256]{1,0:T(8,128)(2,1)S(1)} %constant_dynamic-update-slice_fusion.refs_0_), channel_id=1, source_target_pairs={{0,1},{1,0},{2,3},{3,2},{4,5},{5,4},{6,7},{7,6},{8,9},{9,8},{10,11... | collective-permute-start | bytes 1769480 | tf_op jit(solution)/shard_map/ppermute | solution.py:363
  67.2 9.1 %collective-permute-start.28 = (bf16[1152,256]{1,0:T(8,128)(2,1)S(1)}, bf16[1152,256]{1,0:T(8,128)(2,1)S(1)}, u32[]{:S(2)}, u32[]{:S(2)}) collective-permute-start(bf16[1152,256]{1,0:T(8,128)(2,1)S(1)} %collective-permute-done.17.refs_2_), channel_id=1, source_target_pairs={{0,1},{1,0},{2,3},{3,2},{4,5},{5,4},{6,7},{7,6},{8,9},{9,8},{10,11... | collective-permute-start | bytes 1769480 | tf_op jit(solution)/shard_map/ppermute | solution.py:363
  74.3 9.0 %collective-permute-start.25 = (bf16[576,256]{1,0:T(8,128)(2,1)S(1)}, bf16[576,256]{1,0:T(8,128)(2,1)S(1)}, u32[]{:S(2)}, u32[]{:S(2)}) collective-permute-start(bf16[576,256]{1,0:T(8,128)(2,1)S(1)} %add_convert_fusion.1), channel_id=1, source_target_pairs={{0,4},{1,5},{4,8},{5,9},{8,12},{9,13},{12,14},{13,15},{14,10},{15,... | collective-permute-start | bytes 884744 | tf_op jit(solution)/shard_map/ppermute | solution.py:361
  75.8 8.7 %collective-permute-start.26 = (bf16[576,256]{1,0:T(8,128)(2,1)S(1)}, bf16[576,256]{1,0:T(8,128)(2,1)S(1)}, u32[]{:S(2)}, u32[]{:S(2)}) collective-permute-start(bf16[576,256]{1,0:T(8,128)(2,1)S(1)} %add_convert_fusion), channel_id=1, source_target_pairs={{0,2},{1,3},{4,0},{5,1},{8,4},{9,5},{12,8},{13,9},{14,12},{15,13},... | collective-permute-start | bytes 884744 | tf_op jit(solution)/shard_map/ppermute | solution.py:362
  76.3 8.9 %collective-permute-start.30 = (bf16[1728,256]{1,0:T(8,128)(2,1)S(1)}, bf16[1728,256]{1,0:T(8,128)(2,1)S(1)}, u32[]{:S(2)}, u32[]{:S(2)}) collective-permute-start(bf16[1728,256]{1,0:T(8,128)(2,1)S(1)} %constant_dynamic-update-slice_fusion.2.refs_0_), channel_id=1, source_target_pairs={{0,1},{1,0},{2,3},{3,2},{4,5},{5,4},{6,7},{7,6},{8,9},{9,8},{10,11... | collective-permute-start | bytes 2654216 | tf_op jit(solution)/shard_map/ppermute | solution.py:363
  84.5 2.4 %collective-permute-start.31 = (bf16[1728,256]{1,0:T(8,128)(2,1)S(1)}, bf16[1728,256]{1,0:T(8,128)(2,1)S(1)}, u32[]{:S(2)}, u32[]{:S(2)}) collective-permute-start(bf16[1728,256]{1,0:T(8,128)(2,1)S(1)} %collective-permute-done.29.refs_2_), channel_id=1, source_target_pairs={{0,1},{1,0},{2,3},{3,2},{4,5},{5,4},{6,7},{7,6},{8,9},{9,8},{10,11... | collective-permute-start | bytes 2654216 | tf_op jit(solution)/shard_map/ppermute | solution.py:363
  84.7 8.6 %collective-permute-start.32 = (bf16[576,128]{1,0:T(8,128)(2,1)S(1)}, bf16[576,128]{1,0:T(8,128)(2,1)S(1)}, u32[]{:S(2)}, u32[]{:S(2)}) collective-permute-start(bf16[576,128]{1,0:T(8,128)(2,1)S(1)} %get-tuple-element.155), channel_id=1, source_target_pairs={{0,1},{1,0},{2,3},{3,2},{4,5},{5,4},{6,7},{7,6},{8,9},{9,8},{10,11... | collective-permute-start | bytes 442376 | tf_op jit(solution)/shard_map/ppermute | solution.py:363

commit v3 on v2

--- a/solution.py
+++ b/solution.py
@@ -425,7 +425,8 @@
     p_ahead, p_behind, token = grad_at(after_top, [far - 1, -(far - 1)], F32)
     gs = [jnp.concatenate([g_own, g_recv], axis=0)]
     waits = [act_recv, gs[0]] + [x for _, _, x in stacks[1:] if pair]
-    ahead, behind, token, act_recv, gs[0], *done = tie(ahead, behind, token, *waits)
+    ahead, token, act_recv, gs[0], *done = tie(ahead, token, *waits)
+    behind, token = tie(behind, token)
     others += done
     if pair:
         gs.append(across(gs[0]))
@@ -435,12 +436,12 @@
     hop = half // 2
     ahead = jnp.concatenate([p_ahead[:hop] + ahead.astype(F32), p_ahead[hop:]], axis=0)
     behind = jnp.concatenate([p_behind[:hop], p_behind[hop:] + behind.astype(F32)], axis=0)
-    ahead, behind = tie(ahead.astype(BF16), behind.astype(BF16))
-    ahead, behind = onward(ahead), back(behind)
+    ahead, behind = onward(ahead.astype(BF16)), back(behind.astype(BF16))
     rest_ds = [d for n in range(far - 2, 0, -1) for d in (n, -n)] + [0]
     *rest, token = grad_at(token, rest_ds, F32)
     rest = dict(zip(rest_ds, rest))
-    ahead, behind, token, *gs = tie(ahead, behind, token, *gs)
+    ahead, token, *gs = tie(ahead, token, *gs)
+    behind, token = tie(behind, token)
 
     g9t, bias_grad, activated = displaced_call(core[None], token, act_own, act_recv, gs, scale)
     state = {"total": None, "next": 0, "token": token}

time: 94.4 us -> 91.8 us (0.972)
  waiting for transfers between devices: 21.5 us -> 18.9 us
    ppermute x8, waiting for transfers between devices: 6.49 us -> 4.07 us  [body(): back = lambda v: lax.ppermute(v, 'filt', backwards)]
  transfers between devices with their start and end apart: 33 -> 33, of which waited for: 15 -> 13; matrix products, arithmetic and copies ran while one was open for 3% -> 3% of each run, Pallas kernels for 41% -> 42%
where the time goes in v3:
time: 91.8 us; the launch traced here: 91.6 us
  Pallas kernels  39.4 us (43%)
  starting transfers between devices  25.9 us (28%)
  waiting for transfers between devices  18.9 us (21%)
  local copies, waits for them, and re-layouts  5.85 us (6%)
    pallas_call x3, Pallas kernels, weight_grad_call(): pl.pallas_call(functools.partial(weight_grad_kernel, len(xs), scale), out...  17.2 us
    ppermute x8, starting transfers between devices, body(): onward = lambda v: lax.ppermute(v, 'filt', forwards)  14 us
    pallas_call x3, Pallas kernels, input_grad_call(): pl.pallas_call(functools.partial(input_grad_kernel, slots, pieces), out_s...  7.69 us
    pallas_call x2, Pallas kernels, forward_call(): pl.pallas_call(functools.partial(forward_kernel, slots, carry is not None...  6.38 us
    ppermute x8, waiting for transfers between devices, body(): onward = lambda v: lax.ppermute(v, 'filt', forwards)  6.02 us
    ppermute x13, waiting for transfers between devices, body(): sibling = lambda v: lax.ppermute(v, 'filt', swap)  5.64 us
    ppermute x4, starting transfers between devices, body(): across = lambda v: lax.ppermute(v, 'case', [(0, 1), (1, 0)])  5.19 us
    ppermute x8, waiting for transfers between devices, body(): back = lambda v: lax.ppermute(v, 'filt', backwards)  4.07 us
  transfers between devices with their start and end apart: 33, of which 13 were waited for; matrix products, arithmetic and copies ran while one was open for 3% of the time, Pallas kernels for 42%

profile of v3, /device:TPU:0, one launch (start us, length us, event | category | flops | bytes accessed | tf_op | source)
XLA Modules:
  0.0 91.6 jit_solution(1522300393352966264)
XLA Ops:
  0.7 1.2 %constant_dynamic-slice_fusion.1 = (bf16[128,576]{1,0:T(8,128)(2,1)S(1)}, bf16[128,576]{1,0:T(8,128)(2,1)S(1)}) fusion(bf16[128,1152]{1,0:T(8,128)(2,1)} %param.5, s32[]{:T(128)S(6)} %select_n.35, s32[]{:T(128)S(6)} %select_n.36), kind=kLoop, calls=%fused_computation.22 | loop fusion | bytes 589832 | tf_op jit(solution)/shard_map/dynamic-slice
  1.8 0.1 copy.16
  2.0 0.5 collective-permute-start
  2.5 1.0 %collective-permute-done = bf16[576,128]{1,0:T(8,128)(2,1)S(1)} collective-permute-done((bf16[576,128]{1,0:T(8,128)(2,1)S(1)}, bf16[576,128]{1,0:T(8,128)(2,1)S(1)}, u32[]{:S(2)}, u32[]{:S(2)}) %collective-permute-start) | collective-permute-done | bytes 147488 | tf_op jit(solution)/shard_map/ppermute | solution.py:363
  3.5 0.4 collective-permute-start.6
  3.9 0.1 copy.15
  4.0 0.1 maximum_select_fusion.refs_0_
  4.1 2.8 %collective-permute-start.1 = (bf16[576,256]{1,0:T(8,128)(2,1)S(1)}, bf16[576,256]{1,0:T(8,128)(2,1)S(1)}, u32[]{:S(2)}, u32[]{:S(2)}) collective-permute-start(bf16[576,256]{1,0:T(8,128)(2,1)S(1)} %maximum_select_fusion.refs_0_), channel_id=1, source_target_pairs={{0,4},{1,5},{4,8},{5,9},{8,12},{9,13},{12,14},{13,15},{14,10},{15,... | collective-permute-start | bytes 884744 | tf_op jit(solution)/shard_map/ppermute | solution.py:361
  6.9 1.2 %copy.13 = bf16[128,1152]{0,1:T(8,128)(2,1)S(1)} copy(bf16[128,1152]{1,0:T(8,128)(2,1)} %param.8) | data formatting | bytes 589824 | tf_op jit(solution)/shard_map/optimization_barrier | solution.py:366
  8.1 0.1 collective-permute-start.3
  8.3 0.4 collective-permute-start.4
  8.7 2.9 %collective-permute-done.4 = f32[1,128]{1,0:T(1,128)S(1)} collective-permute-done((f32[1,128]{1,0:T(1,128)S(1)}, f32[1,128]{1,0:T(1,128)S(1)}, u32[]{:S(2)}, u32[]{:S(2)}) %collective-permute-start.4) | collective-permute-done | bytes 544 | tf_op jit(solution)/shard_map/ppermute | solution.py:363
  11.6 2.7 %collective-permute-done.1.refs_1_ = bf16[576,256]{1,0:T(8,128)(2,1)S(1)} collective-permute-done((bf16[576,256]{1,0:T(8,128)(2,1)S(1)}, bf16[576,256]{1,0:T(8,128)(2,1)S(1)}, u32[]{:S(2)}, u32[]{:S(2)}) %collective-permute-start.1) | collective-permute-done | bytes 294944 | tf_op jit(solution)/shard_map/ppermute | solution.py:361
  14.4 1.5 %collective-permute-done.2.refs_2_ = bf16[576,256]{1,0:T(8,128)(2,1)S(1)} collective-permute-done((bf16[576,256]{1,0:T(8,128)(2,1)S(1)}, bf16[576,256]{1,0:T(8,128)(2,1)S(1)}, u32[]{:S(2)}, u32[]{:S(2)}) %collective-permute-start.2) | collective-permute-done | bytes 294944 | tf_op jit(solution)/shard_map/ppermute | solution.py:362
  16.0 1.6 %collective-permute-start.12 = (bf16[1728,256]{1,0:T(8,128)(2,1)S(1)}, bf16[1728,256]{1,0:T(8,128)(2,1)S(1)}, u32[]{:S(2)}, u32[]{:S(2)}) collective-permute-start(bf16[1728,256]{1,0:T(8,128)(2,1)S(1)} %pad_maximum_fusion.refs_0_), channel_id=1, source_target_pairs={{0,16},{16,0},{1,17},{17,1},{2,18},{18,2},{3,19},{19,3},{4,20},{20... | collective-permute-start | bytes 2654216 | tf_op jit(solution)/shard_map/ppermute | solution.py:365
  17.6 1.6 %collective-permute-start.5 = (bf16[576,256]{1,0:T(8,128)(2,1)S(1)}, bf16[576,256]{1,0:T(8,128)(2,1)S(1)}, u32[]{:S(2)}, u32[]{:S(2)}) collective-permute-start(bf16[576,256]{1,0:T(8,128)(2,1)S(1)} %collective-permute-done.1.refs_1_), channel_id=1, source_target_pairs={{0,4},{1,5},{4,8},{5,9},{8,12},{9,13},{12,14},{13,15},{14,10},{15,... | collective-permute-start | bytes 884744 | tf_op jit(solution)/shard_map/ppermute | solution.py:361
  19.1 0.4 collective-permute-start.8
  19.6 2.3 %copy-done = bf16[9,128,2048]{2,1,0:T(8,128)(2,1)S(1)} copy-done((bf16[9,128,2048]{2,1,0:T(8,128)(2,1)S(1)}, bf16[9,128,2048]{2,1,0:T(8,128)(2,1)}, u32[]{:S(2)}) %copy-start) | copy-done | bytes 4718616
  21.9 2.7 %hold.1 = (bf16[9,256,2048]{2,1,0:T(8,128)(2,1)S(1)}, f32[8,128]{1,0:T(8,128)S(1)}) custom-call(bf16[9,128,2048]{2,1,0:T(8,128)(2,1)S(1)} %copy-done, bf16[9,128,2048]{2,1,0:T(8,128)(2,1)} %collective-permute-done.6.w_sib), custom_call_target="tpu_custom_call" | custom-call | flops 1000 | bytes 1000 | tf_op jit(solution)/shard_map/hold/pallas_call | solution.py:81
  24.6 0.8 collective-permute-done.5.refs_3_
  25.4 1.6 %collective-permute-start.7 = (bf16[576,256]{1,0:T(8,128)(2,1)S(1)}, bf16[576,256]{1,0:T(8,128)(2,1)S(1)}, u32[]{:S(2)}, u32[]{:S(2)}) collective-permute-start(bf16[576,256]{1,0:T(8,128)(2,1)S(1)} %collective-permute-done.5.refs_3_), channel_id=1, source_target_pairs={{0,4},{1,5},{4,8},{5,9},{8,12},{9,13},{12,14},{13,15},{14,10},{15,... | collective-permute-start | bytes 884744 | tf_op jit(solution)/shard_map/ppermute | solution.py:361
  27.0 0.4 collective-permute-start.10
  27.5 0.6 collective-permute-start.17
  28.1 0.7 fusion.q_ref
  28.8 4.2 %forward.2 = (f32[3,576,256]{2,1,0:T(8,128)S(1)}, f32[8,128]{1,0:T(8,128)S(1)}) custom-call(s32[8]{0:T(128)S(1)} %fusion.q_ref, f32[8,128]{1,0:T(8,128)S(1)} %get-tuple-element.87.after, bf16[9,256,2048]{2,1,0:T(8,128)(2,1)S(1)} %get-tuple-element.88.w_all, bf16[576,256]{1,0:T(8,128)(2,1)S(1)} %maximum_select_fusion.refs_0_, ...), custom_call_target="tpu_custom_call" | custom-call | flops 1000 | bytes 1000 | tf_op jit(solution)/shard_map/forward/pallas_call | solution.py:124
  33.0 1.6 %collective-permute-start.9 = (bf16[288,256]{1,0:T(8,128)(2,1)S(1)}, bf16[288,256]{1,0:T(8,128)(2,1)S(1)}, u32[]{:S(2)}, u32[]{:S(2)}) collective-permute-start(bf16[288,256]{1,0:T(8,128)(2,1)S(1)} %slice.20), channel_id=1, source_target_pairs={{0,4},{1,5},{4,8},{5,9},{8,12},{9,13},{12,14},{13,15},{14,10},{15,... | collective-permute-start | bytes 442376 | tf_op jit(solution)/shard_map/ppermute | solution.py:361
  34.7 0.5 collective-permute-start.11
  35.2 2.2 %forward.3 = (f32[3,576,256]{2,1,0:T(8,128)S(1)}, f32[8,128]{1,0:T(8,128)S(1)}) custom-call(s32[8]{0:T(128)S(1)} %fusion.q_ref, f32[8,128]{1,0:T(8,128)S(1)} %get-tuple-element.94.after, bf16[9,256,2048]{2,1,0:T(8,128)(2,1)S(1)} %get-tuple-element.88.w_all, f32[3,576,256]{2,1,0:T(8,128)S(1)} %get-tuple-element.95.refs_0_, ...), custom_call_target="tpu_custom_call" | custom-call | flops 1000 | bytes 1000 | tf_op jit(solution)/shard_map/forward/pallas_call | solution.py:124
  37.3 1.3 %collective-permute-done.12.refs_2_ = bf16[1728,256]{1,0:T(8,128)(2,1)S(1)} collective-permute-done((bf16[1728,256]{1,0:T(8,128)(2,1)S(1)}, bf16[1728,256]{1,0:T(8,128)(2,1)S(1)}, u32[]{:S(2)}, u32[]{:S(2)}) %collective-permute-start.12) | collective-permute-done | bytes 884768 | tf_op jit(solution)/shard_map/ppermute | solution.py:365
  38.6 1.2 %collective-permute-done.11.refs_1_ = bf16[288,256]{1,0:T(8,128)(2,1)S(1)} collective-permute-done((bf16[288,256]{1,0:T(8,128)(2,1)S(1)}, bf16[288,256]{1,0:T(8,128)(2,1)S(1)}, u32[]{:S(2)}, u32[]{:S(2)}) %collective-permute-start.11) | collective-permute-done | bytes 147488 | tf_op jit(solution)/shard_map/ppermute | solution.py:362
  39.9 2.0 %gate.1 = (bf16[576,128]{1,0:T(8,128)(2,1)S(1)}, bf16[576,128]{1,0:T(8,128)(2,1)S(1)}, bf16[576,128]{1,0:T(8,128)(2,1)S(1)}, bf16[576,128]{1,0:T(8,128)(2,1)S(1)}, bf16[576,2304]{1,0:T(8,128)(2,1)S(1)}) custom-call(s32[8]{0:T(128)S(1)} %fusion.q_ref, f32[8,128]{1,0:T(8,128)S(1)} %get-tuple-element.97.after, ...), custom_call_target="tpu_custom_call" | custom-call | flops 1000 | bytes 1000 | tf_op jit(solution)/shard_map/gate/pallas_call | solution.py:169
  41.8 0.1 collective-permute-start.13
  41.9 0.5 collective-permute-start.23
  42.4 1.4 %input_grad.3 = (bf16[288,256]{1,0:T(8,128)(2,1)S(1)}, bf16[288,256]{1,0:T(8,128)(2,1)S(1)}, f32[8,128]{1,0:T(8,128)S(1)}) custom-call(s32[8]{0:T(128)S(1)} %fusion.q_ref, f32[8,128]{1,0:T(8,128)S(1)} %get-tuple-element.97.after, bf16[9,256,2048]{2,1,0:T(8,128)(2,1)S(1)} %get-tuple-element.88.w_all, bf16[576,2304]{1,0:T(8,128)(2,1)S(1)} %get-tuple-element.103.g9), custom_call_target="tpu_custom_call" | custom-call | flops 1000 | bytes 1000 | tf_op jit(solution)/shard_map/input_grad/pallas_call | solution.py:199
  43.9 0.5 collective-permute-start.14
  44.4 1.6 %collective-permute-start.15 = (bf16[288,256]{1,0:T(8,128)(2,1)S(1)}, bf16[288,256]{1,0:T(8,128)(2,1)S(1)}, u32[]{:S(2)}, u32[]{:S(2)}) collective-permute-start(bf16[288,256]{1,0:T(8,128)(2,1)S(1)} %get-tuple-element.109), channel_id=1, source_target_pairs={{0,4},{1,5},{4,8},{5,9},{8,12},{9,13},{12,14},{13,15},{14,10},{15,... | collective-permute-start | bytes 442376 | tf_op jit(solution)/shard_map/ppermute | solution.py:361
  45.9 2.1 %input_grad.4 = (f32[576,256]{1,0:T(8,128)S(1)}, f32[576,256]{1,0:T(8,128)S(1)}, f32[8,128]{1,0:T(8,128)S(1)}) custom-call(s32[8]{0:T(128)S(1)} %fusion.q_ref, f32[8,128]{1,0:T(8,128)S(1)} %get-tuple-element.106.after, bf16[9,256,2048]{2,1,0:T(8,128)(2,1)S(1)} %get-tuple-element.88.w_all, bf16[576,2304]{1,0:T(8,128)(2,1)S(1)} %get-tuple-element.103.g9), custom_call_target="tpu_custom_call" | custom-call | flops 1000 | bytes 1000 | tf_op jit(solution)/shard_map/input_grad/pallas_call | solution.py:199
  48.1 1.8 %collective-permute-done.15 = bf16[288,256]{1,0:T(8,128)(2,1)S(1)} collective-permute-done((bf16[288,256]{1,0:T(8,128)(2,1)S(1)}, bf16[288,256]{1,0:T(8,128)(2,1)S(1)}, u32[]{:S(2)}, u32[]{:S(2)}) %collective-permute-start.15) | collective-permute-done | bytes 147488 | tf_op jit(solution)/shard_map/ppermute | solution.py:361
  50.0 0.6 collective-permute-start.18
  50.8 1.7 %collective-permute-start.19 = (bf16[576,256]{1,0:T(8,128)(2,1)S(1)}, bf16[576,256]{1,0:T(8,128)(2,1)S(1)}, u32[]{:S(2)}, u32[]{:S(2)}) collective-permute-start(bf16[576,256]{1,0:T(8,128)(2,1)S(1)} %pad_maximum_fusion.3), channel_id=1, source_target_pairs={{0,4},{1,5},{4,8},{5,9},{8,12},{9,13},{12,14},{13,15},{14,10},{15,... | collective-permute-start | bytes 884744 | tf_op jit(solution)/shard_map/ppermute | solution.py:361
  52.4 1.5 %collective-permute-start.20 = (bf16[1152,128]{1,0:T(8,128)(2,1)S(1)}, bf16[1152,128]{1,0:T(8,128)(2,1)S(1)}, u32[]{:S(2)}, u32[]{:S(2)}) collective-permute-start(bf16[1152,128]{1,0:T(8,128)(2,1)S(1)} %pad_maximum_fusion.1.refs_0_), channel_id=1, source_target_pairs={{0,16},{16,0},{1,17},{17,1},{2,18},{18,2},{3,19},{19,3},{4,20},{20... | collective-permute-start | bytes 884744 | tf_op jit(solution)/shard_map/ppermute | solution.py:365
  54.0 0.1 collective-permute-start.24
  54.1 4.2 %input_grad.5 = (f32[576,256]{1,0:T(8,128)S(1)}, f32[576,256]{1,0:T(8,128)S(1)}, f32[576,256]{1,0:T(8,128)S(1)}, f32[576,256]{1,0:T(8,128)S(1)}, f32[576,256]{1,0:T(8,128)S(1)}, /*index=5*/f32[8,128]{1,0:T(8,128)S(1)}) custom-call(s32[8]{0:T(128)S(1)} %fusion.q_ref, f32[8,128]{1,0:T(8,128)S(1)} %get-tuple-element.118.after, ...), custom_call_target="tpu_custom_call" | custom-call | flops 1000 | bytes 1000 | tf_op jit(solution)/shard_map/input_grad/pallas_call | solution.py:199
  58.3 0.3 collective-permute-done.19
  58.6 1.5 %collective-permute-start.29 = (bf16[1728,256]{1,0:T(8,128)(2,1)S(1)}, bf16[1728,256]{1,0:T(8,128)(2,1)S(1)}, u32[]{:S(2)}, u32[]{:S(2)}) collective-permute-start(bf16[1728,256]{1,0:T(8,128)(2,1)S(1)} %constant_dynamic-update-slice_fusion.2.refs_0_), channel_id=1, source_target_pairs={{0,16},{16,0},{1,17},{17,1},{2,18},{18,2},{3,19},{19,3},{4,20},{20... | collective-permute-start | bytes 2654216 | tf_op jit(solution)/shard_map/ppermute | solution.py:365
  60.1 0.1 add_convert_fusion.3
  60.2 0.1 add_convert_fusion.2
  60.3 1.6 %collective-permute-start.21 = (bf16[576,256]{1,0:T(8,128)(2,1)S(1)}, bf16[576,256]{1,0:T(8,128)(2,1)S(1)}, u32[]{:S(2)}, u32[]{:S(2)}) collective-permute-start(bf16[576,256]{1,0:T(8,128)(2,1)S(1)} %add_convert_fusion.3), channel_id=1, source_target_pairs={{0,4},{1,5},{4,8},{5,9},{8,12},{9,13},{12,14},{13,15},{14,10},{15,... | collective-permute-start | bytes 884744 | tf_op jit(solution)/shard_map/ppermute | solution.py:361
  61.9 0.5 collective-permute-start.22
  62.4 0.5 collective-permute-start.28
  62.9 2.4 %displaced.1 = (bf16[1152,2304]{1,0:T(8,128)(2,1)S(1)}, f32[1,128]{1,0:T(1,128)}, bf16[128,1152]{1,0:T(8,128)(2,1)}) custom-call(s32[1]{0:T(128)} %bitcast.core, f32[8,128]{1,0:T(8,128)S(1)} %get-tuple-element.122.after, bf16[576,128]{1,0:T(8,128)(2,1)S(1)} %get-tuple-element.123.act_own, bf16[576,128]{1,0:T(8,128)(2,1)S(1)} %collective-permute-done.16.act_sib, ...), custom_call_target="tpu_custom_call" | custom-call | flops 1000 | bytes 1000 | tf_op jit(solution)/shard_map/displaced/pallas_call | solution.py:236
  65.3 6.2 %weight_grad.3 = (f32[1152,2048]{1,0:T(8,128)}, f32[8,128]{1,0:T(8,128)S(1)}) custom-call(s32[8]{0:T(128)S(1)} %fusion.q_ref, f32[8,128]{1,0:T(8,128)S(1)} %get-tuple-element.122.after, bf16[1152,2304]{1,0:T(8,128)(2,1)S(1)} %get-tuple-element.135.g9t, bf16[1728,256]{1,0:T(8,128)(2,1)S(1)} %pad_maximum_fusion.refs_0_, ...), custom_call_target="tpu_custom_call" | custom-call | flops 1000 | bytes 1000 | tf_op jit(solution)/shard_map/weight_grad/pallas_call | solution.py:265
  71.5 0.2 add_convert_fusion
  71.7 1.6 %collective-permute-start.25 = (bf16[576,256]{1,0:T(8,128)(2,1)S(1)}, bf16[576,256]{1,0:T(8,128)(2,1)S(1)}, u32[]{:S(2)}, u32[]{:S(2)}) collective-permute-start(bf16[576,256]{1,0:T(8,128)(2,1)S(1)} %get-tuple-element.141), channel_id=1, source_target_pairs={{0,4},{1,5},{4,8},{5,9},{8,12},{9,13},{12,14},{13,15},{14,10},{15,... | collective-permute-start | bytes 884744 | tf_op jit(solution)/shard_map/ppermute | solution.py:361
  73.3 0.5 collective-permute-start.26
  73.8 4.7 %weight_grad.4 = (f32[1152,2048]{1,0:T(8,128)}, f32[8,128]{1,0:T(8,128)S(1)}) custom-call(s32[8]{0:T(128)S(1)} %fusion.q_ref, f32[8,128]{1,0:T(8,128)S(1)} %get-tuple-element.143.after, bf16[1152,2304]{1,0:T(8,128)(2,1)S(1)} %get-tuple-element.135.g9t, ...), custom_call_target="tpu_custom_call", output_to_operand_aliasing={{0}: (7, {})} | custom-call | flops 1000 | bytes 1000 | tf_op jit(solution)/shard_map/weight_grad/pallas_call | solution.py:265
  78.5 1.9 %collective-permute-done.29.refs_2_ = bf16[1728,256]{1,0:T(8,128)(2,1)S(1)} collective-permute-done((bf16[1728,256]{1,0:T(8,128)(2,1)S(1)}, bf16[1728,256]{1,0:T(8,128)(2,1)S(1)}, u32[]{:S(2)}, u32[]{:S(2)}) %collective-permute-start.29) | collective-permute-done | bytes 884768 | tf_op jit(solution)/shard_map/ppermute | solution.py:365
  80.4 0.3 collective-permute-done.25.ahead
  80.7 1.3 %collective-permute-done.26.behind = bf16[576,256]{1,0:T(8,128)(2,1)S(1)} collective-permute-done((bf16[576,256]{1,0:T(8,128)(2,1)S(1)}, bf16[576,256]{1,0:T(8,128)(2,1)S(1)}, u32[]{:S(2)}, u32[]{:S(2)}) %collective-permute-start.26) | collective-permute-done | bytes 294944 | tf_op jit(solution)/shard_map/ppermute | solution.py:362
  82.0 0.2 last_sum.1
  82.2 0.6 collective-permute-start.32
  82.8 1.7 %collective-permute-done.31.refs_3_ = bf16[1728,256]{1,0:T(8,128)(2,1)S(1)} collective-permute-done((bf16[1728,256]{1,0:T(8,128)(2,1)S(1)}, bf16[1728,256]{1,0:T(8,128)(2,1)S(1)}, u32[]{:S(2)}, u32[]{:S(2)}) %collective-permute-start.31) | collective-permute-done | bytes 884768 | tf_op jit(solution)/shard_map/ppermute | solution.py:363
  84.4 6.3 %weight_grad.5 = (f32[1152,2048]{1,0:T(8,128)}, f32[8,128]{1,0:T(8,128)S(1)}) custom-call(s32[8]{0:T(128)S(1)} %fusion.q_ref, f32[8,128]{1,0:T(8,128)S(1)} %get-tuple-element.147.after, bf16[1152,2304]{1,0:T(8,128)(2,1)S(1)} %get-tuple-element.135.g9t, ...), custom_call_target="tpu_custom_call", output_to_operand_aliasing={{0}: (7, {})} | custom-call | flops 1000 | bytes 1000 | tf_op jit(solution)/shard_map/weight_grad/pallas_call | solution.py:265
  90.7 0.9 join.1
  (46 shorter events, 0.5 us)
Async XLA Ops:
  0.6 7.6 %copy-start.1 = (f32[128]{0:T(128)S(1)}, f32[128]{0:T(128)}, u32[]{:S(2)}) copy-start(f32[128]{0:T(128)} %param.7) | copy-start | bytes 1540
  2.0 1.5 %collective-permute-start = (bf16[576,128]{1,0:T(8,128)(2,1)S(1)}, bf16[576,128]{1,0:T(8,128)(2,1)S(1)}, u32[]{:S(2)}, u32[]{:S(2)}) collective-permute-start(bf16[576,128]{1,0:T(8,128)(2,1)S(1)} %bitcast.14), channel_id=1, source_target_pairs={{0,1},{1,0},{2,3},{3,2},{4,5},{5,4},{6,7},{7,6},{8,9},{9,8},{10,11... | collective-permute-start | bytes 442376 | tf_op jit(solution)/shard_map/ppermute | solution.py:363
  3.5 16.1 %collective-permute-start.6 = (bf16[9,128,2048]{2,1,0:T(8,128)(2,1)}, bf16[9,128,2048]{2,1,0:T(8,128)(2,1)}, u32[]{:S(2)}, u32[]{:S(2)}) collective-permute-start(bf16[9,128,2048]{2,1,0:T(8,128)(2,1)} %w_own), channel_id=1, source_target_pairs={{0,1},{1,0},{2,3},{3,2},{4,5},{5,4},{6,7},{7,6},{8,9},{9,8},{10,11... | collective-permute-start | bytes 14155784 | tf_op jit(solution)/shard_map/ppermute | solution.py:363
  4.1 10.2 %collective-permute-start.1 = (bf16[576,256]{1,0:T(8,128)(2,1)S(1)}, bf16[576,256]{1,0:T(8,128)(2,1)S(1)}, u32[]{:S(2)}, u32[]{:S(2)}) collective-permute-start(bf16[576,256]{1,0:T(8,128)(2,1)S(1)} %maximum_select_fusion.refs_0_), channel_id=1, source_target_pairs={{0,4},{1,5},{4,8},{5,9},{8,12},{9,13},{12,14},{13,15},{14,10},{15,... | collective-permute-start | bytes 884744 | tf_op jit(solution)/shard_map/ppermute | solution.py:361
  6.9 9.0 %collective-permute-start.2 = (bf16[576,256]{1,0:T(8,128)(2,1)S(1)}, bf16[576,256]{1,0:T(8,128)(2,1)S(1)}, u32[]{:S(2)}, u32[]{:S(2)}) collective-permute-start(bf16[576,256]{1,0:T(8,128)(2,1)S(1)} %maximum_select_fusion.refs_0_), channel_id=1, source_target_pairs={{0,2},{1,3},{4,0},{5,1},{8,4},{9,5},{12,8},{13,9},{14,12},{15,13},... | collective-permute-start | bytes 884744 | tf_op jit(solution)/shard_map/ppermute | solution.py:362
  8.1 3.5 %collective-permute-start.3 = (bf16[576,128]{1,0:T(8,128)(2,1)S(1)}, bf16[576,128]{1,0:T(8,128)(2,1)S(1)}, u32[]{:S(2)}, u32[]{:S(2)}) collective-permute-start(bf16[576,128]{1,0:T(8,128)(2,1)S(1)} %get-tuple-element.159), channel_id=1, source_target_pairs={{0,1},{1,0},{2,3},{3,2},{4,5},{5,4},{6,7},{7,6},{8,9},{9,8},{10,11... | collective-permute-start | bytes 442376 | tf_op jit(solution)/shard_map/ppermute | solution.py:363
  8.3 3.4 %collective-permute-start.4 = (f32[1,128]{1,0:T(1,128)S(1)}, f32[1,128]{1,0:T(1,128)S(1)}, u32[]{:S(2)}, u32[]{:S(2)}) collective-permute-start(f32[1,128]{1,0:T(1,128)S(1)} %bitcast.15), channel_id=1, source_target_pairs={{0,1},{1,0},{2,3},{3,2},{4,5},{5,4},{6,7},{7,6},{8,9},{9,8},{10,11... | collective-permute-start | bytes 1544 | tf_op jit(solution)/shard_map/ppermute | solution.py:363
  16.0 22.6 %collective-permute-start.12 = (bf16[1728,256]{1,0:T(8,128)(2,1)S(1)}, bf16[1728,256]{1,0:T(8,128)(2,1)S(1)}, u32[]{:S(2)}, u32[]{:S(2)}) collective-permute-start(bf16[1728,256]{1,0:T(8,128)(2,1)S(1)} %pad_maximum_fusion.refs_0_), channel_id=1, source_target_pairs={{0,16},{16,0},{1,17},{17,1},{2,18},{18,2},{3,19},{19,3},{4,20},{20... | collective-permute-start | bytes 2654216 | tf_op jit(solution)/shard_map/ppermute | solution.py:365
  17.6 7.9 %collective-permute-start.5 = (bf16[576,256]{1,0:T(8,128)(2,1)S(1)}, bf16[576,256]{1,0:T(8,128)(2,1)S(1)}, u32[]{:S(2)}, u32[]{:S(2)}) collective-permute-start(bf16[576,256]{1,0:T(8,128)(2,1)S(1)} %collective-permute-done.1.refs_1_), channel_id=1, source_target_pairs={{0,4},{1,5},{4,8},{5,9},{8,12},{9,13},{12,14},{13,15},{14,10},{15,... | collective-permute-start | bytes 884744 | tf_op jit(solution)/shard_map/ppermute | solution.py:361
  19.1 7.9 %collective-permute-start.8 = (bf16[576,256]{1,0:T(8,128)(2,1)S(1)}, bf16[576,256]{1,0:T(8,128)(2,1)S(1)}, u32[]{:S(2)}, u32[]{:S(2)}) collective-permute-start(bf16[576,256]{1,0:T(8,128)(2,1)S(1)} %collective-permute-done.2.refs_2_), channel_id=1, source_target_pairs={{0,2},{1,3},{4,0},{5,1},{8,4},{9,5},{12,8},{13,9},{14,12},{15,13},... | collective-permute-start | bytes 884744 | tf_op jit(solution)/shard_map/ppermute | solution.py:362
  19.6 2.3 %copy-start = (bf16[9,128,2048]{2,1,0:T(8,128)(2,1)S(1)}, bf16[9,128,2048]{2,1,0:T(8,128)(2,1)}, u32[]{:S(2)}) copy-start(bf16[9,128,2048]{2,1,0:T(8,128)(2,1)} %w_own) | copy-start | bytes 14155780
  25.4 7.6 %collective-permute-start.7 = (bf16[576,256]{1,0:T(8,128)(2,1)S(1)}, bf16[576,256]{1,0:T(8,128)(2,1)S(1)}, u32[]{:S(2)}, u32[]{:S(2)}) collective-permute-start(bf16[576,256]{1,0:T(8,128)(2,1)S(1)} %collective-permute-done.5.refs_3_), channel_id=1, source_target_pairs={{0,4},{1,5},{4,8},{5,9},{8,12},{9,13},{12,14},{13,15},{14,10},{15,... | collective-permute-start | bytes 884744 | tf_op jit(solution)/shard_map/ppermute | solution.py:361
  27.0 7.7 %collective-permute-start.10 = (bf16[576,256]{1,0:T(8,128)(2,1)S(1)}, bf16[576,256]{1,0:T(8,128)(2,1)S(1)}, u32[]{:S(2)}, u32[]{:S(2)}) collective-permute-start(bf16[576,256]{1,0:T(8,128)(2,1)S(1)} %collective-permute-done.8.refs_4_), channel_id=1, source_target_pairs={{0,2},{1,3},{4,0},{5,1},{8,4},{9,5},{12,8},{13,9},{14,12},{15,13},... | collective-permute-start | bytes 884744 | tf_op jit(solution)/shard_map/ppermute | solution.py:362
  27.5 22.4 %collective-permute-start.17 = (bf16[1152,256]{1,0:T(8,128)(2,1)S(1)}, bf16[1152,256]{1,0:T(8,128)(2,1)S(1)}, u32[]{:S(2)}, u32[]{:S(2)}) collective-permute-start(bf16[1152,256]{1,0:T(8,128)(2,1)S(1)} %constant_dynamic-update-slice_fusion.refs_0_), channel_id=1, source_target_pairs={{0,16},{16,0},{1,17},{17,1},{2,18},{18,2},{3,19},{19,3},{4,20},{20... | collective-permute-start | bytes 1769480 | tf_op jit(solution)/shard_map/ppermute | solution.py:365
  33.0 5.6 %collective-permute-start.9 = (bf16[288,256]{1,0:T(8,128)(2,1)S(1)}, bf16[288,256]{1,0:T(8,128)(2,1)S(1)}, u32[]{:S(2)}, u32[]{:S(2)}) collective-permute-start(bf16[288,256]{1,0:T(8,128)(2,1)S(1)} %slice.20), channel_id=1, source_target_pairs={{0,4},{1,5},{4,8},{5,9},{8,12},{9,13},{12,14},{13,15},{14,10},{15,... | collective-permute-start | bytes 442376 | tf_op jit(solution)/shard_map/ppermute | solution.py:361
  34.7 5.2 %collective-permute-start.11 = (bf16[288,256]{1,0:T(8,128)(2,1)S(1)}, bf16[288,256]{1,0:T(8,128)(2,1)S(1)}, u32[]{:S(2)}, u32[]{:S(2)}) collective-permute-start(bf16[288,256]{1,0:T(8,128)(2,1)S(1)} %slice.21), channel_id=1, source_target_pairs={{0,2},{1,3},{4,0},{5,1},{8,4},{9,5},{12,8},{13,9},{14,12},{15,13},... | collective-permute-start | bytes 442376 | tf_op jit(solution)/shard_map/ppermute | solution.py:362
  41.8 4.1 %collective-permute-start.13 = (bf16[576,128]{1,0:T(8,128)(2,1)S(1)}, bf16[576,128]{1,0:T(8,128)(2,1)S(1)}, u32[]{:S(2)}, u32[]{:S(2)}) collective-permute-start(bf16[576,128]{1,0:T(8,128)(2,1)S(1)} %get-tuple-element.105), channel_id=1, source_target_pairs={{0,1},{1,0},{2,3},{3,2},{4,5},{5,4},{6,7},{7,6},{8,9},{9,8},{10,11... | collective-permute-start | bytes 442376 | tf_op jit(solution)/shard_map/ppermute | solution.py:363
  41.9 20.4 %collective-permute-start.23 = (bf16[1728,256]{1,0:T(8,128)(2,1)S(1)}, bf16[1728,256]{1,0:T(8,128)(2,1)S(1)}, u32[]{:S(2)}, u32[]{:S(2)}) collective-permute-start(bf16[1728,256]{1,0:T(8,128)(2,1)S(1)} %pad_maximum_fusion.refs_0_), channel_id=1, source_target_pairs={{0,1},{1,0},{2,3},{3,2},{4,5},{5,4},{6,7},{7,6},{8,9},{9,8},{10,11... | collective-permute-start | bytes 2654216 | tf_op jit(solution)/shard_map/ppermute | solution.py:363
  43.9 6.1 %collective-permute-start.14 = (bf16[288,256]{1,0:T(8,128)(2,1)S(1)}, bf16[288,256]{1,0:T(8,128)(2,1)S(1)}, u32[]{:S(2)}, u32[]{:S(2)}) collective-permute-start(bf16[288,256]{1,0:T(8,128)(2,1)S(1)} %get-tuple-element.108), channel_id=1, source_target_pairs={{0,2},{1,3},{4,0},{5,1},{8,4},{9,5},{12,8},{13,9},{14,12},{15,13},... | collective-permute-start | bytes 442376 | tf_op jit(solution)/shard_map/ppermute | solution.py:362
  44.4 5.6 %collective-permute-start.15 = (bf16[288,256]{1,0:T(8,128)(2,1)S(1)}, bf16[288,256]{1,0:T(8,128)(2,1)S(1)}, u32[]{:S(2)}, u32[]{:S(2)}) collective-permute-start(bf16[288,256]{1,0:T(8,128)(2,1)S(1)} %get-tuple-element.109), channel_id=1, source_target_pairs={{0,4},{1,5},{4,8},{5,9},{8,12},{9,13},{12,14},{13,15},{14,10},{15,... | collective-permute-start | bytes 442376 | tf_op jit(solution)/shard_map/ppermute | solution.py:361
  45.9 4.0 %collective-permute-start.16 = (bf16[576,128]{1,0:T(8,128)(2,1)S(1)}, bf16[576,128]{1,0:T(8,128)(2,1)S(1)}, u32[]{:S(2)}, u32[]{:S(2)}) collective-permute-start(bf16[576,128]{1,0:T(8,128)(2,1)S(1)} %get-tuple-element.111), channel_id=1, source_target_pairs={{0,1},{1,0},{2,3},{3,2},{4,5},{5,4},{6,7},{7,6},{8,9},{9,8},{10,11... | collective-permute-start | bytes 442376 | tf_op jit(solution)/shard_map/ppermute | solution.py:363
  50.0 10.0 %collective-permute-start.18 = (bf16[576,256]{1,0:T(8,128)(2,1)S(1)}, bf16[576,256]{1,0:T(8,128)(2,1)S(1)}, u32[]{:S(2)}, u32[]{:S(2)}) collective-permute-start(bf16[576,256]{1,0:T(8,128)(2,1)S(1)} %pad_maximum_fusion.2), channel_id=1, source_target_pairs={{0,2},{1,3},{4,0},{5,1},{8,4},{9,5},{12,8},{13,9},{14,12},{15,13},... | collective-permute-start | bytes 884744 | tf_op jit(solution)/shard_map/ppermute | solution.py:362
  50.8 7.8 %collective-permute-start.19 = (bf16[576,256]{1,0:T(8,128)(2,1)S(1)}, bf16[576,256]{1,0:T(8,128)(2,1)S(1)}, u32[]{:S(2)}, u32[]{:S(2)}) collective-permute-start(bf16[576,256]{1,0:T(8,128)(2,1)S(1)} %pad_maximum_fusion.3), channel_id=1, source_target_pairs={{0,4},{1,5},{4,8},{5,9},{8,12},{9,13},{12,14},{13,15},{14,10},{15,... | collective-permute-start | bytes 884744 | tf_op jit(solution)/shard_map/ppermute | solution.py:361
  52.4 7.6 %collective-permute-start.20 = (bf16[1152,128]{1,0:T(8,128)(2,1)S(1)}, bf16[1152,128]{1,0:T(8,128)(2,1)S(1)}, u32[]{:S(2)}, u32[]{:S(2)}) collective-permute-start(bf16[1152,128]{1,0:T(8,128)(2,1)S(1)} %pad_maximum_fusion.1.refs_0_), channel_id=1, source_target_pairs={{0,16},{16,0},{1,17},{17,1},{2,18},{18,2},{3,19},{19,3},{4,20},{20... | collective-permute-start | bytes 884744 | tf_op jit(solution)/shard_map/ppermute | solution.py:365
  54.0 8.4 %collective-permute-start.24 = (bf16[1728,256]{1,0:T(8,128)(2,1)S(1)}, bf16[1728,256]{1,0:T(8,128)(2,1)S(1)}, u32[]{:S(2)}, u32[]{:S(2)}) collective-permute-start(bf16[1728,256]{1,0:T(8,128)(2,1)S(1)} %collective-permute-done.12.refs_2_), channel_id=1, source_target_pairs={{0,1},{1,0},{2,3},{3,2},{4,5},{5,4},{6,7},{7,6},{8,9},{9,8},{10,11... | collective-permute-start | bytes 2654216 | tf_op jit(solution)/shard_map/ppermute | solution.py:363
  58.6 21.8 %collective-permute-start.29 = (bf16[1728,256]{1,0:T(8,128)(2,1)S(1)}, bf16[1728,256]{1,0:T(8,128)(2,1)S(1)}, u32[]{:S(2)}, u32[]{:S(2)}) collective-permute-start(bf16[1728,256]{1,0:T(8,128)(2,1)S(1)} %constant_dynamic-update-slice_fusion.2.refs_0_), channel_id=1, source_target_pairs={{0,16},{16,0},{1,17},{17,1},{2,18},{18,2},{3,19},{19,3},{4,20},{20... | collective-permute-start | bytes 2654216 | tf_op jit(solution)/shard_map/ppermute | solution.py:365
  60.3 11.3 %collective-permute-start.21 = (bf16[576,256]{1,0:T(8,128)(2,1)S(1)}, bf16[576,256]{1,0:T(8,128)(2,1)S(1)}, u32[]{:S(2)}, u32[]{:S(2)}) collective-permute-start(bf16[576,256]{1,0:T(8,128)(2,1)S(1)} %add_convert_fusion.3), channel_id=1, source_target_pairs={{0,4},{1,5},{4,8},{5,9},{8,12},{9,13},{12,14},{13,15},{14,10},{15,... | collective-permute-start | bytes 884744 | tf_op jit(solution)/shard_map/ppermute | solution.py:361
  61.9 9.7 %collective-permute-start.22 = (bf16[576,256]{1,0:T(8,128)(2,1)S(1)}, bf16[576,256]{1,0:T(8,128)(2,1)S(1)}, u32[]{:S(2)}, u32[]{:S(2)}) collective-permute-start(bf16[576,256]{1,0:T(8,128)(2,1)S(1)} %add_convert_fusion.2), channel_id=1, source_target_pairs={{0,2},{1,3},{4,0},{5,1},{8,4},{9,5},{12,8},{13,9},{14,12},{15,13},... | collective-permute-start | bytes 884744 | tf_op jit(solution)/shard_map/ppermute | solution.py:362
  62.3 11.4 %collective-permute-start.27 = (bf16[1152,256]{1,0:T(8,128)(2,1)S(1)}, bf16[1152,256]{1,0:T(8,128)(2,1)S(1)}, u32[]{:S(2)}, u32[]{:S(2)}) collective-permute-start(bf16[1152,256]{1,0:T(8,128)(2,1)S(1)} %constant_dynamic-update-slice_fusion.refs_0_), channel_id=1, source_target_pairs={{0,1},{1,0},{2,3},{3,2},{4,5},{5,4},{6,7},{7,6},{8,9},{9,8},{10,11... | collective-permute-start | bytes 1769480 | tf_op jit(solution)/shard_map/ppermute | solution.py:363
  62.4 11.4 %collective-permute-start.28 = (bf16[1152,256]{1,0:T(8,128)(2,1)S(1)}, bf16[1152,256]{1,0:T(8,128)(2,1)S(1)}, u32[]{:S(2)}, u32[]{:S(2)}) collective-permute-start(bf16[1152,256]{1,0:T(8,128)(2,1)S(1)} %collective-permute-done.17.refs_2_), channel_id=1, source_target_pairs={{0,1},{1,0},{2,3},{3,2},{4,5},{5,4},{6,7},{7,6},{8,9},{9,8},{10,11... | collective-permute-start | bytes 1769480 | tf_op jit(solution)/shard_map/ppermute | solution.py:363
  71.7 9.0 %collective-permute-start.25 = (bf16[576,256]{1,0:T(8,128)(2,1)S(1)}, bf16[576,256]{1,0:T(8,128)(2,1)S(1)}, u32[]{:S(2)}, u32[]{:S(2)}) collective-permute-start(bf16[576,256]{1,0:T(8,128)(2,1)S(1)} %get-tuple-element.141), channel_id=1, source_target_pairs={{0,4},{1,5},{4,8},{5,9},{8,12},{9,13},{12,14},{13,15},{14,10},{15,... | collective-permute-start | bytes 884744 | tf_op jit(solution)/shard_map/ppermute | solution.py:361
  73.3 8.7 %collective-permute-start.26 = (bf16[576,256]{1,0:T(8,128)(2,1)S(1)}, bf16[576,256]{1,0:T(8,128)(2,1)S(1)}, u32[]{:S(2)}, u32[]{:S(2)}) collective-permute-start(bf16[576,256]{1,0:T(8,128)(2,1)S(1)} %get-tuple-element.142), channel_id=1, source_target_pairs={{0,2},{1,3},{4,0},{5,1},{8,4},{9,5},{12,8},{13,9},{14,12},{15,13},... | collective-permute-start | bytes 884744 | tf_op jit(solution)/shard_map/ppermute | solution.py:362
  73.8 9.0 %collective-permute-start.30 = (bf16[1728,256]{1,0:T(8,128)(2,1)S(1)}, bf16[1728,256]{1,0:T(8,128)(2,1)S(1)}, u32[]{:S(2)}, u32[]{:S(2)}) collective-permute-start(bf16[1728,256]{1,0:T(8,128)(2,1)S(1)} %constant_dynamic-update-slice_fusion.2.refs_0_), channel_id=1, source_target_pairs={{0,1},{1,0},{2,3},{3,2},{4,5},{5,4},{6,7},{7,6},{8,9},{9,8},{10,11... | collective-permute-start | bytes 2654216 | tf_op jit(solution)/shard_map/ppermute | solution.py:363
  82.0 2.4 %collective-permute-start.31 = (bf16[1728,256]{1,0:T(8,128)(2,1)S(1)}, bf16[1728,256]{1,0:T(8,128)(2,1)S(1)}, u32[]{:S(2)}, u32[]{:S(2)}) collective-permute-start(bf16[1728,256]{1,0:T(8,128)(2,1)S(1)} %collective-permute-done.29.refs_2_), channel_id=1, source_target_pairs={{0,1},{1,0},{2,3},{3,2},{4,5},{5,4},{6,7},{7,6},{8,9},{9,8},{10,11... | collective-permute-start | bytes 2654216 | tf_op jit(solution)/shard_map/ppermute | solution.py:363
  82.2 8.5 %collective-permute-start.32 = (bf16[576,128]{1,0:T(8,128)(2,1)S(1)}, bf16[576,128]{1,0:T(8,128)(2,1)S(1)}, u32[]{:S(2)}, u32[]{:S(2)}) collective-permute-start(bf16[576,128]{1,0:T(8,128)(2,1)S(1)} %get-tuple-element.155), channel_id=1, source_target_pairs={{0,1},{1,0},{2,3},{3,2},{4,5},{5,4},{6,7},{7,6},{8,9},{9,8},{10,11... | collective-permute-start | bytes 442376 | tf_op jit(solution)/shard_map/ppermute | solution.py:363
